TPU v7x, 128 devices: a whole 4x4x4 slice. The times are simulated.
128 devices in a mesh: snap: 16 (over x_lo, y, core), clus: 8 (over z, x_hi).
Axes of the slice: x: 4 (x_hi: 2, x_lo: 2; x = x_hi * 2 + x_lo), y: 4, z: 4, core: 2. Of those that a mesh axis runs over, the one named last changes fastest.
Arguments:
- features: bfloat16 [64, 4096, 512], P('snap', 'clus'), parts along dimension 1, may hold values from -6 to 6
- adjacency: int32 [64, 4096, 512], P('snap', 'clus'), parts along dimension 1, may hold values 0 or 1
- first_seen: int32 [4096], P(('clus', 'snap')), parts along dimension 0, may hold values from 0 to 31
- pos_embed: bfloat16 [64, 512], replicated, may hold values from -3 to 3
- w_struct: bfloat16 [2, 512, 512], replicated, may hold values from -0.25 to 0.25
- w_query: bfloat16 [2, 512, 512], replicated, as said below
- w_key: bfloat16 [2, 512, 512], replicated, as said below
- w_value: bfloat16 [2, 512, 512], replicated, may hold values from -0.25 to 0.25
- w_out: bfloat16 [2, 512, 512], replicated, may hold values from -0.25 to 0.25
- w_up: bfloat16 [2, 512, 1024], replicated, may hold values from -0.25 to 0.25
- w_down: bfloat16 [2, 1024, 512], replicated, may hold values from -0.1875 to 0.1875
- norm_gain: float32 [2, 2, 512], replicated, may hold values from 0.1 to 1.9
Outputs:
- hidden_out: bfloat16 [64, 4096, 512], P('snap', 'clus'), parts along dimension 1
There are 8 independent parts, one for each index of `clus`. A program takes and returns all parts, laid end to end along the dimension named above; an argument that names none is the same for every part. Nothing has to cross between parts.
Inputs may be any that keep to these rules, and one draw needn't show every extreme that they name: `w_query`: entries lie within -30 / sqrt(512) to 30 / sqrt(512). `w_key`: entries lie within -5 / sqrt(512) to 5 / sqrt(512).
All inputs are finite; a program needn't handle non-finite values. No bound on the sum of `adjacency` on one device may be relied on, other than what follows from the above.
Results may differ from a plain program's by a relative error of at most 0.012.
Values may be sent and summed in bfloat16 or wider, within the bound.
No kernel may reach another device: no remote copies, remote signals or barrier semaphores. Data moves between devices by JAX's collectives and lax.ppermute only.
A program may use at most 128 MiB of HBM per device.

v0:
```python
import jax
import jax.numpy as jnp
from jax import lax
from jax.sharding import PartitionSpec as P

HEADS = 8
BLOCKS = 2


def layer_norm(values_in, gain):
    average = jnp.mean(values_in, axis=-1, keepdims=True)
    centred = values_in - average
    scattered_rows = jnp.mean(centred * centred, axis=-1, keepdims=True)
    return centred * lax.rsqrt(scattered_rows + 1e-05) * gain


def convolve(hidden, adjacent, degree, weight_matrix):
    summed = jnp.einsum(
        "snm,smd->snd", adjacent, hidden, preferred_element_type=jnp.float32
    ) + hidden.astype(jnp.float32)
    blended_values = (summed / degree[..., None]).astype(jnp.bfloat16)
    convolved = jax.nn.elu(
        jnp.einsum("zfk,kb->zfb", blended_values, weight_matrix, preferred_element_type=jnp.float32)
    )
    return (convolved + hidden.astype(jnp.float32)).astype(jnp.bfloat16)


def temporal(
    vertex_rows, first_seen, pos_embed, w_query, w_key, w_value, w_out, w_up, w_down, gain_pair
):
    timestep_count, vertex_count, model_width = vertex_rows.shape
    head_count = w_struct_heads()
    head_dim = model_width // head_count
    row_totals = vertex_rows.astype(jnp.float32) + pos_embed.astype(jnp.float32)[:, None, :]
    row_totals = row_totals.reshape(-1, model_width)
    normed = layer_norm(row_totals, gain_pair[0]).astype(jnp.bfloat16)
    shape_heads = (timestep_count, vertex_count, head_count, head_dim)
    queries = (
        jnp.dot(normed, w_query, preferred_element_type=jnp.float32)
        .astype(jnp.bfloat16)
        .reshape(shape_heads)
    )
    key_rows = (
        jnp.dot(normed, w_key, preferred_element_type=jnp.float32)
        .astype(jnp.bfloat16)
        .reshape(shape_heads)
    )
    values = (
        jnp.dot(normed, w_value, preferred_element_type=jnp.float32)
        .astype(jnp.bfloat16)
        .reshape(shape_heads)
    )
    scores = jnp.einsum(
        "tvhd,jvhd->vhtj", queries, key_rows, preferred_element_type=jnp.float32
    ) * head_dim ** (-0.5)
    positions = jnp.arange(timestep_count, dtype=jnp.int32)
    causal = positions[None, :] <= positions[:, None]
    diagonal_mask = positions[None, :] == positions[:, None]
    present = positions[None, None, :] >= first_seen[:, None, None]
    allowed = causal[None] & (present | diagonal_mask[None])
    scores = jnp.where(allowed[:, None], scores, -1e30)
    weights = jax.nn.softmax(scores, axis=-1).astype(jnp.bfloat16)
    attended_heads = jnp.einsum(
        "vhtj,jvhd->tvhd", weights, values, preferred_element_type=jnp.float32
    )
    attended_heads = attended_heads.astype(jnp.bfloat16).reshape(-1, model_width)
    attended = row_totals + jnp.dot(attended_heads, w_out, preferred_element_type=jnp.float32)
    normed_two = layer_norm(attended, gain_pair[1]).astype(jnp.bfloat16)
    inner_rows = jax.nn.gelu(jnp.dot(normed_two, w_up, preferred_element_type=jnp.float32)).astype(
        jnp.bfloat16
    )
    finished = attended + jnp.dot(inner_rows, w_down, preferred_element_type=jnp.float32)
    return finished.astype(jnp.bfloat16).reshape(timestep_count, vertex_count, model_width)


def w_struct_heads():
    return HEADS


def on_device(
    features,
    adjacency,
    first_seen,
    pos_embed,
    w_struct,
    w_query,
    w_key,
    w_value,
    w_out,
    w_up,
    w_down,
    norm_gain,
):
    adjacent = adjacency.astype(jnp.bfloat16)
    degree = 1.0 + jnp.sum(adjacency, axis=2).astype(jnp.float32)
    hidden = features
    for layer in range(BLOCKS):
        weight_matrix = w_struct[layer]
        convolved = convolve(hidden, adjacent, degree, weight_matrix)
        vertex_rows = lax.all_to_all(convolved, "snap", split_axis=1, concat_axis=0, tiled=True)
        finished = temporal(
            vertex_rows,
            first_seen,
            pos_embed,
            w_query[layer],
            w_key[layer],
            w_value[layer],
            w_out[layer],
            w_up[layer],
            w_down[layer],
            norm_gain[layer],
        )
        hidden = lax.all_to_all(finished, "snap", split_axis=0, concat_axis=1, tiled=True)
    return hidden


def solution(mesh):
    in_specs = (
        P("snap", "clus", None),
        P("snap", "clus", None),
        P(("clus", "snap")),
        P(),
        P(),
        P(),
        P(),
        P(),
        P(),
        P(),
        P(),
        P(),
    )
    out_specs = P("snap", "clus", None)
    return jax.shard_map(
        on_device, mesh=mesh, in_specs=in_specs, out_specs=out_specs, check_vma=False
    )
```

profile of v0, /device:TPU:1, one launch (start us, length us, event | category | flops | bytes accessed | tf_op | source)
XLA Modules:
  0.0 307.2 jit_solution(3006731191875920725)
XLA Ops:
  2.7 7.9 %fusion.22 = bf16[4,512,512]{2,1,0:T(8,128)(2,1)S(1)} fusion(bf16[4,512,512]{2,1,0:T(8,128)(2,1)} %param.12, f32[4,512]{1,0:T(4,128)S(1)} %convert_add_fusion.4, s32[4,512,512]{2,1,0:T(8,128)} %param.13, bf16[2,512,512]{2,1,0:T(8,128)(2,1)S(1)} %copy-done.12), kind=kOutput, calls=%fused_computation.40 | convolution fusion | flops 2159017984 | bytes 13115392 | tf_op jit(solution)/shard_map/zfk,kb->zfb/dot_general | solution.py:23
  13.6 7.2 %all-to-all-start = ((bf16[4,512,512]{2,0,1:T(4,128)(2,1)}), bf16[4,512,512]{2,0,1:T(4,128)(2,1)S(1)}, u32[]{:S(2)}, u32[]{:S(2)}) async-start(bf16[4,512,512]{2,0,1:T(4,128)(2,1)} %copy.80), calls=%async_computation | async-start | bytes 4194304 | tf_op jit(solution)/shard_map/all_to_all | solution.py:100
  21.4 26.9 %all-to-all-done = bf16[4,512,512]{2,0,1:T(4,128)(2,1)S(1)} async-done(((bf16[4,512,512]{2,0,1:T(4,128)(2,1)}), bf16[4,512,512]{2,0,1:T(4,128)(2,1)S(1)}, u32[]{:S(2)}, u32[]{:S(2)}) %all-to-all-start) | async-done | bytes 2097184 | tf_op jit(solution)/shard_map/all_to_all | solution.py:100
  63.7 3.7 %reshape.652 = bf16[64,32,8,64]{3,2,1,0:T(8,128)(2,1)} reshape(bf16[2048,512]{1,0:T(8,128)(2,1)S(1)} %convolution_convert_fusion.3) | data formatting | bytes 4194304 | tf_op jit(solution)/shard_map/reshape | solution.py:46
  70.2 3.9 %reshape.650 = bf16[64,32,8,64]{3,2,1,0:T(8,128)(2,1)} reshape(bf16[2048,512]{1,0:T(8,128)(2,1)S(1)} %convolution_convert_fusion.5) | data formatting | bytes 4194304 | tf_op jit(solution)/shard_map/reshape | solution.py:51
  74.1 8.4 %fusion.45 = f32[32,8,64,64]{2,3,1,0:T(8,128)S(1)} fusion(bf16[64,32,8,64]{3,2,1,0:T(8,128)(2,1)} %reshape.652, bf16[64,32,8,64]{3,2,1,0:T(8,128)(2,1)} %reshape.651), kind=kOutput, calls=%fused_computation.67 | convolution fusion | flops 134217728 | bytes 8388608 | tf_op jit(solution)/shard_map/tvhd,jvhd->vhtj/dot_general | solution.py:53
  82.5 4.6 %fusion.135 = (f32[32,8,64]{2,1,0:T(8,128)S(1)}, f32[32,8,64,64]{2,3,1,0:T(8,128)}) fusion(f32[32,8,64,64]{2,3,1,0:T(8,128)S(1)} %fusion.45, pred[32,64,64]{1,2,0:T(8,128)(4,1)S(1)} %or_and_fusion), kind=kOutput, calls=%fused_computation.164 | output fusion | flops 6291519 | bytes 8585216 | tf_op jit(solution)/shard_map/sub | solution.py:62
  87.1 8.4 %convert_bitcast_fusion.3 = bf16[64,32,8,64]{0,3,2,1:T(8,128)(2,1)} fusion(f32[32,8,64,64]{2,3,1,0:T(8,128)} %get-tuple-element.14, f32[32,8,64]{2,1,0:T(8,128)S(1)} %get-tuple-element.13, bf16[64,32,8,64]{3,2,1,0:T(8,128)(2,1)S(1)} %copy-done.4), kind=kOutput, calls=%fused_computation.79 | convolution fusion | flops 137363456 | bytes 8454144 | tf_op jit(solution)/shard_map/vhtj,jvhd->tvhd/dot_general | solution.py:63
  95.5 7.1 %copy.91 = bf16[64,32,8,64]{3,2,1,0:T(8,128)(2,1)} copy(bf16[64,32,8,64]{0,3,2,1:T(8,128)(2,1)} %convert_bitcast_fusion.3) | data formatting | bytes 4194304 | tf_op jit(solution)/shard_map/convert_element_type | solution.py:66
  102.6 5.9 %reshape.653 = bf16[2048,512]{1,0:T(8,128)(2,1)S(1)} reshape(bf16[64,32,8,64]{3,2,1,0:T(8,128)(2,1)} %copy.91) | data formatting | bytes 4194304 | tf_op jit(solution)/shard_map/reshape | solution.py:66
  114.9 8.4 %add_convert_fusion.1 = bf16[2048,512]{1,0:T(8,128)(2,1)S(1)} fusion(f32[2048,512]{1,0:T(8,128)} %copy-done.3, f32[512]{0:T(512)S(1)} %bitcast.163, f32[2048]{0:T(1024)S(1)} %add_rsqrt_fusion.3, f32[2048]{0:T(1024)S(1)} %broadcast_multiply_fusion.3, bf16[2,1024,512]{2,1,0:T(8,128)(2,1)} %param.22, bf16[2,512,1024]{2,1,0:T(8,128)(2,1)} %param.21), kind=kOutput, calls=%fused_computation.76 | convolution fusion | flops 4320133120 | bytes 12601344 | tf_op jit(solution)/shard_map/dot_general | solution.py:72
  123.3 32.6 %all_to_all.54 = bf16[64,32,512]{2,1,0:T(8,128)(2,1)S(1)} all-to-all(bf16[64,32,512]{2,1,0:T(8,128)(2,1)S(1)} %bitcast.153), channel_id=1, replica_groups=mesh['snap'=16,'clus'=8] {'snap'}, dimensions={0} | all-to-all | bytes 4194304 | tf_op jit(solution)/shard_map/all_to_all | solution.py:113
  156.1 7.5 %fusion.25 = bf16[4,512,512]{2,1,0:T(8,128)(2,1)} fusion(bf16[4,512,512]{2,1,0:T(8,128)(2,1)S(1)} %bitcast.155, f32[4,512]{1,0:T(4,128)S(1)} %convert_add_fusion.4, s32[4,512,512]{2,1,0:T(8,128)} %param.13, bf16[2,512,512]{2,1,0:T(8,128)(2,1)} %param.16), kind=kOutput, calls=%fused_computation.43 | convolution fusion | flops 2159017984 | bytes 13115392 | tf_op jit(solution)/shard_map/zfk,kb->zfb/dot_general | solution.py:23
  166.8 30.5 %all_to_all.55 = bf16[4,512,512]{2,0,1:T(4,128)(2,1)S(1)} all-to-all(bf16[4,512,512]{2,0,1:T(4,128)(2,1)S(1)} %copy.95), channel_id=1, replica_groups=mesh['snap'=16,'clus'=8] {'snap'}, dimensions={1} | all-to-all | bytes 4194304 | tf_op jit(solution)/shard_map/all_to_all | solution.py:100
  208.8 6.2 %reshape.656 = bf16[64,32,8,64]{3,2,1,0:T(8,128)(2,1)} reshape(bf16[2048,512]{1,0:T(8,128)(2,1)} %convolution_convert_fusion.1) | data formatting | bytes 4194304 | tf_op jit(solution)/shard_map/reshape | solution.py:41
  215.0 6.3 %reshape.657 = bf16[64,32,8,64]{3,2,1,0:T(8,128)(2,1)} reshape(bf16[2048,512]{1,0:T(8,128)(2,1)} %convolution_convert_fusion) | data formatting | bytes 4194304 | tf_op jit(solution)/shard_map/reshape | solution.py:46
  221.4 8.4 %fusion.41 = f32[32,8,64,64]{2,3,1,0:T(8,128)S(1)} fusion(bf16[64,32,8,64]{3,2,1,0:T(8,128)(2,1)} %reshape.657, bf16[64,32,8,64]{3,2,1,0:T(8,128)(2,1)} %reshape.656), kind=kOutput, calls=%fused_computation.63 | convolution fusion | flops 134217728 | bytes 8388608 | tf_op jit(solution)/shard_map/tvhd,jvhd->vhtj/dot_general | solution.py:53
  229.8 4.6 %fusion.137 = (f32[32,8,64]{2,1,0:T(8,128)S(1)}, f32[32,8,64,64]{2,3,1,0:T(8,128)}) fusion(f32[32,8,64,64]{2,3,1,0:T(8,128)S(1)} %fusion.41, pred[32,64,64]{1,2,0:T(8,128)(4,1)S(1)} %copy-done.9), kind=kOutput, calls=%fused_computation.166 | output fusion | flops 6291519 | bytes 8585216 | tf_op jit(solution)/shard_map/sub | solution.py:62
  234.4 3.6 %reshape.655 = bf16[64,32,8,64]{3,2,1,0:T(8,128)(2,1)} reshape(bf16[2048,512]{1,0:T(8,128)(2,1)S(1)} %convolution_convert_fusion.2) | data formatting | bytes 4194304 | tf_op jit(solution)/shard_map/reshape | solution.py:51
  238.0 9.5 %convert_bitcast_fusion.2 = bf16[64,32,8,64]{0,3,2,1:T(8,128)(2,1)} fusion(f32[32,8,64,64]{2,3,1,0:T(8,128)} %get-tuple-element.18, f32[32,8,64]{2,1,0:T(8,128)S(1)} %get-tuple-element.17, bf16[64,32,8,64]{3,2,1,0:T(8,128)(2,1)} %reshape.655), kind=kOutput, calls=%fused_computation.73 | convolution fusion | flops 137363456 | bytes 8454144 | tf_op jit(solution)/shard_map/vhtj,jvhd->tvhd/dot_general | solution.py:63
  247.5 7.1 %copy.105 = bf16[64,32,8,64]{3,2,1,0:T(8,128)(2,1)} copy(bf16[64,32,8,64]{0,3,2,1:T(8,128)(2,1)} %convert_bitcast_fusion.2) | data formatting | bytes 4194304 | tf_op jit(solution)/shard_map/convert_element_type | solution.py:66
  254.6 5.6 %reshape.658 = bf16[2048,512]{1,0:T(8,128)(2,1)S(1)} reshape(bf16[64,32,8,64]{3,2,1,0:T(8,128)(2,1)} %copy.105) | data formatting | bytes 4194304 | tf_op jit(solution)/shard_map/reshape | solution.py:66
  266.7 8.4 %add_convert_fusion = bf16[2048,512]{1,0:T(8,128)(2,1)S(1)} fusion(f32[2048,512]{1,0:T(8,128)} %copy-done.2, f32[512]{0:T(512)S(1)} %bitcast.162, f32[2048]{0:T(1024)S(1)} %add_rsqrt_fusion.2, f32[2048]{0:T(1024)S(1)} %broadcast_multiply_fusion.2, bf16[2,1024,512]{2,1,0:T(8,128)(2,1)} %param.22, bf16[2,512,1024]{2,1,0:T(8,128)(2,1)} %param.21), kind=kOutput, calls=%fused_computation.70 | convolution fusion | flops 4320133120 | bytes 12601344 | tf_op jit(solution)/shard_map/dot_general | solution.py:72
  275.0 30.3 %all_to_all.56 = bf16[64,32,512]{2,1,0:T(8,128)(2,1)S(1)} all-to-all(bf16[64,32,512]{2,1,0:T(8,128)(2,1)S(1)} %bitcast.154), channel_id=1, replica_groups=mesh['snap'=16,'clus'=8] {'snap'}, dimensions={0} | all-to-all | bytes 4194304 | tf_op jit(solution)/shard_map/all_to_all | solution.py:113
  (80 shorter events, 53.7 us)
Async XLA Ops:
  0.0 2.6 copy-start.12
  10.6 10.1 %copy-start.7 = (bf16[64,512]{1,0:T(8,128)(2,1)S(1)}, bf16[64,512]{1,0:T(8,128)(2,1)}, u32[]{:S(2)}) copy-start(bf16[64,512]{1,0:T(8,128)(2,1)} %param.15) | copy-start | bytes 196612
  10.6 10.3 %copy-start.11 = (s32[32]{0:T(128)S(1)}, s32[32]{0:T(128)}, u32[]{:S(2)}) copy-start(s32[32]{0:T(128)} %param.14) | copy-start | bytes 388
  10.6 10.4 %copy-start.10 = (f32[2,2,512]{2,1,0:T(2,128)S(1)}, f32[2,2,512]{2,1,0:T(2,128)}, u32[]{:S(2)}) copy-start(f32[2,2,512]{2,1,0:T(2,128)} %param.23) | copy-start | bytes 24580
  13.6 34.6 %all-to-all-start = ((bf16[4,512,512]{2,0,1:T(4,128)(2,1)}), bf16[4,512,512]{2,0,1:T(4,128)(2,1)S(1)}, u32[]{:S(2)}, u32[]{:S(2)}) async-start(bf16[4,512,512]{2,0,1:T(4,128)(2,1)} %copy.80), calls=%async_computation | async-start | bytes 4194304 | tf_op jit(solution)/shard_map/all_to_all | solution.py:100
  21.4 61.2 %copy-start.8 = (pred[32,64,64]{1,2,0:T(8,128)(4,1)}, pred[32,64,64]{1,2,0:T(8,128)(4,1)S(1)}, u32[]{:S(2)}) copy-start(pred[32,64,64]{1,2,0:T(8,128)(4,1)S(1)} %or_and_fusion) | copy-start | bytes 393220
  51.4 2.0 copy-start.1
  51.4 4.5 %copy-start.13 = (bf16[2,512,512]{2,1,0:T(8,128)(2,1)S(1)}, bf16[2,512,512]{2,1,0:T(8,128)(2,1)}, u32[]{:S(2)}) copy-start(bf16[2,512,512]{2,1,0:T(8,128)(2,1)} %param.17) | copy-start | bytes 3145732
  54.5 1.3 copy-start.5
  82.5 4.6 %copy-start.4 = (bf16[64,32,8,64]{3,2,1,0:T(8,128)(2,1)S(1)}, bf16[64,32,8,64]{3,2,1,0:T(8,128)(2,1)}, u32[]{:S(2)}) copy-start(bf16[64,32,8,64]{3,2,1,0:T(8,128)(2,1)} %reshape.650) | copy-start | bytes 6291460
  102.6 5.9 %copy-start.6 = (bf16[2,512,512]{2,1,0:T(8,128)(2,1)S(1)}, bf16[2,512,512]{2,1,0:T(8,128)(2,1)}, u32[]{:S(2)}) copy-start(bf16[2,512,512]{2,1,0:T(8,128)(2,1)} %param.20) | copy-start | bytes 3145732
  112.1 1.9 copy-start.3
  200.4 4.6 %copy-start = (f32[16,4,32,512]{3,2,1,0:T(8,128)}, f32[16,4,32,512]{3,2,1,0:T(8,128)S(1)}, u32[]{:S(2)}) copy-start(f32[16,4,32,512]{3,2,1,0:T(8,128)S(1)} %copy.97) | copy-start | bytes 12582916
  200.4 2.0 copy-start.14
  202.4 2.6 copy-start.15
  205.0 2.6 copy-start.16
  221.4 8.5 %copy-start.9 = (pred[32,64,64]{1,2,0:T(8,128)(4,1)S(1)}, pred[32,64,64]{1,2,0:T(8,128)(4,1)}, u32[]{:S(2)}) copy-start(pred[32,64,64]{1,2,0:T(8,128)(4,1)} %copy-done.8) | copy-start | bytes 393220
  263.9 1.9 copy-start.2
where the time goes:
time: 313 us; the launch traced here: 307 us
  blocking collectives  93.4 us (30%)
  matrix products  87.6 us (28%)
  local copies, waits for them, and re-layouts  70.6 us (23%)
  waiting for transfers between devices  26.9 us (9%)
  other arithmetic  20.8 us (7%)
  starting transfers between devices  7.16 us (2%)
    all_to_all x2, blocking collectives, on_device(): lax.all_to_all(finished, 'snap', split_axis=0, concat_axis=1, tiled=True)  63 us
    all_to_all x1, blocking collectives, on_device(): lax.all_to_all(convolved, 'snap', split_axis=1, concat_axis=0, tiled=True)  30.5 us
    all_to_all x1, waiting for transfers between devices, on_device(): lax.all_to_all(convolved, 'snap', split_axis=1, concat_axis=0, tiled=True)  26.9 us
    dot_general x2, matrix products, temporal(): jnp.einsum('vhtj,jvhd->tvhd', weights, values, preferred_element_type=jnp...  17.9 us
    dot_general x2, matrix products, temporal(): jnp.einsum('tvhd,jvhd->vhtj', queries, key_rows, preferred_element_type=j...  16.9 us
    dot_general x2, matrix products, temporal(): jnp.dot(inner_rows, w_down, preferred_element_type=jnp.float32)  16.7 us
    dot_general x2, matrix products, convolve(): jnp.einsum('zfk,kb->zfb', blended_values, weight_matrix, preferred_elemen...  15.4 us
    convert_element_type x2, local copies, waits for them, and re-layouts, temporal(): attended_heads.astype(jnp.bfloat16).reshape(-1, model_width)  14.1 us
  transfers between devices with their start and end apart: 1, of which 1 were waited for; matrix products, arithmetic and copies ran while one was open for 0% of the time, Pallas kernels for 0%

commit v1 on v0

v1 whole, which is shorter than its diff:
```python
import functools

import jax
import jax.numpy as jnp
from jax import lax
from jax.experimental import pallas as pl
from jax.experimental.pallas import tpu as pltpu
from jax.sharding import PartitionSpec as P

HEADS = 8
BLOCKS = 2
CHUNKS = 2
GROUP = 8
LANES = 128
VMEM_LIMIT = 48 * 1024 * 1024


def normalise(rows, gain):
    average = jnp.mean(rows, axis=-1, keepdims=True)
    centred = rows - average
    spread = jnp.mean(centred * centred, axis=-1, keepdims=True)
    return (centred * lax.rsqrt(spread + 1e-05) * gain).astype(jnp.bfloat16)


def structure_kernel(*refs, pieces, chunk):
    hidden_refs = refs[:pieces]
    adjacency_ref, weight_ref, out_ref, gathered = refs[pieces:]
    owners, _, rows, width = out_ref.shape
    nodes = adjacency_ref.shape[-1]
    part = nodes // owners // pieces
    if pieces == 1:
        hidden = hidden_refs[0][...].reshape(nodes, width)
        own = hidden.reshape(owners, nodes // owners, width)[:, chunk * rows : (chunk + 1) * rows]
    else:
        for piece in range(pieces):
            gathered[:, piece * part : (piece + 1) * part, :] = hidden_refs[piece][:, 0]
        hidden = gathered[...].reshape(nodes, width)
        own = hidden_refs[chunk][:, 0]
    own = own.reshape(owners * rows, width).astype(jnp.float32)
    links = adjacency_ref[...].reshape(owners * rows, nodes).astype(jnp.float32)
    degree = 1.0 + jnp.sum(links, axis=1, keepdims=True)
    summed = jnp.dot(links.astype(jnp.bfloat16), hidden, preferred_element_type=jnp.float32)
    mixture = ((summed + own) / degree).astype(jnp.bfloat16)
    mapped = jnp.dot(mixture, weight_ref[0], preferred_element_type=jnp.float32)
    bent = jnp.where(mapped > 0, mapped, jnp.exp(jnp.minimum(mapped, 0.0)) - 1.0)
    out_ref[...] = (bent + own).astype(jnp.bfloat16).reshape(out_ref.shape)


def structure(hidden, adjacency, w_struct, layer, chunk, owners):
    snapshots, nodes, _ = adjacency.shape
    width = w_struct.shape[-1]
    rows = nodes // owners // CHUNKS
    pieces = len(hidden)
    if pieces == 1:
        hidden_specs = [pl.BlockSpec((1, nodes, width), lambda s: (s, 0, 0))]
    else:
        hidden_specs = [pl.BlockSpec((owners, 1, rows, width), lambda s: (0, s, 0, 0))] * pieces
    links = adjacency.reshape(snapshots, owners, CHUNKS, rows, nodes)
    flops = 2 * snapshots * owners * rows * width * (nodes + width)
    return pl.pallas_call(
        functools.partial(structure_kernel, pieces=pieces, chunk=chunk),
        grid=(snapshots,),
        out_shape=jax.ShapeDtypeStruct((owners, snapshots, rows, width), jnp.bfloat16),
        in_specs=hidden_specs
        + [
            pl.BlockSpec((1, owners, 1, rows, nodes), lambda s: (s, 0, chunk, 0, 0)),
            pl.BlockSpec((1, width, width), lambda s: (layer, 0, 0)),
        ],
        out_specs=pl.BlockSpec((owners, 1, rows, width), lambda s: (0, s, 0, 0)),
        scratch_shapes=[pltpu.VMEM((owners, nodes // owners, width), jnp.bfloat16)],
        compiler_params=pltpu.CompilerParams(vmem_limit_bytes=VMEM_LIMIT),
        cost_estimate=pl.CostEstimate(
            flops=flops, transcendentals=0, bytes_accessed=snapshots * owners * rows * nodes * 8
        ),
        name=f"structure_{layer}_{chunk}",
    )(*hidden, links, w_struct)


def temporal_kernel(
    first_ref,
    x_ref,
    pos_ref,
    wq_ref,
    wk_ref,
    wv_ref,
    wo_ref,
    wu_ref,
    wd_ref,
    gain_ref,
    out_ref,
    mixed,
    rows_sum,
    normed,
    queries,
    key_rows,
    values,
    joined,
    order,
    *,
    first_vertex,
):
    steps, group, width = x_ref.shape
    head_dim = width // HEADS
    pair = 2 * head_dim
    f32 = jnp.float32

    row = lax.broadcasted_iota(jnp.int32, (steps, pair), 0)
    lane = lax.broadcasted_iota(jnp.int32, (steps, pair), 1)
    column = lane & (head_dim - 1)
    order[...] = jnp.where(row < column, row, jnp.where(row == column, 1 << 20, -1))
    left = lane < head_dim

    for tile in range(width // LANES):
        mixed[tile] = (
            x_ref[:, :, tile * LANES : (tile + 1) * LANES]
            .astype(f32)
            .reshape(steps * group, LANES)
        )
    gain_one = gain_ref[0, 0:1, :]
    gain_two = gain_ref[0, 1:2, :]
    pos = pos_ref[...].astype(f32)
    for v in range(group):
        span = slice(v * steps, (v + 1) * steps)
        parts = [mixed[tile, pl.ds(v, steps, stride=group), :] for tile in range(width // LANES)]
        total = jnp.concatenate(parts, axis=1) + pos
        rows_sum[span, :] = total
        normed[span, :] = normalise(total, gain_one)
    rows = normed[...]
    queries[...] = (
        jnp.dot(rows, wq_ref[0], preferred_element_type=f32) * head_dim ** (-0.5)
    ).astype(jnp.bfloat16)
    key_rows[...] = jnp.dot(rows, wk_ref[0], preferred_element_type=f32).astype(jnp.bfloat16)
    values[...] = jnp.dot(rows, wv_ref[0], preferred_element_type=f32).astype(jnp.bfloat16)

    base = first_vertex + pl.program_id(0) * group

    zero = jnp.zeros((steps, pair), jnp.bfloat16)
    for v in range(group):
        first = first_ref[base + v]
        allowed = order[...] >= first
        span = slice(v * steps, (v + 1) * steps)
        for p in range(width // pair):
            lanes = slice(p * pair, (p + 1) * pair)
            q = queries[span, lanes]
            stacked = jnp.concatenate(
                [jnp.where(left, q, zero), jnp.where(left, zero, q)], axis=0
            )
            scores = lax.dot_general(
                key_rows[span, lanes], stacked, (((1,), (1,)), ((), ())), preferred_element_type=f32
            )
            scores = jnp.where(allowed, scores, -1e30)
            top = jnp.max(scores, axis=0, keepdims=True)
            raised = jnp.exp(scores - top)
            weights = (raised * (1.0 / jnp.sum(raised, axis=0, keepdims=True))).astype(jnp.bfloat16)
            both = lax.dot_general(
                weights, values[span, lanes], (((0,), (0,)), ((), ())), preferred_element_type=f32
            )
            joined[span, lanes] = jnp.where(left, both[:steps], both[steps:]).astype(jnp.bfloat16)

    attended = rows_sum[...] + jnp.dot(joined[...], wo_ref[0], preferred_element_type=f32)
    inner = jax.nn.gelu(
        jnp.dot(normalise(attended, gain_two), wu_ref[0], preferred_element_type=f32)
    ).astype(jnp.bfloat16)
    finished = attended + jnp.dot(inner, wd_ref[0], preferred_element_type=f32)
    for tile in range(width // LANES):
        lanes = slice(tile * LANES, (tile + 1) * LANES)
        for v in range(group):
            mixed[tile, pl.ds(v, steps, stride=group), :] = finished[
                v * steps : (v + 1) * steps, lanes
            ]
        out_ref[:, :, lanes] = mixed[tile].reshape(steps, group, LANES).astype(jnp.bfloat16)


def temporal(
    rows, first_seen, pos_embed, w_query, w_key, w_value, w_out, w_up, w_down, norm_gain, layer, chunk
):
    steps, count, width = rows.shape
    inner = w_up.shape[-1]
    group = min(GROUP, count)

    def weight(array):
        return pl.BlockSpec(
            (1,) + array.shape[1:], lambda i: (layer, 0, 0), pipeline_mode=pl.Buffered(1)
        )

    size = steps * group
    flops = 2 * steps * count * width * (4 * width + 2 * inner)
    return pl.pallas_call(
        functools.partial(temporal_kernel, first_vertex=chunk * count),
        grid=(count // group,),
        out_shape=jax.ShapeDtypeStruct(rows.shape, jnp.bfloat16),
        in_specs=[
            pl.BlockSpec(memory_space=pltpu.SMEM),
            pl.BlockSpec((steps, group, width), lambda i: (0, i, 0)),
            pl.BlockSpec(pos_embed.shape, lambda i: (0, 0), pipeline_mode=pl.Buffered(1)),
            weight(w_query),
            weight(w_key),
            weight(w_value),
            weight(w_out),
            weight(w_up),
            weight(w_down),
            weight(norm_gain),
        ],
        out_specs=pl.BlockSpec((steps, group, width), lambda i: (0, i, 0)),
        scratch_shapes=[
            pltpu.VMEM((width // LANES, size, LANES), jnp.float32),
            pltpu.VMEM((size, width), jnp.float32),
            pltpu.VMEM((size, width), jnp.bfloat16),
            pltpu.VMEM((size, width), jnp.bfloat16),
            pltpu.VMEM((size, width), jnp.bfloat16),
            pltpu.VMEM((size, width), jnp.bfloat16),
            pltpu.VMEM((size, width), jnp.bfloat16),
            pltpu.VMEM((steps, 2 * width // HEADS), jnp.int32),
        ],
        compiler_params=pltpu.CompilerParams(vmem_limit_bytes=VMEM_LIMIT),
        cost_estimate=pl.CostEstimate(
            flops=flops, transcendentals=0, bytes_accessed=4 * steps * count * width + 4 * 2**20
        ),
        name=f"temporal_{layer}_{chunk}",
    )(first_seen, rows, pos_embed, w_query, w_key, w_value, w_out, w_up, w_down, norm_gain)


def on_device(
    features,
    adjacency,
    first_seen,
    pos_embed,
    w_struct,
    w_query,
    w_key,
    w_value,
    w_out,
    w_up,
    w_down,
    norm_gain,
    *,
    owners,
):
    snapshots, nodes, width = features.shape

    def exchange(array):
        return lax.all_to_all(array, "snap", split_axis=0, concat_axis=0, tiled=True)

    hidden = (features,)
    for layer in range(BLOCKS):
        arrived = [
            exchange(structure(hidden, adjacency, w_struct, layer, chunk, owners))
            for chunk in range(CHUNKS)
        ]
        hidden = []
        for chunk in range(CHUNKS):
            rows = arrived[chunk].shape[2]
            finished = temporal(
                arrived[chunk].reshape(owners * snapshots, rows, width),
                first_seen,
                pos_embed,
                w_query,
                w_key,
                w_value,
                w_out,
                w_up,
                w_down,
                norm_gain,
                layer,
                chunk,
            )
            hidden.append(exchange(finished.reshape(owners, snapshots, rows, width)))
    joined = jnp.concatenate(hidden, axis=2)
    return joined.transpose(1, 0, 2, 3).reshape(snapshots, nodes, width)


def solution(mesh):
    in_specs = (
        P("snap", "clus", None),
        P("snap", "clus", None),
        P(("clus", "snap")),
        P(),
        P(),
        P(),
        P(),
        P(),
        P(),
        P(),
        P(),
        P(),
    )
    out_specs = P("snap", "clus", None)
    return jax.shard_map(
        functools.partial(on_device, owners=mesh.shape["snap"]),
        mesh=mesh,
        in_specs=in_specs,
        out_specs=out_specs,
        check_vma=False,
    )
```

time: 313 us -> 234 us (0.75); the launches traced: 307 us -> 233 us
  Pallas kernels: 0 us -> 115 us
  matrix products: 87.6 us -> 0 us
  blocking collectives: 93.4 us -> 41.8 us
  local copies, waits for them, and re-layouts: 70.6 us -> 19.9 us
  starting transfers between devices: 7.16 us -> 32.8 us
  other arithmetic: 20.8 us -> 1.39 us
  waiting for transfers between devices: 26.9 us -> 21.5 us
    pallas_call x0 -> x8, Pallas kernels: none -> 115 us  [the longest x4 98.9 us: temporal(): pl.pallas_call(functools.partial(temporal_kernel, first_vertex=chunk * co...]
    dot_general x16 -> x0, matrix products: 87.6 us -> none  [the longest x2 17.9 us: temporal(): jnp.einsum('vhtj,jvhd->tvhd', weights, values, preferred_element_type=jnp...]
    all_to_all x3 -> x2, blocking collectives: 93.4 us -> 41.8 us  [exchange(): lax.all_to_all(array, 'snap', split_axis=0, concat_axis=0, tiled=True)]
    reshape x8 -> x0, local copies, waits for them, and re-layouts: 38.9 us -> none  [the longest x2 11.5 us: temporal(): attended_heads.astype(jnp.bfloat16).reshape(-1, model_width)]
    all_to_all x1 -> x6, starting transfers between devices: 7.16 us -> 32.8 us  [exchange(): lax.all_to_all(array, 'snap', split_axis=0, concat_axis=0, tiled=True)]
    convert_element_type x6 -> x0, local copies, waits for them, and re-layouts: 21.9 us -> none  [the longest x2 14.1 us: temporal(): attended_heads.astype(jnp.bfloat16).reshape(-1, model_width)]
    unnamed x34 -> x48, local copies, waits for them, and re-layouts: 7.95 us -> 18.4 us
    sub x2 -> x0, other arithmetic: 9.12 us -> none  [temporal(): weights = jax.nn.softmax(scores, axis=-1).astype(jnp.bfloat16)]
  transfers between devices with their start and end apart: 1 -> 6, of which waited for: 1 -> 2; matrix products, arithmetic and copies ran while one was open for 0% -> 0% of each run, Pallas kernels for 0% -> 46%
where the time goes in v1:
time: 234 us; the launch traced here: 233 us
  Pallas kernels  115 us (49%)
  blocking collectives  41.8 us (18%)
  starting transfers between devices  32.8 us (14%)
  waiting for transfers between devices  21.5 us (9%)
  local copies, waits for them, and re-layouts  19.9 us (9%)
    pallas_call x4, Pallas kernels, temporal(): pl.pallas_call(functools.partial(temporal_kernel, first_vertex=chunk * co...  98.9 us
    all_to_all x2, blocking collectives, exchange(): lax.all_to_all(array, 'snap', split_axis=0, concat_axis=0, tiled=True)  41.8 us
    all_to_all x6, starting transfers between devices, exchange(): lax.all_to_all(array, 'snap', split_axis=0, concat_axis=0, tiled=True)  32.8 us
    all_to_all x6, waiting for transfers between devices, exchange(): lax.all_to_all(array, 'snap', split_axis=0, concat_axis=0, tiled=True)  21.5 us
    unnamed x48, local copies, waits for them, and re-layouts  18.4 us
    pallas_call x4, Pallas kernels, structure(): pl.pallas_call(functools.partial(structure_kernel, pieces=pieces, chunk=c...  16.5 us
  transfers between devices with their start and end apart: 6, of which 2 were waited for; matrix products, arithmetic and copies ran while one was open for 0% of the time, Pallas kernels for 46%

profile of v1, /device:TPU:1, one launch (start us, length us, event | category | flops | bytes accessed | tf_op | source)
XLA Modules:
  0.0 232.8 jit_solution(1860459802008022546)
XLA Ops:
  0.0 1.2 copy-done
  1.2 1.6 copy-done.2
  2.8 4.2 %structure_0_1.1 = bf16[16,4,16,512]{3,2,1,0:T(8,128)(2,1)S(1)} custom-call(bf16[4,512,512]{2,1,0:T(8,128)(2,1)S(1)} %copy-done.2, s32[4,16,2,16,512]{4,3,2,1,0:T(8,128)} %bitcast.17, bf16[2,512,512]{2,1,0:T(8,128)(2,1)S(1)} %copy-done), custom_call_target="tpu_custom_call" | custom-call | flops 1073741824 | bytes 4194304 | tf_op jit(solution)/shard_map/structure_0_1/pallas_call | solution.py:60
  8.0 7.0 %all-to-all-start.2 = ((bf16[16,4,16,512]{3,2,1,0:T(8,128)(2,1)}), bf16[16,4,16,512]{3,2,1,0:T(8,128)(2,1)}, u32[]{:S(2)}, u32[]{:S(2)}) async-start(bf16[16,4,16,512]{3,2,1,0:T(8,128)(2,1)} %copy-done.7), calls=%async_computation.2 | async-start | bytes 2097152 | tf_op jit(solution)/shard_map/all_to_all | solution.py:242
  15.0 4.0 %structure_0_0.1 = bf16[16,4,16,512]{3,2,1,0:T(8,128)(2,1)S(1)} custom-call(bf16[4,512,512]{2,1,0:T(8,128)(2,1)S(1)} %copy-done.3, s32[4,16,2,16,512]{4,3,2,1,0:T(8,128)} %bitcast.18, bf16[2,512,512]{2,1,0:T(8,128)(2,1)S(1)} %copy-done.1), custom_call_target="tpu_custom_call" | custom-call | flops 1073741824 | bytes 4194304 | tf_op jit(solution)/shard_map/structure_0_0/pallas_call | solution.py:60
  20.0 10.7 %all-to-all-done.2 = bf16[16,4,16,512]{3,2,1,0:T(8,128)(2,1)} async-done(((bf16[16,4,16,512]{3,2,1,0:T(8,128)(2,1)}), bf16[16,4,16,512]{3,2,1,0:T(8,128)(2,1)}, u32[]{:S(2)}, u32[]{:S(2)}) %all-to-all-start.2) | async-done | bytes 1048608 | tf_op jit(solution)/shard_map/all_to_all | solution.py:242
  30.8 4.4 %all-to-all-start = ((bf16[16,4,16,512]{3,2,1,0:T(8,128)(2,1)}), bf16[16,4,16,512]{3,2,1,0:T(8,128)(2,1)S(1)}, u32[]{:S(2)}, u32[]{:S(2)}) async-start(bf16[16,4,16,512]{3,2,1,0:T(8,128)(2,1)} %copy-done.5), calls=%async_computation | async-start | bytes 2097152 | tf_op jit(solution)/shard_map/all_to_all | solution.py:242
  36.4 1.2 copy-done.17
  37.7 24.6 %temporal_0_1.1 = bf16[64,16,512]{2,1,0:T(8,128)(2,1)S(1)} custom-call(s32[32]{0:T(128)S(1)} %copy-done.23, bf16[64,16,512]{2,1,0:T(8,128)(2,1)} %bitcast.3.x_ref, bf16[64,512]{1,0:T(8,128)(2,1)S(1)} %copy-done.21, bf16[2,512,512]{2,1,0:T(8,128)(2,1)S(1)} %copy-done.10, bf16[2,512,512]{2,1,0:T(8,128)(2,1)S(1)} %copy-done.13, ...), custom_call_target="tpu_custom_call" | custom-call | flops 4294967296 | bytes 6291456 | tf_op jit(solution)/shard_map/temporal_0_1/pallas_call | solution.py:188
  63.2 5.8 %all-to-all-start.3 = ((bf16[16,4,16,512]{3,2,1,0:T(8,128)(2,1)}), bf16[16,4,16,512]{3,2,1,0:T(8,128)(2,1)S(1)}, u32[]{:S(2)}, u32[]{:S(2)}) async-start(bf16[16,4,16,512]{3,2,1,0:T(8,128)(2,1)} %bitcast.14), calls=%async_computation.3 | async-start | bytes 2097152 | tf_op jit(solution)/shard_map/all_to_all | solution.py:242
  72.7 24.5 %temporal_0_0.1 = bf16[64,16,512]{2,1,0:T(8,128)(2,1)S(1)} custom-call(s32[32]{0:T(128)S(1)} %copy-done.23, bf16[64,16,512]{2,1,0:T(8,128)(2,1)S(1)} %bitcast.12, bf16[64,512]{1,0:T(8,128)(2,1)S(1)} %copy-done.21, bf16[2,512,512]{2,1,0:T(8,128)(2,1)S(1)} %copy-done.11, bf16[2,512,512]{2,1,0:T(8,128)(2,1)S(1)} %copy-done.14, ...), custom_call_target="tpu_custom_call" | custom-call | flops 4294967296 | bytes 6291456 | tf_op jit(solution)/shard_map/temporal_0_0/pallas_call | solution.py:188
  98.2 21.0 %all_to_all.40.refs_0_ = bf16[16,4,16,512]{3,2,1,0:T(8,128)(2,1)S(1)} all-to-all(bf16[16,4,16,512]{3,2,1,0:T(8,128)(2,1)} %bitcast.15), channel_id=1, replica_groups=mesh['snap'=16,'clus'=8] {'snap'}, dimensions={0} | all-to-all | bytes 2097152 | tf_op jit(solution)/shard_map/all_to_all | solution.py:242
  119.2 4.1 %structure_1_0.1 = bf16[16,4,16,512]{3,2,1,0:T(8,128)(2,1)S(1)} custom-call(bf16[16,4,16,512]{3,2,1,0:T(8,128)(2,1)S(1)} %all_to_all.40.refs_0_, bf16[16,4,16,512]{3,2,1,0:T(8,128)(2,1)S(1)} %all-to-all-done.3.refs_1_, s32[4,16,2,16,512]{4,3,2,1,0:T(8,128)} %bitcast.19, bf16[2,512,512]{2,1,0:T(8,128)(2,1)S(1)} %copy-done.1), custom_call_target="tpu_custom_call" | custom-call | flops 1073741824 | bytes 4194304 | tf_op jit(solution)/shard_map/structure_1_0/pallas_call | solution.py:60
  124.3 5.3 %all-to-all-start.4 = ((bf16[16,4,16,512]{3,2,1,0:T(8,128)(2,1)}), bf16[16,4,16,512]{3,2,1,0:T(8,128)(2,1)}, u32[]{:S(2)}, u32[]{:S(2)}) async-start(bf16[16,4,16,512]{3,2,1,0:T(8,128)(2,1)} %copy-done.6), calls=%async_computation.4 | async-start | bytes 2097152 | tf_op jit(solution)/shard_map/all_to_all | solution.py:242
  129.6 4.1 %structure_1_1.1 = bf16[16,4,16,512]{3,2,1,0:T(8,128)(2,1)S(1)} custom-call(bf16[16,4,16,512]{3,2,1,0:T(8,128)(2,1)S(1)} %all_to_all.40.refs_0_, bf16[16,4,16,512]{3,2,1,0:T(8,128)(2,1)S(1)} %all-to-all-done.3.refs_1_, s32[4,16,2,16,512]{4,3,2,1,0:T(8,128)} %bitcast.20, bf16[2,512,512]{2,1,0:T(8,128)(2,1)S(1)} %copy-done.1), custom_call_target="tpu_custom_call" | custom-call | flops 1073741824 | bytes 4194304 | tf_op jit(solution)/shard_map/structure_1_1/pallas_call | solution.py:60
  134.7 10.7 %all-to-all-done.4 = bf16[16,4,16,512]{3,2,1,0:T(8,128)(2,1)} async-done(((bf16[16,4,16,512]{3,2,1,0:T(8,128)(2,1)}), bf16[16,4,16,512]{3,2,1,0:T(8,128)(2,1)}, u32[]{:S(2)}, u32[]{:S(2)}) %all-to-all-start.4) | async-done | bytes 1048608 | tf_op jit(solution)/shard_map/all_to_all | solution.py:242
  145.5 4.4 %all-to-all-start.6 = ((bf16[16,4,16,512]{3,2,1,0:T(8,128)(2,1)}), bf16[16,4,16,512]{3,2,1,0:T(8,128)(2,1)S(1)}, u32[]{:S(2)}, u32[]{:S(2)}) async-start(bf16[16,4,16,512]{3,2,1,0:T(8,128)(2,1)} %copy-done.4), calls=%async_computation.6 | async-start | bytes 2097152 | tf_op jit(solution)/shard_map/all_to_all | solution.py:242
  151.1 25.3 %temporal_1_0.1 = bf16[64,16,512]{2,1,0:T(8,128)(2,1)} custom-call(s32[32]{0:T(128)S(1)} %copy-done.23, bf16[64,16,512]{2,1,0:T(8,128)(2,1)} %bitcast.5.x_ref, bf16[64,512]{1,0:T(8,128)(2,1)S(1)} %copy-done.21, bf16[2,512,512]{2,1,0:T(8,128)(2,1)S(1)} %copy-done.12, bf16[2,512,512]{2,1,0:T(8,128)(2,1)S(1)} %copy-done.15, ...), custom_call_target="tpu_custom_call" | custom-call | flops 4294967296 | bytes 6291456 | tf_op jit(solution)/shard_map/temporal_1_0/pallas_call | solution.py:188
  176.4 5.8 %all-to-all-start.5 = ((bf16[16,4,16,512]{3,2,1,0:T(8,128)(2,1)}), bf16[16,4,16,512]{3,2,1,0:T(8,128)(2,1)}, u32[]{:S(2)}, u32[]{:S(2)}) async-start(bf16[16,4,16,512]{3,2,1,0:T(8,128)(2,1)} %bitcast.6), calls=%async_computation.5 | async-start | bytes 2097152 | tf_op jit(solution)/shard_map/all_to_all | solution.py:242
  183.5 1.2 copy-done.20
  184.7 24.5 %temporal_1_1.1 = bf16[64,16,512]{2,1,0:T(8,128)(2,1)S(1)} custom-call(s32[32]{0:T(128)S(1)} %copy-done.23, bf16[64,16,512]{2,1,0:T(8,128)(2,1)S(1)} %bitcast.13, bf16[64,512]{1,0:T(8,128)(2,1)S(1)} %copy-done.21, bf16[2,512,512]{2,1,0:T(8,128)(2,1)S(1)} %copy-done.12, bf16[2,512,512]{2,1,0:T(8,128)(2,1)S(1)} %copy-done.16, ...), custom_call_target="tpu_custom_call" | custom-call | flops 4294967296 | bytes 6291456 | tf_op jit(solution)/shard_map/temporal_1_1/pallas_call | solution.py:188
  209.2 20.8 %all_to_all.41 = bf16[16,4,16,512]{3,2,1,0:T(8,128)(2,1)S(1)} all-to-all(bf16[16,4,16,512]{3,2,1,0:T(8,128)(2,1)S(1)} %bitcast.16), channel_id=1, replica_groups=mesh['snap'=16,'clus'=8] {'snap'}, dimensions={0} | all-to-all | bytes 2097152 | tf_op jit(solution)/shard_map/all_to_all | solution.py:242
  230.0 1.4 maximum_bitcast_fusion
  231.4 1.5 copy.13
  (48 shorter events, 13.2 us)
Async XLA Ops:
  0.0 1.2 copy-start
  1.2 1.6 copy-start.2
  2.8 12.2 %copy-start.3 = (bf16[4,512,512]{2,1,0:T(8,128)(2,1)S(1)}, bf16[4,512,512]{2,1,0:T(8,128)(2,1)}, u32[]{:S(2)}) copy-start(bf16[4,512,512]{2,1,0:T(8,128)(2,1)} %refs_0_.3) | copy-start | bytes 6291460
  8.0 7.0 %copy-start.1 = (bf16[2,512,512]{2,1,0:T(8,128)(2,1)S(1)}, bf16[2,512,512]{2,1,0:T(8,128)(2,1)}, u32[]{:S(2)}) copy-start(bf16[2,512,512]{2,1,0:T(8,128)(2,1)} %refs_3_.3) | copy-start | bytes 3145732
  8.0 22.8 %all-to-all-start.2 = ((bf16[16,4,16,512]{3,2,1,0:T(8,128)(2,1)}), bf16[16,4,16,512]{3,2,1,0:T(8,128)(2,1)}, u32[]{:S(2)}, u32[]{:S(2)}) async-start(bf16[16,4,16,512]{3,2,1,0:T(8,128)(2,1)} %copy-done.7), calls=%async_computation.2 | async-start | bytes 2097152 | tf_op jit(solution)/shard_map/all_to_all | solution.py:242
  20.0 15.1 %copy-start.10 = (bf16[2,512,512]{2,1,0:T(8,128)(2,1)S(1)}, bf16[2,512,512]{2,1,0:T(8,128)(2,1)}, u32[]{:S(2)}) copy-start(bf16[2,512,512]{2,1,0:T(8,128)(2,1)} %wq_ref.7) | copy-start | bytes 3145732
  20.0 15.1 %copy-start.21 = (bf16[64,512]{1,0:T(8,128)(2,1)S(1)}, bf16[64,512]{1,0:T(8,128)(2,1)}, u32[]{:S(2)}) copy-start(bf16[64,512]{1,0:T(8,128)(2,1)} %pos_ref.7) | copy-start | bytes 196612
  20.0 15.2 %copy-start.22 = (f32[2,2,512]{2,1,0:T(2,128)S(1)}, f32[2,2,512]{2,1,0:T(2,128)}, u32[]{:S(2)}) copy-start(f32[2,2,512]{2,1,0:T(2,128)} %gain_ref.7) | copy-start | bytes 24580
  20.0 15.2 %copy-start.23 = (s32[32]{0:T(128)S(1)}, s32[32]{0:T(128)}, u32[]{:S(2)}) copy-start(s32[32]{0:T(128)} %first_ref.7) | copy-start | bytes 388
  30.8 32.5 %all-to-all-start = ((bf16[16,4,16,512]{3,2,1,0:T(8,128)(2,1)}), bf16[16,4,16,512]{3,2,1,0:T(8,128)(2,1)S(1)}, u32[]{:S(2)}, u32[]{:S(2)}) async-start(bf16[16,4,16,512]{3,2,1,0:T(8,128)(2,1)} %copy-done.5), calls=%async_computation | async-start | bytes 2097152 | tf_op jit(solution)/shard_map/all_to_all | solution.py:242
  35.2 1.2 copy-start.13
  36.4 1.2 copy-start.17
  63.2 34.9 %all-to-all-start.3 = ((bf16[16,4,16,512]{3,2,1,0:T(8,128)(2,1)}), bf16[16,4,16,512]{3,2,1,0:T(8,128)(2,1)S(1)}, u32[]{:S(2)}, u32[]{:S(2)}) async-start(bf16[16,4,16,512]{3,2,1,0:T(8,128)(2,1)} %bitcast.14), calls=%async_computation.3 | async-start | bytes 2097152 | tf_op jit(solution)/shard_map/all_to_all | solution.py:242
  69.0 1.2 copy-start.11
  70.3 1.2 copy-start.14
  71.5 1.2 copy-start.18
  124.3 21.2 %all-to-all-start.4 = ((bf16[16,4,16,512]{3,2,1,0:T(8,128)(2,1)}), bf16[16,4,16,512]{3,2,1,0:T(8,128)(2,1)}, u32[]{:S(2)}, u32[]{:S(2)}) async-start(bf16[16,4,16,512]{3,2,1,0:T(8,128)(2,1)} %copy-done.6), calls=%async_computation.4 | async-start | bytes 2097152 | tf_op jit(solution)/shard_map/all_to_all | solution.py:242
  134.7 15.2 %copy-start.12 = (bf16[2,512,512]{2,1,0:T(8,128)(2,1)S(1)}, bf16[2,512,512]{2,1,0:T(8,128)(2,1)}, u32[]{:S(2)}) copy-start(bf16[2,512,512]{2,1,0:T(8,128)(2,1)} %wq_ref.7) | copy-start | bytes 3145732
  134.7 15.2 %copy-start.15 = (bf16[2,512,512]{2,1,0:T(8,128)(2,1)S(1)}, bf16[2,512,512]{2,1,0:T(8,128)(2,1)}, u32[]{:S(2)}) copy-start(bf16[2,512,512]{2,1,0:T(8,128)(2,1)} %wk_ref.7) | copy-start | bytes 3145732
  145.5 31.0 %all-to-all-start.6 = ((bf16[16,4,16,512]{3,2,1,0:T(8,128)(2,1)}), bf16[16,4,16,512]{3,2,1,0:T(8,128)(2,1)S(1)}, u32[]{:S(2)}, u32[]{:S(2)}) async-start(bf16[16,4,16,512]{3,2,1,0:T(8,128)(2,1)} %copy-done.4), calls=%async_computation.6 | async-start | bytes 2097152 | tf_op jit(solution)/shard_map/all_to_all | solution.py:242
  149.9 1.2 copy-start.19
  176.4 32.7 %all-to-all-start.5 = ((bf16[16,4,16,512]{3,2,1,0:T(8,128)(2,1)}), bf16[16,4,16,512]{3,2,1,0:T(8,128)(2,1)}, u32[]{:S(2)}, u32[]{:S(2)}) async-start(bf16[16,4,16,512]{3,2,1,0:T(8,128)(2,1)} %bitcast.6), calls=%async_computation.5 | async-start | bytes 2097152 | tf_op jit(solution)/shard_map/all_to_all | solution.py:242
  182.2 1.2 copy-start.16
  183.5 1.2 copy-start.20
  (6 other events, 5.8 us)

commit v2 on v1

v2 whole, which is shorter than its diff:
```python
import functools

import jax
import jax.numpy as jnp
from jax import lax
from jax.experimental import pallas as pl
from jax.experimental.pallas import tpu as pltpu
from jax.sharding import PartitionSpec as P

HEADS = 8
BLOCKS = 2
GROUP = 8
LANES = 128
LEAD_QUARTERS = 3
VMEM_LIMIT = 40 * 1024 * 1024


def in_hbm(array):
    return pltpu.with_memory_space_constraint(array, pltpu.HBM)


def normalise(rows, gain):
    average = jnp.mean(rows, axis=-1, keepdims=True)
    centred = rows - average
    spread = jnp.mean(centred * centred, axis=-1, keepdims=True)
    return (centred * lax.rsqrt(spread + 1e-05) * gain).astype(jnp.bfloat16)


def structure_kernel(hidden_ref, adjacency_ref, weight_ref, out_ref, *, start):
    owners, _, rows, width = out_ref.shape
    nodes = adjacency_ref.shape[-1]
    hidden = hidden_ref[...].reshape(nodes, width)
    own = hidden.reshape(owners, nodes // owners, width)[:, start : start + rows]
    own = own.reshape(owners * rows, width).astype(jnp.float32)
    links = adjacency_ref[0, :, start : start + rows, :]
    links = links.reshape(owners * rows, nodes).astype(jnp.float32)
    degree = 1.0 + jnp.sum(links, axis=1, keepdims=True)
    summed = jnp.dot(links.astype(jnp.bfloat16), hidden, preferred_element_type=jnp.float32)
    mixture = ((summed + own) / degree).astype(jnp.bfloat16)
    mapped = jnp.dot(mixture, weight_ref[0], preferred_element_type=jnp.float32)
    bent = jnp.where(mapped > 0, mapped, jnp.exp(jnp.minimum(mapped, 0.0)) - 1.0)
    out_ref[...] = (bent + own).astype(jnp.bfloat16).reshape(out_ref.shape)


def structure(hidden, adjacency, w_struct, layer, start, rows, owners):
    snapshots, nodes, _ = adjacency.shape
    width = w_struct.shape[-1]
    share = nodes // owners
    if hidden.ndim == 3:
        hidden_spec = pl.BlockSpec((1, nodes, width), lambda s: (s, 0, 0))
    else:
        hidden_spec = pl.BlockSpec((owners, 1, share, width), lambda s: (0, s, 0, 0))
    links = adjacency.reshape(snapshots, owners, share, nodes)
    flops = 2 * snapshots * owners * rows * width * (nodes + width)
    return pl.pallas_call(
        functools.partial(structure_kernel, start=start),
        grid=(snapshots,),
        out_shape=pltpu.HBM((owners, snapshots, rows, width), jnp.bfloat16),
        in_specs=[
            hidden_spec,
            pl.BlockSpec((1, owners, share, nodes), lambda s: (s, 0, 0, 0)),
            pl.BlockSpec((1, width, width), lambda s: (layer, 0, 0)),
        ],
        out_specs=pl.BlockSpec((owners, 1, rows, width), lambda s: (0, s, 0, 0)),
        compiler_params=pltpu.CompilerParams(vmem_limit_bytes=VMEM_LIMIT),
        cost_estimate=pl.CostEstimate(
            flops=flops, transcendentals=0, bytes_accessed=snapshots * owners * rows * nodes * 8
        ),
        name=f"structure_{layer}_{start}",
    )(in_hbm(hidden), in_hbm(links), in_hbm(w_struct))


def temporal_kernel(
    first_ref,
    x_ref,
    pos_ref,
    gain_ref,
    wq_hbm,
    wk_hbm,
    wv_hbm,
    wo_hbm,
    wu_hbm,
    wd_hbm,
    out_ref,
    wq,
    wk,
    wv,
    wo,
    wu,
    wd,
    sems,
    mixed,
    rows_sum,
    normed,
    queries,
    key_rows,
    values,
    joined,
    order,
    scores,
    weights,
    *,
    layer,
    first_vertex,
):
    steps, group, width = x_ref.shape
    head_dim = width // HEADS
    pair = 2 * head_dim
    f32 = jnp.float32
    pairs = ((wq_hbm, wq), (wk_hbm, wk), (wv_hbm, wv), (wo_hbm, wo), (wu_hbm, wu), (wd_hbm, wd))
    fetches = [
        pltpu.make_async_copy(source.at[layer], target, sems.at[index])
        for index, (source, target) in enumerate(pairs)
    ]

    row = lax.broadcasted_iota(jnp.int32, (steps, pair), 0)
    lane = lax.broadcasted_iota(jnp.int32, (steps, pair), 1)
    column = lane & (head_dim - 1)
    left = lane < head_dim

    @pl.when(pl.program_id(0) == 0)
    def _():
        for fetch in fetches:
            fetch.start()
        order[...] = jnp.where(row < column, row, jnp.where(row == column, 1 << 20, -1))

    for tile in range(width // LANES):
        mixed[tile] = (
            x_ref[:, :, tile * LANES : (tile + 1) * LANES]
            .astype(f32)
            .reshape(steps * group, LANES)
        )
    gain_one = gain_ref[0, 0:1, :]
    gain_two = gain_ref[0, 1:2, :]
    pos = pos_ref[...].astype(f32)
    for v in range(group):
        span = slice(v * steps, (v + 1) * steps)
        parts = [mixed[tile, pl.ds(v, steps, stride=group), :] for tile in range(width // LANES)]
        total = jnp.concatenate(parts, axis=1) + pos
        rows_sum[span, :] = total
        normed[span, :] = normalise(total, gain_one)

    @pl.when(pl.program_id(0) == 0)
    def _():
        for fetch in fetches[:3]:
            fetch.wait()

    rows = normed[...]
    queries[...] = (jnp.dot(rows, wq[...], preferred_element_type=f32) * head_dim ** (-0.5)).astype(
        jnp.bfloat16
    )
    key_rows[...] = jnp.dot(rows, wk[...], preferred_element_type=f32).astype(jnp.bfloat16)
    values[...] = jnp.dot(rows, wv[...], preferred_element_type=f32).astype(jnp.bfloat16)

    base = first_vertex + pl.program_id(0) * group
    zero = jnp.zeros((steps, pair), jnp.bfloat16)
    for v in range(group):
        span = slice(v * steps, (v + 1) * steps)
        for p in range(width // pair):
            lanes = slice(p * pair, (p + 1) * pair)
            q = queries[span, lanes]
            stacked = jnp.concatenate([jnp.where(left, q, zero), jnp.where(left, zero, q)], axis=0)
            scores[span, lanes] = lax.dot_general(
                key_rows[span, lanes], stacked, (((1,), (1,)), ((), ())), preferred_element_type=f32
            )
    for v in range(group):
        allowed = order[...] >= first_ref[base + v]
        span = slice(v * steps, (v + 1) * steps)
        for p in range(width // pair):
            lanes = slice(p * pair, (p + 1) * pair)
            seen = jnp.where(allowed, scores[span, lanes], -1e30)
            raised = jnp.exp(seen - jnp.max(seen, axis=0, keepdims=True))
            share = 1.0 / jnp.sum(raised, axis=0, keepdims=True)
            weights[span, lanes] = (raised * share).astype(jnp.bfloat16)
    for v in range(group):
        span = slice(v * steps, (v + 1) * steps)
        for p in range(width // pair):
            lanes = slice(p * pair, (p + 1) * pair)
            both = lax.dot_general(
                weights[span, lanes],
                values[span, lanes],
                (((0,), (0,)), ((), ())),
                preferred_element_type=f32,
            )
            joined[span, lanes] = jnp.where(left, both[:steps], both[steps:]).astype(jnp.bfloat16)

    @pl.when(pl.program_id(0) == 0)
    def _():
        for fetch in fetches[3:]:
            fetch.wait()

    attended = rows_sum[...] + jnp.dot(joined[...], wo[...], preferred_element_type=f32)
    inner = jax.nn.gelu(
        jnp.dot(normalise(attended, gain_two), wu[...], preferred_element_type=f32)
    ).astype(jnp.bfloat16)
    finished = attended + jnp.dot(inner, wd[...], preferred_element_type=f32)
    for tile in range(width // LANES):
        lanes = slice(tile * LANES, (tile + 1) * LANES)
        for v in range(group):
            mixed[tile, pl.ds(v, steps, stride=group), :] = finished[
                v * steps : (v + 1) * steps, lanes
            ]
        out_ref[:, :, lanes] = mixed[tile].reshape(steps, group, LANES).astype(jnp.bfloat16)


def temporal_piece(
    rows, first_seen, pos_embed, weights, norm_gain, layer, start, out_count, previous
):
    steps, count, width = rows.shape
    group = min(GROUP, count)
    inner = weights[-1].shape[1]
    size = steps * group
    flops = 2 * steps * count * width * (4 * width + 2 * inner)
    hbm = pl.BlockSpec(memory_space=pltpu.HBM)
    kernel = functools.partial(temporal_kernel, layer=layer, first_vertex=start)
    operands = [first_seen, rows, pos_embed, norm_gain] + [in_hbm(w) for w in weights]
    in_specs = [
        pl.BlockSpec(memory_space=pltpu.SMEM),
        pl.BlockSpec((steps, group, width), lambda i: (0, i, 0)),
        pl.BlockSpec(pos_embed.shape, lambda i: (0, 0)),
        pl.BlockSpec((1,) + norm_gain.shape[1:], lambda i: (layer, 0, 0)),
    ] + [hbm] * len(weights)
    aliases = {}
    if previous is not None:
        aliases = {len(operands): 0}
        operands.append(previous)
        in_specs.append(hbm)
        inner_kernel = kernel

        def kernel(*refs):
            inner_kernel(*refs[: len(operands) - 1], *refs[len(operands) :])

    bf16 = jnp.bfloat16
    return pl.pallas_call(
        kernel,
        grid=(count // group,),
        out_shape=pltpu.HBM((steps, out_count, width), bf16),
        in_specs=in_specs,
        out_specs=pl.BlockSpec((steps, group, width), lambda i: (0, start // group + i, 0)),
        scratch_shapes=[pltpu.VMEM(w.shape[1:], bf16) for w in weights]
        + [
            pltpu.SemaphoreType.DMA((len(weights),)),
            pltpu.VMEM((width // LANES, size, LANES), jnp.float32),
            pltpu.VMEM((size, width), jnp.float32),
            pltpu.VMEM((size, width), bf16),
            pltpu.VMEM((size, width), bf16),
            pltpu.VMEM((size, width), bf16),
            pltpu.VMEM((size, width), bf16),
            pltpu.VMEM((size, width), bf16),
            pltpu.VMEM((steps, 2 * width // HEADS), jnp.int32),
            pltpu.VMEM((size, width), jnp.float32),
            pltpu.VMEM((size, width), bf16),
        ],
        input_output_aliases=aliases,
        compiler_params=pltpu.CompilerParams(vmem_limit_bytes=VMEM_LIMIT),
        cost_estimate=pl.CostEstimate(
            flops=flops, transcendentals=0, bytes_accessed=4 * steps * count * width + 4 * 2**20
        ),
        name=f"temporal_{layer}_{start}",
    )(*operands)


def temporal(x, first_seen, pos_embed, wq, wk, wv, wo, wu, wd, norm_gain, layer, chunk):
    return temporal_piece(
        x, first_seen, pos_embed, (wq, wk, wv, wo, wu, wd), norm_gain, layer, 0, x.shape[1], None
    )


def on_device(
    features,
    adjacency,
    first_seen,
    pos_embed,
    w_struct,
    w_query,
    w_key,
    w_value,
    w_out,
    w_up,
    w_down,
    norm_gain,
    *,
    owners,
):
    snapshots, nodes, width = features.shape
    share = nodes // owners
    lead = share * LEAD_QUARTERS // 4
    chunks = ((0, lead), (lead, share - lead)) if lead < share else ((0, share),)
    weights = (w_query, w_key, w_value, w_out, w_up, w_down)

    def exchange(array):
        return lax.all_to_all(array, "snap", split_axis=0, concat_axis=0, tiled=True)

    hidden = features
    for layer in range(BLOCKS):
        arrived = [
            exchange(structure(hidden, adjacency, w_struct, layer, start, rows, owners))
            for start, rows in chunks
        ]
        finished = None
        for (start, rows), piece in zip(chunks, arrived):
            finished = temporal_piece(
                piece.reshape(owners * snapshots, rows, width),
                first_seen,
                pos_embed,
                weights,
                norm_gain,
                layer,
                start,
                share,
                finished,
            )
        hidden = exchange(finished.reshape(owners, snapshots, share, width))
    return hidden.transpose(1, 0, 2, 3).reshape(snapshots, nodes, width)


def solution(mesh):
    in_specs = (
        P("snap", "clus", None),
        P("snap", "clus", None),
        P(("clus", "snap")),
        P(),
        P(),
        P(),
        P(),
        P(),
        P(),
        P(),
        P(),
        P(),
    )
    out_specs = P("snap", "clus", None)
    return jax.shard_map(
        functools.partial(on_device, owners=mesh.shape["snap"]),
        mesh=mesh,
        in_specs=in_specs,
        out_specs=out_specs,
        check_vma=False,
    )
```

time: 234 us -> 191 us (0.82)
  Pallas kernels: 115 us -> 70.9 us
  blocking collectives: 41.8 us -> 64.6 us
  local copies, waits for them, and re-layouts: 19.9 us -> 1.58 us
  starting transfers between devices: 32.8 us -> 21 us
  waiting for transfers between devices: 21.5 us -> 32 us
    pallas_call x8, Pallas kernels: 115 us -> 70.9 us  [the longest x4 47.6 us: temporal_piece(): pl.pallas_call(kernel, grid=(count // group,), out_shape=pltpu.HBM((steps...]
    all_to_all x2, blocking collectives: 41.8 us -> 64.6 us  [exchange(): lax.all_to_all(array, 'snap', split_axis=0, concat_axis=0, tiled=True)]
    unnamed x48 -> x6, local copies, waits for them, and re-layouts: 18.4 us -> 0.02 us
    all_to_all x6 -> x4, starting transfers between devices: 32.8 us -> 21 us  [exchange(): lax.all_to_all(array, 'snap', split_axis=0, concat_axis=0, tiled=True)]
    all_to_all x6 -> x4, waiting for transfers between devices: 21.5 us -> 32 us  [exchange(): lax.all_to_all(array, 'snap', split_axis=0, concat_axis=0, tiled=True)]
  transfers between devices with their start and end apart: 6 -> 4, of which waited for: 2 -> 2; matrix products, arithmetic and copies ran while one was open for 0% -> 0% of each run, Pallas kernels for 46% -> 23%
where the time goes in v2:
time: 191 us; the launch traced here: 190 us
  Pallas kernels  70.9 us (37%)
  blocking collectives  64.6 us (34%)
  waiting for transfers between devices  32 us (17%)
  starting transfers between devices  21 us (11%)
    all_to_all x2, blocking collectives, exchange(): lax.all_to_all(array, 'snap', split_axis=0, concat_axis=0, tiled=True)  64.6 us
    pallas_call x4, Pallas kernels, temporal_piece(): pl.pallas_call(kernel, grid=(count // group,), out_shape=pltpu.HBM((steps...  47.6 us
    all_to_all x4, waiting for transfers between devices, exchange(): lax.all_to_all(array, 'snap', split_axis=0, concat_axis=0, tiled=True)  32 us
    pallas_call x4, Pallas kernels, structure(): pl.pallas_call(functools.partial(structure_kernel, start=start), grid=(sn...  23.3 us
    all_to_all x4, starting transfers between devices, exchange(): lax.all_to_all(array, 'snap', split_axis=0, concat_axis=0, tiled=True)  21 us
  transfers between devices with their start and end apart: 4, of which 2 were waited for; matrix products, arithmetic and copies ran while one was open for 0% of the time, Pallas kernels for 23%

profile of v2, /device:TPU:1, one launch (start us, length us, event | category | flops | bytes accessed | tf_op | source)
XLA Modules:
  0.0 190.2 jit_solution(2232458770299137790)
XLA Ops:
  0.0 6.4 %structure_0_0.1 = bf16[16,4,24,512]{3,2,1,0:T(8,128)(2,1)} custom-call(bf16[4,512,512]{2,1,0:T(8,128)(2,1)} %hidden_ref.3, s32[4,16,32,512]{3,2,1,0:T(8,128)} %bitcast.13, bf16[2,512,512]{2,1,0:T(8,128)(2,1)} %weight_ref.7), custom_call_target="tpu_custom_call" | custom-call | flops 1610612736 | bytes 6291456 | tf_op jit(solution)/shard_map/structure_0_0/pallas_call | solution.py:55
  6.4 6.9 %all-to-all-start.1 = ((bf16[16,4,24,512]{3,2,1,0:T(8,128)(2,1)}), bf16[16,4,24,512]{3,2,1,0:T(8,128)(2,1)S(1)}, u32[]{:S(2)}, u32[]{:S(2)}) async-start(bf16[16,4,24,512]{3,2,1,0:T(8,128)(2,1)} %structure_0_0.1), calls=%async_computation.1 | async-start | bytes 3145728 | tf_op jit(solution)/shard_map/all_to_all | solution.py:292
  13.3 0.0 copy-start.1
  13.3 0.0 copy-start.2
  13.3 5.5 %structure_0_24.1 = bf16[16,4,8,512]{3,2,1,0:T(8,128)(2,1)} custom-call(bf16[4,512,512]{2,1,0:T(8,128)(2,1)} %hidden_ref.3, s32[4,16,32,512]{3,2,1,0:T(8,128)} %bitcast.14, bf16[2,512,512]{2,1,0:T(8,128)(2,1)} %weight_ref.7), custom_call_target="tpu_custom_call" | custom-call | flops 536870912 | bytes 2097152 | tf_op jit(solution)/shard_map/structure_0_24/pallas_call | solution.py:55
  18.8 15.9 %all-to-all-done.1 = bf16[16,4,24,512]{3,2,1,0:T(8,128)(2,1)S(1)} async-done(((bf16[16,4,24,512]{3,2,1,0:T(8,128)(2,1)}), bf16[16,4,24,512]{3,2,1,0:T(8,128)(2,1)S(1)}, u32[]{:S(2)}, u32[]{:S(2)}) %all-to-all-start.1) | async-done | bytes 1572896 | tf_op jit(solution)/shard_map/all_to_all | solution.py:292
  34.6 4.7 %all-to-all-start = ((bf16[16,4,8,512]{3,2,1,0:T(8,128)(2,1)}), bf16[16,4,8,512]{3,2,1,0:T(8,128)(2,1)S(1)}, u32[]{:S(2)}, u32[]{:S(2)}) async-start(bf16[16,4,8,512]{3,2,1,0:T(8,128)(2,1)} %structure_0_24.1), calls=%async_computation | async-start | bytes 1048576 | tf_op jit(solution)/shard_map/all_to_all | solution.py:292
  39.3 0.0 copy-done
  39.3 0.0 copy-done.1
  39.3 0.0 copy-done.2
  39.3 16.8 %temporal_0_0.1.refs_10_ = bf16[64,32,512]{2,1,0:T(8,128)(2,1)} custom-call(s32[32]{0:T(128)S(1)} %copy-done.2, bf16[64,24,512]{2,1,0:T(8,128)(2,1)S(1)} %bitcast.12, bf16[64,512]{1,0:T(8,128)(2,1)S(1)} %copy-done, f32[2,2,512]{2,1,0:T(2,128)S(1)} %copy-done.1, bf16[2,512,512]{2,1,0:T(8,128)(2,1)} %refs_4_.3, bf16[2,512,512]{2,1,0:T(8,128)(2,1)} %refs_5_.3, ...), custom_call_target="tpu_custom_call" | custom-call | flops 6442450944 | bytes 7340032 | tf_op jit(solution)/shard_map/temporal_0_0/pallas_call | solution.py:234
  56.1 0.0 all-to-all-done
  56.1 7.0 %temporal_0_24.1 = bf16[64,32,512]{2,1,0:T(8,128)(2,1)} custom-call(s32[32]{0:T(128)S(1)} %copy-done.2, bf16[64,8,512]{2,1,0:T(8,128)(2,1)S(1)} %bitcast.9, bf16[64,512]{1,0:T(8,128)(2,1)S(1)} %copy-done, f32[2,2,512]{2,1,0:T(2,128)S(1)} %copy-done.1, bf16[2,512,512]{2,1,0:T(8,128)(2,1)} %refs_4_.3, ...), custom_call_target="tpu_custom_call", output_to_operand_aliasing={{}: (10, {})} | custom-call | flops 2147483648 | bytes 5242880 | tf_op jit(solution)/shard_map/temporal_0_24/pallas_call | solution.py:234
  63.2 32.3 %all_to_all.30.hidden_ref = bf16[16,4,32,512]{3,2,1,0:T(8,128)(2,1)} all-to-all(bf16[16,4,32,512]{3,2,1,0:T(8,128)(2,1)} %bitcast.18), channel_id=1, replica_groups=mesh['snap'=16,'clus'=8] {'snap'}, dimensions={0} | all-to-all | bytes 4194304 | tf_op jit(solution)/shard_map/all_to_all | solution.py:292
  95.5 6.2 %structure_1_0.1 = bf16[16,4,24,512]{3,2,1,0:T(8,128)(2,1)} custom-call(bf16[16,4,32,512]{3,2,1,0:T(8,128)(2,1)} %all_to_all.30.hidden_ref, s32[4,16,32,512]{3,2,1,0:T(8,128)} %bitcast.15, bf16[2,512,512]{2,1,0:T(8,128)(2,1)} %weight_ref.7), custom_call_target="tpu_custom_call" | custom-call | flops 1610612736 | bytes 6291456 | tf_op jit(solution)/shard_map/structure_1_0/pallas_call | solution.py:55
  101.7 4.8 %all-to-all-start.4 = ((bf16[16,4,24,512]{3,2,1,0:T(8,128)(2,1)}), bf16[16,4,24,512]{3,2,1,0:T(8,128)(2,1)S(1)}, u32[]{:S(2)}, u32[]{:S(2)}) async-start(bf16[16,4,24,512]{3,2,1,0:T(8,128)(2,1)} %structure_1_0.1), calls=%async_computation.4 | async-start | bytes 3145728 | tf_op jit(solution)/shard_map/all_to_all | solution.py:292
  106.5 5.3 %structure_1_24.1 = bf16[16,4,8,512]{3,2,1,0:T(8,128)(2,1)} custom-call(bf16[16,4,32,512]{3,2,1,0:T(8,128)(2,1)} %all_to_all.30.hidden_ref, s32[4,16,32,512]{3,2,1,0:T(8,128)} %bitcast.16, bf16[2,512,512]{2,1,0:T(8,128)(2,1)} %weight_ref.7), custom_call_target="tpu_custom_call" | custom-call | flops 536870912 | bytes 2097152 | tf_op jit(solution)/shard_map/structure_1_24/pallas_call | solution.py:55
  111.7 16.2 %all-to-all-done.4 = bf16[16,4,24,512]{3,2,1,0:T(8,128)(2,1)S(1)} async-done(((bf16[16,4,24,512]{3,2,1,0:T(8,128)(2,1)}), bf16[16,4,24,512]{3,2,1,0:T(8,128)(2,1)S(1)}, u32[]{:S(2)}, u32[]{:S(2)}) %all-to-all-start.4) | async-done | bytes 1572896 | tf_op jit(solution)/shard_map/all_to_all | solution.py:292
  127.9 4.6 %all-to-all-start.3 = ((bf16[16,4,8,512]{3,2,1,0:T(8,128)(2,1)}), bf16[16,4,8,512]{3,2,1,0:T(8,128)(2,1)S(1)}, u32[]{:S(2)}, u32[]{:S(2)}) async-start(bf16[16,4,8,512]{3,2,1,0:T(8,128)(2,1)} %structure_1_24.1), calls=%async_computation.3 | async-start | bytes 1048576 | tf_op jit(solution)/shard_map/all_to_all | solution.py:292
  132.5 16.8 %temporal_1_0.1.refs_10_ = bf16[64,32,512]{2,1,0:T(8,128)(2,1)} custom-call(s32[32]{0:T(128)S(1)} %copy-done.2, bf16[64,24,512]{2,1,0:T(8,128)(2,1)S(1)} %bitcast.11, bf16[64,512]{1,0:T(8,128)(2,1)S(1)} %copy-done, f32[2,2,512]{2,1,0:T(2,128)S(1)} %copy-done.1, bf16[2,512,512]{2,1,0:T(8,128)(2,1)} %refs_4_.3, bf16[2,512,512]{2,1,0:T(8,128)(2,1)} %refs_5_.3, ...), custom_call_target="tpu_custom_call" | custom-call | flops 6442450944 | bytes 7340032 | tf_op jit(solution)/shard_map/temporal_1_0/pallas_call | solution.py:234
  149.3 0.0 all-to-all-done.3
  149.4 7.0 %temporal_1_24.1 = bf16[64,32,512]{2,1,0:T(8,128)(2,1)} custom-call(s32[32]{0:T(128)S(1)} %copy-done.2, bf16[64,8,512]{2,1,0:T(8,128)(2,1)S(1)} %bitcast.10, bf16[64,512]{1,0:T(8,128)(2,1)S(1)} %copy-done, f32[2,2,512]{2,1,0:T(2,128)S(1)} %copy-done.1, bf16[2,512,512]{2,1,0:T(8,128)(2,1)} %refs_4_.3, ...), custom_call_target="tpu_custom_call", output_to_operand_aliasing={{}: (10, {})} | custom-call | flops 2147483648 | bytes 5242880 | tf_op jit(solution)/shard_map/temporal_1_24/pallas_call | solution.py:234
  156.4 32.2 %all_to_all.31 = bf16[16,4,32,512]{3,2,1,0:T(8,128)(2,1)S(1)} all-to-all(bf16[16,4,32,512]{3,2,1,0:T(8,128)(2,1)} %bitcast.19), channel_id=1, replica_groups=mesh['snap'=16,'clus'=8] {'snap'}, dimensions={0} | all-to-all | bytes 4194304 | tf_op jit(solution)/shard_map/all_to_all | solution.py:292
  188.6 1.6 copy.15
  (1 shorter events, 0.0 us)
Async XLA Ops:
  6.4 28.3 %all-to-all-start.1 = ((bf16[16,4,24,512]{3,2,1,0:T(8,128)(2,1)}), bf16[16,4,24,512]{3,2,1,0:T(8,128)(2,1)S(1)}, u32[]{:S(2)}, u32[]{:S(2)}) async-start(bf16[16,4,24,512]{3,2,1,0:T(8,128)(2,1)} %structure_0_0.1), calls=%async_computation.1 | async-start | bytes 3145728 | tf_op jit(solution)/shard_map/all_to_all | solution.py:292
  13.3 26.1 %copy-start = (bf16[64,512]{1,0:T(8,128)(2,1)S(1)}, bf16[64,512]{1,0:T(8,128)(2,1)}, u32[]{:S(2)}) copy-start(bf16[64,512]{1,0:T(8,128)(2,1)} %refs_2_.3) | copy-start | bytes 196612
  13.3 26.1 %copy-start.1 = (f32[2,2,512]{2,1,0:T(2,128)S(1)}, f32[2,2,512]{2,1,0:T(2,128)}, u32[]{:S(2)}) copy-start(f32[2,2,512]{2,1,0:T(2,128)} %refs_3_.3) | copy-start | bytes 24580
  13.3 26.0 %copy-start.2 = (s32[32]{0:T(128)S(1)}, s32[32]{0:T(128)}, u32[]{:S(2)}) copy-start(s32[32]{0:T(128)} %refs_0_.3) | copy-start | bytes 388
  34.6 21.5 %all-to-all-start = ((bf16[16,4,8,512]{3,2,1,0:T(8,128)(2,1)}), bf16[16,4,8,512]{3,2,1,0:T(8,128)(2,1)S(1)}, u32[]{:S(2)}, u32[]{:S(2)}) async-start(bf16[16,4,8,512]{3,2,1,0:T(8,128)(2,1)} %structure_0_24.1), calls=%async_computation | async-start | bytes 1048576 | tf_op jit(solution)/shard_map/all_to_all | solution.py:292
  101.7 26.2 %all-to-all-start.4 = ((bf16[16,4,24,512]{3,2,1,0:T(8,128)(2,1)}), bf16[16,4,24,512]{3,2,1,0:T(8,128)(2,1)S(1)}, u32[]{:S(2)}, u32[]{:S(2)}) async-start(bf16[16,4,24,512]{3,2,1,0:T(8,128)(2,1)} %structure_1_0.1), calls=%async_computation.4 | async-start | bytes 3145728 | tf_op jit(solution)/shard_map/all_to_all | solution.py:292
  127.9 21.4 %all-to-all-start.3 = ((bf16[16,4,8,512]{3,2,1,0:T(8,128)(2,1)}), bf16[16,4,8,512]{3,2,1,0:T(8,128)(2,1)S(1)}, u32[]{:S(2)}, u32[]{:S(2)}) async-start(bf16[16,4,8,512]{3,2,1,0:T(8,128)(2,1)} %structure_1_24.1), calls=%async_computation.3 | async-start | bytes 1048576 | tf_op jit(solution)/shard_map/all_to_all | solution.py:292

commit v3 on v2

v3 whole, which is shorter than its diff:
```python
import functools

import jax
import jax.numpy as jnp
from jax import lax
from jax.experimental import pallas as pl
from jax.experimental.pallas import tpu as pltpu
from jax.sharding import PartitionSpec as P

HEADS = 8
BLOCKS = 2
PARTS = 1
SPLIT = 1
OUTWARD = (16, 16)
HOMEWARD = (16, 16)
LANES = 128
VMEM_LIMIT = 32 * 1024 * 1024


def in_hbm(array):
    return pltpu.with_memory_space_constraint(array, pltpu.HBM)


def normalise(rows, gain):
    average = jnp.mean(rows, axis=-1, keepdims=True)
    centred = rows - average
    spread = jnp.mean(centred * centred, axis=-1, keepdims=True)
    return (centred * lax.rsqrt(spread + 1e-05) * gain).astype(jnp.bfloat16)


def bend(mapped):
    return jnp.where(mapped > 0, mapped, jnp.exp(jnp.minimum(mapped, 0.0)) - 1.0)


def structure_kernel(*refs, pieces, layer, start):
    hidden_hbm = refs[:pieces]
    links_hbm, weight_hbm, out_hbm, hidden_buf, links_buf, weight, out_buf, sems = refs[pieces:]
    snapshots, owners, rows, width = out_buf.shape
    nodes = links_buf.shape[-1]
    share = nodes // owners
    loads = []
    for s in range(snapshots):
        group = []
        below = 0
        for index, ref in enumerate(hidden_hbm):
            count = share if ref.ndim == 3 else ref.shape[2]
            if ref.ndim == 3:
                source, target = ref.at[s], hidden_buf.at[s]
            else:
                source, target = ref.at[:, s], hidden_buf.at[s, :, below : below + count]
            group.append(pltpu.make_async_copy(source, target, sems.at[s, index]))
            below += count
        group.append(
            pltpu.make_async_copy(
                links_hbm.at[s, :, start : start + rows], links_buf.at[s], sems.at[s, pieces]
            )
        )
        loads.append(group)
    fetch = pltpu.make_async_copy(weight_hbm.at[layer], weight, sems.at[snapshots, 0])
    for index, group in enumerate(loads):
        for load in group:
            load.start()
        if index == 0:
            fetch.start()
    stores = []
    for s in range(snapshots):
        for load in loads[s]:
            load.wait()
        if s == 0:
            fetch.wait()
        hidden = hidden_buf[s].reshape(nodes, width)
        per = owners // SPLIT
        for part in range(SPLIT):
            span = slice(part * per, (part + 1) * per)
            if hidden_buf.ndim == 3:
                own = hidden_buf[s, part * per * share : (part + 1) * per * share, :]
                own = own.reshape(per, share, width)[:, start : start + rows]
            else:
                own = hidden_buf[s, span, start : start + rows, :]
            own = own.reshape(per * rows, width).astype(jnp.float32)
            links = links_buf[s, span].reshape(per * rows, nodes).astype(jnp.float32)
            scale = 1.0 / (1.0 + jnp.sum(links, axis=1, keepdims=True))
            summed = jnp.dot(
                links.astype(jnp.bfloat16), hidden, preferred_element_type=jnp.float32
            )
            mixture = ((summed + own) * scale).astype(jnp.bfloat16)
            mapped = jnp.dot(mixture, weight[...], preferred_element_type=jnp.float32)
            out_buf[s, span] = (bend(mapped) + own).astype(jnp.bfloat16).reshape(per, rows, width)
        stores.append(
            pltpu.make_async_copy(out_buf.at[s], out_hbm.at[:, s], sems.at[snapshots, s + 1])
        )
        stores[-1].start()
    for store in stores:
        store.wait()


def structure(hidden, adjacency, w_struct, layer, start, rows, owners):
    hidden = hidden if isinstance(hidden, (list, tuple)) else [hidden]
    snapshots, nodes, _ = adjacency.shape
    width = w_struct.shape[-1]
    share = nodes // owners
    links = adjacency.reshape(snapshots, owners, share, nodes)
    near = [in_hbm(h) if h.ndim == 3 else h for h in hidden]
    flops = 2 * snapshots * owners * rows * width * (nodes + width)
    far = pl.BlockSpec(memory_space=pltpu.HBM)
    if hidden[0].ndim == 3:
        hidden_shape = (snapshots, nodes, width)
    else:
        hidden_shape = (snapshots, owners, share, width)
    return pl.pallas_call(
        functools.partial(structure_kernel, pieces=len(hidden), layer=layer, start=start),
        out_shape=pltpu.HBM((owners, snapshots, rows, width), jnp.bfloat16),
        in_specs=[pl.BlockSpec(memory_space=pl.ANY)] * len(hidden) + [far] * 2,
        out_specs=far,
        scratch_shapes=[
            pltpu.VMEM(hidden_shape, jnp.bfloat16),
            pltpu.VMEM((snapshots, owners, rows, nodes), adjacency.dtype),
            pltpu.VMEM((width, width), jnp.bfloat16),
            pltpu.VMEM((snapshots, owners, rows, width), jnp.bfloat16),
            pltpu.SemaphoreType.DMA((snapshots + 1, snapshots + 1)),
        ],
        compiler_params=pltpu.CompilerParams(vmem_limit_bytes=VMEM_LIMIT),
        cost_estimate=pl.CostEstimate(
            flops=flops, transcendentals=0, bytes_accessed=snapshots * nodes * nodes * 8
        ),
        name=f"structure_{layer}_{start}",
    )(*near, in_hbm(links), in_hbm(w_struct))


def temporal_kernel(
    first_ref,
    x_ref,
    pos_ref,
    gain_ref,
    wq_hbm,
    wk_hbm,
    wv_hbm,
    wo_hbm,
    wu_hbm,
    wd_hbm,
    out_ref,
    wq,
    wk,
    wv,
    wo,
    wu,
    wd,
    sems,
    mixed,
    rows_sum,
    normed,
    queries,
    key_rows,
    values,
    joined,
    order,
    scores,
    weights,
    inner,
    *,
    layer,
    offset,
    first_vertex,
):
    steps, group, width = out_ref.shape
    head_dim = width // HEADS
    pair = 2 * head_dim
    f32 = jnp.float32
    pairs = ((wq_hbm, wq), (wk_hbm, wk), (wv_hbm, wv), (wo_hbm, wo), (wu_hbm, wu), (wd_hbm, wd))
    fetches = [
        pltpu.make_async_copy(source.at[layer], target, sems.at[index])
        for index, (source, target) in enumerate(pairs)
    ]

    @pl.when(pl.program_id(0) == 0)
    def _():
        for fetch in fetches:
            fetch.start()

    row = lax.broadcasted_iota(jnp.int32, (steps, pair), 0)
    lane = lax.broadcasted_iota(jnp.int32, (steps, pair), 1)
    column = lane & (head_dim - 1)
    left = lane < head_dim
    order[...] = jnp.where(row < column, row, jnp.where(row == column, 1 << 20, -1))

    gain_one = gain_ref[layer, 0:1, :]
    gain_two = gain_ref[layer, 1:2, :]
    base = first_vertex + pl.program_id(0) * group
    zero = jnp.zeros((steps, pair), jnp.bfloat16)
    tiles = range(width // LANES)
    half = group // PARTS
    first_row = offset + pl.program_id(0) * group

    def enter(part):
        for tile in tiles:
            mixed[part, tile] = (
                x_ref[
                    :,
                    pl.ds(pl.multiple_of(first_row + part * half, half), half),
                    tile * LANES : (tile + 1) * LANES,
                ]
                .astype(f32)
                .reshape(steps * half, LANES)
            )
        pos = pos_ref[...].astype(f32)
        for v in range(half):
            span = slice(v * steps, (v + 1) * steps)
            parts = [mixed[part, tile, pl.ds(v, steps, stride=half), :] for tile in tiles]
            total = jnp.concatenate(parts, axis=1) + pos
            rows_sum[part, span, :] = total
            normed[part, span, :] = normalise(total, gain_one)

    def project(part):
        rows = normed[part]
        queries[part] = (
            jnp.dot(rows, wq[...], preferred_element_type=f32) * head_dim ** (-0.5)
        ).astype(jnp.bfloat16)
        key_rows[part] = jnp.dot(rows, wk[...], preferred_element_type=f32).astype(jnp.bfloat16)
        values[part] = jnp.dot(rows, wv[...], preferred_element_type=f32).astype(jnp.bfloat16)

    def score(part):
        for v in range(half):
            span = slice(v * steps, (v + 1) * steps)
            for p in range(width // pair):
                lanes = slice(p * pair, (p + 1) * pair)
                q = queries[part, span, lanes]
                stacked = jnp.concatenate(
                    [jnp.where(left, q, zero), jnp.where(left, zero, q)], axis=0
                )
                scores[part, span, lanes] = lax.dot_general(
                    key_rows[part, span, lanes],
                    stacked,
                    (((1,), (1,)), ((), ())),
                    preferred_element_type=f32,
                )

    def soften(part):
        for v in range(half):
            allowed = order[...] >= first_ref[base + part * half + v]
            span = slice(v * steps, (v + 1) * steps)
            for p in range(width // pair):
                lanes = slice(p * pair, (p + 1) * pair)
                seen = jnp.where(allowed, scores[part, span, lanes], -1e30)
                raised = jnp.exp(seen - jnp.max(seen, axis=0, keepdims=True))
                share = 1.0 / jnp.sum(raised, axis=0, keepdims=True)
                weights[part, span, lanes] = (raised * share).astype(jnp.bfloat16)

    def gather(part):
        for v in range(half):
            span = slice(v * steps, (v + 1) * steps)
            for p in range(width // pair):
                lanes = slice(p * pair, (p + 1) * pair)
                both = lax.dot_general(
                    weights[part, span, lanes],
                    values[part, span, lanes],
                    (((0,), (0,)), ((), ())),
                    preferred_element_type=f32,
                )
                joined[part, span, lanes] = jnp.where(left, both[:steps], both[steps:]).astype(
                    jnp.bfloat16
                )

    def attend(part):
        attended = rows_sum[part] + jnp.dot(joined[part], wo[...], preferred_element_type=f32)
        rows_sum[part] = attended

    def second_norm(part):
        normed[part] = normalise(rows_sum[part], gain_two)

    def widen(part):
        inner[part] = jax.nn.gelu(
            jnp.dot(normed[part], wu[...], preferred_element_type=f32)
        ).astype(jnp.bfloat16)

    def finish(part):
        finished = rows_sum[part] + jnp.dot(inner[part], wd[...], preferred_element_type=f32)
        for tile in tiles:
            lanes = slice(tile * LANES, (tile + 1) * LANES)
            for v in range(half):
                mixed[part, tile, pl.ds(v, steps, stride=half), :] = finished[
                    v * steps : (v + 1) * steps, lanes
                ]
            out_ref[:, part * half : (part + 1) * half, lanes] = (
                mixed[part, tile].reshape(steps, half, LANES).astype(jnp.bfloat16)
            )

    def wait_for(some):
        @pl.when(pl.program_id(0) == 0)
        def _():
            for fetch in some:
                fetch.wait()

    def run(*stages):
        for stage in stages:
            for part in range(PARTS):
                stage(part)

    run(enter)
    wait_for(fetches[:3])
    run(project, score, soften, gather)
    wait_for(fetches[3:])
    run(attend, second_norm, widen, finish)


def temporal(rows, first_seen, pos_embed, weights, norm_gain, layer, offset, start, count):
    steps, _, width = rows.shape
    group = 8 * PARTS
    inner = weights[4].shape[-1]
    size = 8 * steps
    flops = 2 * steps * count * width * (4 * width + 2 * inner)
    near = pl.BlockSpec(memory_space=pltpu.VMEM)
    bf16 = jnp.bfloat16
    return pl.pallas_call(
        functools.partial(temporal_kernel, layer=layer, offset=offset, first_vertex=start),
        grid=(count // group,),
        out_shape=pltpu.HBM((steps, count, width), bf16),
        in_specs=[pl.BlockSpec(memory_space=pltpu.SMEM)]
        + [near] * 3
        + [pl.BlockSpec(memory_space=pltpu.HBM)] * len(weights),
        out_specs=pl.BlockSpec((steps, group, width), lambda i: (0, i, 0)),
        scratch_shapes=[pltpu.VMEM(w.shape[1:], bf16) for w in weights]
        + [
            pltpu.SemaphoreType.DMA((len(weights),)),
            pltpu.VMEM((PARTS, width // LANES, size, LANES), jnp.float32),
            pltpu.VMEM((PARTS, size, width), jnp.float32),
            pltpu.VMEM((PARTS, size, width), bf16),
            pltpu.VMEM((PARTS, size, width), bf16),
            pltpu.VMEM((PARTS, size, width), bf16),
            pltpu.VMEM((PARTS, size, width), bf16),
            pltpu.VMEM((PARTS, size, width), bf16),
            pltpu.VMEM((steps, 2 * width // HEADS), jnp.int32),
            pltpu.VMEM((PARTS, size, width), jnp.float32),
            pltpu.VMEM((PARTS, size, width), bf16),
            pltpu.VMEM((PARTS, size, inner), bf16),
        ],
        compiler_params=pltpu.CompilerParams(vmem_limit_bytes=VMEM_LIMIT),
        cost_estimate=pl.CostEstimate(
            flops=flops, transcendentals=0, bytes_accessed=2 * steps * count * width
        ),
        name=f"temporal_{layer}_{start}",
    )(first_seen, rows, pos_embed, norm_gain, *[in_hbm(w) for w in weights])


def deliver_kernel(piece_ref, *refs, start):
    out_hbm, sems = refs[-2:]
    owners, snapshots, rows, _ = piece_ref.shape
    stores = [
        pltpu.make_async_copy(
            piece_ref.at[:, s], out_hbm.at[s, :, start : start + rows], sems.at[s]
        )
        for s in range(snapshots)
    ]
    for store in stores:
        store.start()
    for store in stores:
        store.wait()


def deliver(piece, target, start, share):
    owners, snapshots, _, width = piece.shape
    far = pl.BlockSpec(memory_space=pltpu.HBM)
    operands = [piece] if target is None else [piece, target]
    return pl.pallas_call(
        functools.partial(deliver_kernel, start=start),
        out_shape=pltpu.HBM((snapshots, owners, share, width), piece.dtype),
        in_specs=[pl.BlockSpec(memory_space=pltpu.VMEM)] + [far] * (len(operands) - 1),
        out_specs=far,
        scratch_shapes=[pltpu.SemaphoreType.DMA((snapshots,))],
        input_output_aliases={} if target is None else {1: 0},
        compiler_params=pltpu.CompilerParams(vmem_limit_bytes=VMEM_LIMIT),
        cost_estimate=pl.CostEstimate(
            flops=0, transcendentals=0, bytes_accessed=2 * piece.size * 2
        ),
        name=f"deliver_{start}",
    )(*operands)


def on_device(
    features,
    adjacency,
    first_seen,
    pos_embed,
    w_struct,
    w_query,
    w_key,
    w_value,
    w_out,
    w_up,
    w_down,
    norm_gain,
    *,
    owners,
):
    snapshots, nodes, width = features.shape

    def exchange(array):
        return lax.all_to_all(array, "snap", split_axis=0, concat_axis=0, tiled=True)

    weights = (w_query, w_key, w_value, w_out, w_up, w_down)
    hidden = [features]
    for layer in range(BLOCKS):
        arrived = []
        start = 0
        for rows in OUTWARD:
            piece = structure(hidden, adjacency, w_struct, layer, start, rows, owners)
            piece = exchange(piece)
            arrived.append((start, piece.reshape(owners * snapshots, rows, width)))
            start += rows
        hidden = []
        start = 0
        for rows in HOMEWARD:
            at, piece = [item for item in arrived if item[0] <= start][-1]
            finished = temporal(
                piece, first_seen, pos_embed, weights, norm_gain, layer, start - at, start, rows
            )
            hidden.append(exchange(finished.reshape(owners, snapshots, rows, width)))
            start += rows
    result = None
    start = 0
    for piece in hidden:
        result = deliver(piece, result, start, nodes // owners)
        start += piece.shape[2]
    return result.reshape(snapshots, nodes, width)


def solution(mesh):
    in_specs = (
        P("snap", "clus", None),
        P("snap", "clus", None),
        P(("clus", "snap")),
        P(),
        P(),
        P(),
        P(),
        P(),
        P(),
        P(),
        P(),
        P(),
    )
    out_specs = P("snap", "clus", None)
    return jax.shard_map(
        functools.partial(on_device, owners=mesh.shape["snap"]),
        mesh=mesh,
        in_specs=in_specs,
        out_specs=out_specs,
        check_vma=False,
    )
```

time: 191 us -> 175 us (0.916)
  blocking collectives: 64.6 us -> 19.9 us
  waiting for transfers between devices: 32 us -> 52 us
  starting transfers between devices: 21 us -> 33.6 us
  Pallas kernels: 70.9 us -> 68.3 us
    all_to_all x2 -> x1, blocking collectives: 64.6 us -> 19.9 us  [exchange(): lax.all_to_all(array, 'snap', split_axis=0, concat_axis=0, tiled=True)]
    all_to_all x4 -> x7, waiting for transfers between devices: 32 us -> 52 us  [exchange(): lax.all_to_all(array, 'snap', split_axis=0, concat_axis=0, tiled=True)]
    all_to_all x4 -> x7, starting transfers between devices: 21 us -> 33.6 us  [exchange(): lax.all_to_all(array, 'snap', split_axis=0, concat_axis=0, tiled=True)]
    pallas_call x8 -> x10, Pallas kernels: 70.9 us -> 68.3 us  [the longest x4 48 us: temporal(): pl.pallas_call(functools.partial(temporal_kernel, layer=layer, offset=off...]
  transfers between devices with their start and end apart: 4 -> 7, of which waited for: 2 -> 7; matrix products, arithmetic and copies ran while one was open for 0% -> 0% of each run, Pallas kernels for 23% -> 33%
where the time goes in v3:
time: 175 us; the launch traced here: 174 us
  Pallas kernels  68.3 us (39%)
  waiting for transfers between devices  52 us (30%)
  starting transfers between devices  33.6 us (19%)
  blocking collectives  19.9 us (11%)
    all_to_all x7, waiting for transfers between devices, exchange(): lax.all_to_all(array, 'snap', split_axis=0, concat_axis=0, tiled=True)  52 us
    pallas_call x4, Pallas kernels, temporal(): pl.pallas_call(functools.partial(temporal_kernel, layer=layer, offset=off...  48 us
    all_to_all x7, starting transfers between devices, exchange(): lax.all_to_all(array, 'snap', split_axis=0, concat_axis=0, tiled=True)  33.6 us
    all_to_all x1, blocking collectives, exchange(): lax.all_to_all(array, 'snap', split_axis=0, concat_axis=0, tiled=True)  19.9 us
    pallas_call x4, Pallas kernels, structure(): pl.pallas_call(functools.partial(structure_kernel, pieces=len(hidden), la...  18.3 us
  transfers between devices with their start and end apart: 7, of which 7 were waited for; matrix products, arithmetic and copies ran while one was open for 0% of the time, Pallas kernels for 33%

profile of v3, /device:TPU:1, one launch (start us, length us, event | category | flops | bytes accessed | tf_op | source)
XLA Modules:
  0.0 174.2 jit_solution(308026910410071755)
XLA Ops:
  0.0 4.6 %structure_0_16.1 = bf16[16,4,16,512]{3,2,1,0:T(8,128)(2,1)} custom-call(bf16[4,512,512]{2,1,0:T(8,128)(2,1)} %refs_0_.3, s32[4,16,32,512]{3,2,1,0:T(8,128)} %bitcast.14, bf16[2,512,512]{2,1,0:T(8,128)(2,1)} %refs_3_.3), custom_call_target="tpu_custom_call" | custom-call | flops 1073741824 | bytes 8388608 | tf_op jit(solution)/shard_map/structure_0_16/pallas_call | solution.py:110
  4.7 6.9 %all-to-all-start.2 = ((bf16[16,4,16,512]{3,2,1,0:T(8,128)(2,1)}), bf16[16,4,16,512]{3,2,1,0:T(8,128)(2,1)S(1)}, u32[]{:S(2)}, u32[]{:S(2)}) async-start(bf16[16,4,16,512]{3,2,1,0:T(8,128)(2,1)} %structure_0_16.1), calls=%async_computation.2 | async-start | bytes 2097152 | tf_op jit(solution)/shard_map/all_to_all | solution.py:397
  11.5 4.7 %structure_0_0.1 = bf16[16,4,16,512]{3,2,1,0:T(8,128)(2,1)} custom-call(bf16[4,512,512]{2,1,0:T(8,128)(2,1)} %refs_0_.3, s32[4,16,32,512]{3,2,1,0:T(8,128)} %bitcast.15, bf16[2,512,512]{2,1,0:T(8,128)(2,1)} %refs_3_.3), custom_call_target="tpu_custom_call" | custom-call | flops 1073741824 | bytes 8388608 | tf_op jit(solution)/shard_map/structure_0_0/pallas_call | solution.py:110
  16.2 11.0 %all-to-all-done.2 = bf16[16,4,16,512]{3,2,1,0:T(8,128)(2,1)S(1)} async-done(((bf16[16,4,16,512]{3,2,1,0:T(8,128)(2,1)}), bf16[16,4,16,512]{3,2,1,0:T(8,128)(2,1)S(1)}, u32[]{:S(2)}, u32[]{:S(2)}) %all-to-all-start.2) | async-done | bytes 1048608 | tf_op jit(solution)/shard_map/all_to_all | solution.py:397
  27.2 4.4 %all-to-all-start = ((bf16[16,4,16,512]{3,2,1,0:T(8,128)(2,1)}), bf16[16,4,16,512]{3,2,1,0:T(8,128)(2,1)S(1)}, u32[]{:S(2)}, u32[]{:S(2)}) async-start(bf16[16,4,16,512]{3,2,1,0:T(8,128)(2,1)} %structure_0_0.1), calls=%async_computation | async-start | bytes 2097152 | tf_op jit(solution)/shard_map/all_to_all | solution.py:397
  31.6 12.0 %temporal_0_16.1 = bf16[64,16,512]{2,1,0:T(8,128)(2,1)} custom-call(s32[32]{0:T(128)S(1)} %copy-done.2, bf16[64,16,512]{2,1,0:T(8,128)(2,1)S(1)} %bitcast.13, bf16[64,512]{1,0:T(8,128)(2,1)S(1)} %copy-done, f32[2,2,512]{2,1,0:T(2,128)S(1)} %copy-done.1, bf16[2,512,512]{2,1,0:T(8,128)(2,1)} %wq_hbm.7, bf16[2,512,512]{2,1,0:T(8,128)(2,1)} %wk_hbm.7, ...), custom_call_target="tpu_custom_call" | custom-call | flops 4294967296 | bytes 1048576 | tf_op jit(solution)/shard_map/temporal_0_16/pallas_call | solution.py:313
  43.7 3.7 %all-to-all-done = bf16[16,4,16,512]{3,2,1,0:T(8,128)(2,1)S(1)} async-done(((bf16[16,4,16,512]{3,2,1,0:T(8,128)(2,1)}), bf16[16,4,16,512]{3,2,1,0:T(8,128)(2,1)S(1)}, u32[]{:S(2)}, u32[]{:S(2)}) %all-to-all-start) | async-done | bytes 1048608 | tf_op jit(solution)/shard_map/all_to_all | solution.py:397
  47.4 4.4 %all-to-all-start.3 = ((bf16[16,4,16,512]{3,2,1,0:T(8,128)(2,1)}), bf16[16,4,16,512]{3,2,1,0:T(8,128)(2,1)S(1)}, u32[]{:S(2)}, u32[]{:S(2)}) async-start(bf16[16,4,16,512]{3,2,1,0:T(8,128)(2,1)} %bitcast.18), calls=%async_computation.3 | async-start | bytes 2097152 | tf_op jit(solution)/shard_map/all_to_all | solution.py:397
  51.8 11.9 %temporal_0_0.1 = bf16[64,16,512]{2,1,0:T(8,128)(2,1)} custom-call(s32[32]{0:T(128)S(1)} %copy-done.2, bf16[64,16,512]{2,1,0:T(8,128)(2,1)S(1)} %bitcast.11, bf16[64,512]{1,0:T(8,128)(2,1)S(1)} %copy-done, f32[2,2,512]{2,1,0:T(2,128)S(1)} %copy-done.1, bf16[2,512,512]{2,1,0:T(8,128)(2,1)} %wq_hbm.7, bf16[2,512,512]{2,1,0:T(8,128)(2,1)} %wk_hbm.7, ...), custom_call_target="tpu_custom_call" | custom-call | flops 4294967296 | bytes 1048576 | tf_op jit(solution)/shard_map/temporal_0_0/pallas_call | solution.py:313
  63.7 3.8 %all-to-all-done.3.refs_1_ = bf16[16,4,16,512]{3,2,1,0:T(8,128)(2,1)S(1)} async-done(((bf16[16,4,16,512]{3,2,1,0:T(8,128)(2,1)}), bf16[16,4,16,512]{3,2,1,0:T(8,128)(2,1)S(1)}, u32[]{:S(2)}, u32[]{:S(2)}) %all-to-all-start.3) | async-done | bytes 1048608 | tf_op jit(solution)/shard_map/all_to_all | solution.py:397
  67.5 19.9 %all_to_all.40.refs_0_ = bf16[16,4,16,512]{3,2,1,0:T(8,128)(2,1)S(1)} all-to-all(bf16[16,4,16,512]{3,2,1,0:T(8,128)(2,1)} %bitcast.21), channel_id=1, replica_groups=mesh['snap'=16,'clus'=8] {'snap'}, dimensions={0} | all-to-all | bytes 2097152 | tf_op jit(solution)/shard_map/all_to_all | solution.py:397
  87.5 4.6 %structure_1_0.1 = bf16[16,4,16,512]{3,2,1,0:T(8,128)(2,1)} custom-call(bf16[16,4,16,512]{3,2,1,0:T(8,128)(2,1)S(1)} %all_to_all.40.refs_0_, bf16[16,4,16,512]{3,2,1,0:T(8,128)(2,1)S(1)} %all-to-all-done.3.refs_1_, s32[4,16,32,512]{3,2,1,0:T(8,128)} %bitcast.16, bf16[2,512,512]{2,1,0:T(8,128)(2,1)} %refs_3_.3), custom_call_target="tpu_custom_call" | custom-call | flops 1073741824 | bytes 8388608 | tf_op jit(solution)/shard_map/structure_1_0/pallas_call | solution.py:110
  92.0 4.7 %all-to-all-start.6 = ((bf16[16,4,16,512]{3,2,1,0:T(8,128)(2,1)}), bf16[16,4,16,512]{3,2,1,0:T(8,128)(2,1)S(1)}, u32[]{:S(2)}, u32[]{:S(2)}) async-start(bf16[16,4,16,512]{3,2,1,0:T(8,128)(2,1)} %structure_1_0.1), calls=%async_computation.6 | async-start | bytes 2097152 | tf_op jit(solution)/shard_map/all_to_all | solution.py:397
  96.8 4.5 %structure_1_16.1 = bf16[16,4,16,512]{3,2,1,0:T(8,128)(2,1)} custom-call(bf16[16,4,16,512]{3,2,1,0:T(8,128)(2,1)S(1)} %all_to_all.40.refs_0_, bf16[16,4,16,512]{3,2,1,0:T(8,128)(2,1)S(1)} %all-to-all-done.3.refs_1_, s32[4,16,32,512]{3,2,1,0:T(8,128)} %bitcast.17, bf16[2,512,512]{2,1,0:T(8,128)(2,1)} %refs_3_.3), custom_call_target="tpu_custom_call" | custom-call | flops 1073741824 | bytes 8388608 | tf_op jit(solution)/shard_map/structure_1_16/pallas_call | solution.py:110
  101.3 11.3 %all-to-all-done.6 = bf16[16,4,16,512]{3,2,1,0:T(8,128)(2,1)S(1)} async-done(((bf16[16,4,16,512]{3,2,1,0:T(8,128)(2,1)}), bf16[16,4,16,512]{3,2,1,0:T(8,128)(2,1)S(1)}, u32[]{:S(2)}, u32[]{:S(2)}) %all-to-all-start.6) | async-done | bytes 1048608 | tf_op jit(solution)/shard_map/all_to_all | solution.py:397
  112.5 4.4 %all-to-all-start.4 = ((bf16[16,4,16,512]{3,2,1,0:T(8,128)(2,1)}), bf16[16,4,16,512]{3,2,1,0:T(8,128)(2,1)S(1)}, u32[]{:S(2)}, u32[]{:S(2)}) async-start(bf16[16,4,16,512]{3,2,1,0:T(8,128)(2,1)} %structure_1_16.1), calls=%async_computation.4 | async-start | bytes 2097152 | tf_op jit(solution)/shard_map/all_to_all | solution.py:397
  116.9 12.0 %temporal_1_0.1 = bf16[64,16,512]{2,1,0:T(8,128)(2,1)} custom-call(s32[32]{0:T(128)S(1)} %copy-done.2, bf16[64,16,512]{2,1,0:T(8,128)(2,1)S(1)} %bitcast.10, bf16[64,512]{1,0:T(8,128)(2,1)S(1)} %copy-done, f32[2,2,512]{2,1,0:T(2,128)S(1)} %copy-done.1, bf16[2,512,512]{2,1,0:T(8,128)(2,1)} %wq_hbm.7, bf16[2,512,512]{2,1,0:T(8,128)(2,1)} %wk_hbm.7, ...), custom_call_target="tpu_custom_call" | custom-call | flops 4294967296 | bytes 1048576 | tf_op jit(solution)/shard_map/temporal_1_0/pallas_call | solution.py:313
  129.0 3.7 %all-to-all-done.4 = bf16[16,4,16,512]{3,2,1,0:T(8,128)(2,1)S(1)} async-done(((bf16[16,4,16,512]{3,2,1,0:T(8,128)(2,1)}), bf16[16,4,16,512]{3,2,1,0:T(8,128)(2,1)S(1)}, u32[]{:S(2)}, u32[]{:S(2)}) %all-to-all-start.4) | async-done | bytes 1048608 | tf_op jit(solution)/shard_map/all_to_all | solution.py:397
  132.7 4.4 %all-to-all-start.7 = ((bf16[16,4,16,512]{3,2,1,0:T(8,128)(2,1)}), bf16[16,4,16,512]{3,2,1,0:T(8,128)(2,1)S(1)}, u32[]{:S(2)}, u32[]{:S(2)}) async-start(bf16[16,4,16,512]{3,2,1,0:T(8,128)(2,1)} %bitcast.19), calls=%async_computation.7 | async-start | bytes 2097152 | tf_op jit(solution)/shard_map/all_to_all | solution.py:397
  137.1 12.0 %temporal_1_16.1 = bf16[64,16,512]{2,1,0:T(8,128)(2,1)} custom-call(s32[32]{0:T(128)S(1)} %copy-done.2, bf16[64,16,512]{2,1,0:T(8,128)(2,1)S(1)} %bitcast.12, bf16[64,512]{1,0:T(8,128)(2,1)S(1)} %copy-done, f32[2,2,512]{2,1,0:T(2,128)S(1)} %copy-done.1, bf16[2,512,512]{2,1,0:T(8,128)(2,1)} %wq_hbm.7, bf16[2,512,512]{2,1,0:T(8,128)(2,1)} %wk_hbm.7, ...), custom_call_target="tpu_custom_call" | custom-call | flops 4294967296 | bytes 1048576 | tf_op jit(solution)/shard_map/temporal_1_16/pallas_call | solution.py:313
  149.1 3.7 %all-to-all-done.7.piece_ref = bf16[16,4,16,512]{3,2,1,0:T(8,128)(2,1)S(1)} async-done(((bf16[16,4,16,512]{3,2,1,0:T(8,128)(2,1)}), bf16[16,4,16,512]{3,2,1,0:T(8,128)(2,1)S(1)}, u32[]{:S(2)}, u32[]{:S(2)}) %all-to-all-start.7) | async-done | bytes 1048608 | tf_op jit(solution)/shard_map/all_to_all | solution.py:397
  152.9 4.4 %all-to-all-start.5 = ((bf16[16,4,16,512]{3,2,1,0:T(8,128)(2,1)}), bf16[16,4,16,512]{3,2,1,0:T(8,128)(2,1)S(1)}, u32[]{:S(2)}, u32[]{:S(2)}) async-start(bf16[16,4,16,512]{3,2,1,0:T(8,128)(2,1)} %bitcast.20), calls=%async_computation.5 | async-start | bytes 2097152 | tf_op jit(solution)/shard_map/all_to_all | solution.py:397
  158.3 14.8 %all-to-all-done.5.piece_ref = bf16[16,4,16,512]{3,2,1,0:T(8,128)(2,1)S(1)} async-done(((bf16[16,4,16,512]{3,2,1,0:T(8,128)(2,1)}), bf16[16,4,16,512]{3,2,1,0:T(8,128)(2,1)S(1)}, u32[]{:S(2)}, u32[]{:S(2)}) %all-to-all-start.5) | async-done | bytes 1048608 | tf_op jit(solution)/shard_map/all_to_all | solution.py:397
  173.0 1.0 deliver_16.1
  (7 shorter events, 1.0 us)
Async XLA Ops:
  4.7 22.5 %all-to-all-start.2 = ((bf16[16,4,16,512]{3,2,1,0:T(8,128)(2,1)}), bf16[16,4,16,512]{3,2,1,0:T(8,128)(2,1)S(1)}, u32[]{:S(2)}, u32[]{:S(2)}) async-start(bf16[16,4,16,512]{3,2,1,0:T(8,128)(2,1)} %structure_0_16.1), calls=%async_computation.2 | async-start | bytes 2097152 | tf_op jit(solution)/shard_map/all_to_all | solution.py:397
  16.2 15.4 %copy-start = (bf16[64,512]{1,0:T(8,128)(2,1)S(1)}, bf16[64,512]{1,0:T(8,128)(2,1)}, u32[]{:S(2)}) copy-start(bf16[64,512]{1,0:T(8,128)(2,1)} %pos_ref.7) | copy-start | bytes 196612
  16.2 15.4 %copy-start.1 = (f32[2,2,512]{2,1,0:T(2,128)S(1)}, f32[2,2,512]{2,1,0:T(2,128)}, u32[]{:S(2)}) copy-start(f32[2,2,512]{2,1,0:T(2,128)} %gain_ref.7) | copy-start | bytes 24580
  16.2 15.4 %copy-start.2 = (s32[32]{0:T(128)S(1)}, s32[32]{0:T(128)}, u32[]{:S(2)}) copy-start(s32[32]{0:T(128)} %first_ref.7) | copy-start | bytes 388
  27.2 20.2 %all-to-all-start = ((bf16[16,4,16,512]{3,2,1,0:T(8,128)(2,1)}), bf16[16,4,16,512]{3,2,1,0:T(8,128)(2,1)S(1)}, u32[]{:S(2)}, u32[]{:S(2)}) async-start(bf16[16,4,16,512]{3,2,1,0:T(8,128)(2,1)} %structure_0_0.1), calls=%async_computation | async-start | bytes 2097152 | tf_op jit(solution)/shard_map/all_to_all | solution.py:397
  47.4 20.2 %all-to-all-start.3 = ((bf16[16,4,16,512]{3,2,1,0:T(8,128)(2,1)}), bf16[16,4,16,512]{3,2,1,0:T(8,128)(2,1)S(1)}, u32[]{:S(2)}, u32[]{:S(2)}) async-start(bf16[16,4,16,512]{3,2,1,0:T(8,128)(2,1)} %bitcast.18), calls=%async_computation.3 | async-start | bytes 2097152 | tf_op jit(solution)/shard_map/all_to_all | solution.py:397
  92.0 20.5 %all-to-all-start.6 = ((bf16[16,4,16,512]{3,2,1,0:T(8,128)(2,1)}), bf16[16,4,16,512]{3,2,1,0:T(8,128)(2,1)S(1)}, u32[]{:S(2)}, u32[]{:S(2)}) async-start(bf16[16,4,16,512]{3,2,1,0:T(8,128)(2,1)} %structure_1_0.1), calls=%async_computation.6 | async-start | bytes 2097152 | tf_op jit(solution)/shard_map/all_to_all | solution.py:397
  112.5 20.2 %all-to-all-start.4 = ((bf16[16,4,16,512]{3,2,1,0:T(8,128)(2,1)}), bf16[16,4,16,512]{3,2,1,0:T(8,128)(2,1)S(1)}, u32[]{:S(2)}, u32[]{:S(2)}) async-start(bf16[16,4,16,512]{3,2,1,0:T(8,128)(2,1)} %structure_1_16.1), calls=%async_computation.4 | async-start | bytes 2097152 | tf_op jit(solution)/shard_map/all_to_all | solution.py:397
  132.7 20.2 %all-to-all-start.7 = ((bf16[16,4,16,512]{3,2,1,0:T(8,128)(2,1)}), bf16[16,4,16,512]{3,2,1,0:T(8,128)(2,1)S(1)}, u32[]{:S(2)}, u32[]{:S(2)}) async-start(bf16[16,4,16,512]{3,2,1,0:T(8,128)(2,1)} %bitcast.19), calls=%async_computation.7 | async-start | bytes 2097152 | tf_op jit(solution)/shard_map/all_to_all | solution.py:397
  152.9 20.2 %all-to-all-start.5 = ((bf16[16,4,16,512]{3,2,1,0:T(8,128)(2,1)}), bf16[16,4,16,512]{3,2,1,0:T(8,128)(2,1)S(1)}, u32[]{:S(2)}, u32[]{:S(2)}) async-start(bf16[16,4,16,512]{3,2,1,0:T(8,128)(2,1)} %bitcast.20), calls=%async_computation.5 | async-start | bytes 2097152 | tf_op jit(solution)/shard_map/all_to_all | solution.py:397

commit v4 on v3

--- a/solution.py
+++ b/solution.py
@@ -10,7 +10,6 @@
 HEADS = 8
 BLOCKS = 2
 PARTS = 1
-SPLIT = 1
 OUTWARD = (16, 16)
 HOMEWARD = (16, 16)
 LANES = 128
@@ -34,7 +33,8 @@
 
 def structure_kernel(*refs, pieces, layer, start):
     hidden_hbm = refs[:pieces]
-    links_hbm, weight_hbm, out_hbm, hidden_buf, links_buf, weight, out_buf, sems = refs[pieces:]
+    links_hbm, weight_hbm, out_hbm, hidden_buf, links_buf, weight, out_buf, *rest = refs[pieces:]
+    scales, narrow, mixture, sems = rest
     snapshots, owners, rows, width = out_buf.shape
     nodes = links_buf.shape[-1]
     share = nodes // owners
@@ -63,33 +63,45 @@
         if index == 0:
             fetch.start()
     stores = []
-    for s in range(snapshots):
+
+    def own_rows(s):
+        if hidden_buf.ndim == 3:
+            own = hidden_buf[s].reshape(owners, share, width)[:, start : start + rows]
+        else:
+            own = hidden_buf[s, :, start : start + rows, :]
+        return own.reshape(owners * rows, width).astype(jnp.float32)
+
+    def ready(s):
         for load in loads[s]:
             load.wait()
         if s == 0:
             fetch.wait()
-        hidden = hidden_buf[s].reshape(nodes, width)
-        per = owners // SPLIT
-        for part in range(SPLIT):
-            span = slice(part * per, (part + 1) * per)
-            if hidden_buf.ndim == 3:
-                own = hidden_buf[s, part * per * share : (part + 1) * per * share, :]
-                own = own.reshape(per, share, width)[:, start : start + rows]
-            else:
-                own = hidden_buf[s, span, start : start + rows, :]
-            own = own.reshape(per * rows, width).astype(jnp.float32)
-            links = links_buf[s, span].reshape(per * rows, nodes).astype(jnp.float32)
-            scale = 1.0 / (1.0 + jnp.sum(links, axis=1, keepdims=True))
-            summed = jnp.dot(
-                links.astype(jnp.bfloat16), hidden, preferred_element_type=jnp.float32
-            )
-            mixture = ((summed + own) * scale).astype(jnp.bfloat16)
-            mapped = jnp.dot(mixture, weight[...], preferred_element_type=jnp.float32)
-            out_buf[s, span] = (bend(mapped) + own).astype(jnp.bfloat16).reshape(per, rows, width)
+        links = links_buf[s].reshape(owners * rows, nodes).astype(jnp.float32)
+        scale = 1.0 / (1.0 + jnp.sum(links, axis=1, keepdims=True))
+        scales[s] = jnp.broadcast_to(scale, (owners * rows, LANES))
+        narrow[s] = links.astype(jnp.bfloat16)
+
+    def mix(s):
+        summed = jnp.dot(
+            narrow[s], hidden_buf[s].reshape(nodes, width), preferred_element_type=jnp.float32
+        )
+        scale = jnp.concatenate([scales[s]] * (width // LANES), axis=1)
+        mixture[s] = ((summed + own_rows(s)) * scale).astype(jnp.bfloat16)
+
+    def settle(s):
+        mapped = jnp.dot(mixture[s], weight[...], preferred_element_type=jnp.float32)
+        rounded = (bend(mapped) + own_rows(s)).astype(jnp.bfloat16)
+        out_buf[s] = rounded.reshape(owners, rows, width)
         stores.append(
             pltpu.make_async_copy(out_buf.at[s], out_hbm.at[:, s], sems.at[snapshots, s + 1])
         )
         stores[-1].start()
+
+    stages = (ready, mix, settle)
+    for tick in range(snapshots + len(stages) - 1):
+        for lag, step in enumerate(stages):
+            if 0 <= tick - lag < snapshots:
+                step(tick - lag)
     for store in stores:
         store.wait()
 
@@ -117,6 +129,9 @@
             pltpu.VMEM((snapshots, owners, rows, nodes), adjacency.dtype),
             pltpu.VMEM((width, width), jnp.bfloat16),
             pltpu.VMEM((snapshots, owners, rows, width), jnp.bfloat16),
+            pltpu.VMEM((snapshots, owners * rows, LANES), jnp.float32),
+            pltpu.VMEM((snapshots, owners * rows, nodes), jnp.bfloat16),
+            pltpu.VMEM((snapshots, owners * rows, width), jnp.bfloat16),
             pltpu.SemaphoreType.DMA((snapshots + 1, snapshots + 1)),
         ],
         compiler_params=pltpu.CompilerParams(vmem_limit_bytes=VMEM_LIMIT),
@@ -125,6 +140,140 @@
         ),
         name=f"structure_{layer}_{start}",
     )(*near, in_hbm(links), in_hbm(w_struct))
+
+
+def stage_kernel(links_hbm, after_hbm, narrow_hbm, scale_ref, whole, narrow, sems):
+    del after_hbm
+    snapshots, nodes, _ = whole.shape
+    loads = [
+        pltpu.make_async_copy(links_hbm.at[s], whole.at[s], sems.at[0, s]) for s in range(snapshots)
+    ]
+    stores = [
+        pltpu.make_async_copy(narrow.at[s], narrow_hbm.at[s], sems.at[1, s])
+        for s in range(snapshots)
+    ]
+    for load in loads:
+        load.start()
+    for s in range(snapshots):
+        loads[s].wait()
+        links = whole[s].astype(jnp.float32)
+        scale = 1.0 / (1.0 + jnp.sum(links, axis=1, keepdims=True))
+        scale_ref[s] = jnp.broadcast_to(scale, (nodes, LANES))
+        narrow[s] = links.astype(jnp.bfloat16)
+        stores[s].start()
+    for store in stores:
+        store.wait()
+
+
+def stage(adjacency, after):
+    snapshots, nodes, _ = adjacency.shape
+    far = pl.BlockSpec(memory_space=pltpu.HBM)
+    return pl.pallas_call(
+        stage_kernel,
+        out_shape=[
+            pltpu.HBM(adjacency.shape, jnp.bfloat16),
+            pltpu.VMEM((snapshots, nodes, LANES), jnp.float32),
+        ],
+        in_specs=[far] * 2,
+        out_specs=[far, pl.BlockSpec(memory_space=pltpu.VMEM)],
+        scratch_shapes=[
+            pltpu.VMEM(adjacency.shape, adjacency.dtype),
+            pltpu.VMEM(adjacency.shape, jnp.bfloat16),
+            pltpu.SemaphoreType.DMA((2, snapshots)),
+        ],
+        compiler_params=pltpu.CompilerParams(vmem_limit_bytes=VMEM_LIMIT),
+        cost_estimate=pl.CostEstimate(
+            flops=0, transcendentals=0, bytes_accessed=adjacency.size * 6 + 2**20
+        ),
+        name="stage",
+    )(in_hbm(adjacency), in_hbm(after))
+
+
+def restructure_kernel(*refs, pieces, layer, start):
+    hidden_refs = refs[:pieces]
+    links_hbm, scale_ref, weight_hbm, out_hbm = refs[pieces : pieces + 4]
+    links_buf, weight, gathered, mixture, out_buf, sems = refs[pieces + 4 :]
+    snapshots, owners, rows, width = out_buf.shape
+    nodes = links_hbm.shape[-1]
+    share = nodes // owners
+    chosen = slice(start, start + rows)
+    loads = [
+        pltpu.make_async_copy(links_hbm.at[s, :, chosen], links_buf.at[s], sems.at[0, s])
+        for s in range(snapshots)
+    ]
+    fetch = pltpu.make_async_copy(weight_hbm.at[layer], weight, sems.at[0, snapshots])
+    loads[0].start()
+    fetch.start()
+    for load in loads[1:]:
+        load.start()
+
+    def ready(s):
+        below = 0
+        for ref in hidden_refs:
+            count = ref.shape[2]
+            gathered[s, :, below : below + count, :] = ref[:, s]
+            below += count
+
+    def own_rows(s):
+        return gathered[s, :, chosen, :].reshape(owners * rows, width).astype(jnp.float32)
+
+    def mix(s):
+        loads[s].wait()
+        links = links_buf[s].reshape(owners * rows, nodes)
+        scale = scale_ref[s].reshape(owners, share, LANES)[:, chosen].reshape(owners * rows, LANES)
+        scale = jnp.concatenate([scale] * (width // LANES), axis=1)
+        summed = jnp.dot(
+            links, gathered[s].reshape(nodes, width), preferred_element_type=jnp.float32
+        )
+        mixture[s] = ((summed + own_rows(s)) * scale).astype(jnp.bfloat16)
+
+    stores = []
+
+    def settle(s):
+        if s == 0:
+            fetch.wait()
+        mapped = jnp.dot(mixture[s], weight[...], preferred_element_type=jnp.float32)
+        rounded = (bend(mapped) + own_rows(s)).astype(jnp.bfloat16)
+        out_buf[s] = rounded.reshape(owners, rows, width)
+        stores.append(pltpu.make_async_copy(out_buf.at[s], out_hbm.at[:, s], sems.at[1, s]))
+        stores[-1].start()
+
+    stages = (ready, mix, settle)
+    for tick in range(snapshots + len(stages) - 1):
+        for lag, step in enumerate(stages):
+            if 0 <= tick - lag < snapshots:
+                step(tick - lag)
+    for store in stores:
+        store.wait()
+
+
+def restructure(hidden, links, scale, w_struct, layer, start, rows):
+    snapshots, nodes, _ = links.shape
+    width = w_struct.shape[-1]
+    owners = hidden[0].shape[0]
+    share = nodes // owners
+    flops = 2 * snapshots * owners * rows * width * (nodes + width)
+    near = pl.BlockSpec(memory_space=pltpu.VMEM)
+    far = pl.BlockSpec(memory_space=pltpu.HBM)
+    return pl.pallas_call(
+        functools.partial(restructure_kernel, pieces=len(hidden), layer=layer, start=start),
+        out_shape=pltpu.HBM((owners, snapshots, rows, width), jnp.bfloat16),
+        in_specs=[near] * len(hidden) + [far, near, far],
+        out_specs=far,
+        scratch_shapes=[
+            pltpu.VMEM((snapshots, owners, rows, nodes), jnp.bfloat16),
+            pltpu.VMEM((width, width), jnp.bfloat16),
+            pltpu.VMEM((snapshots, owners, share, width), jnp.bfloat16),
+            pltpu.VMEM((snapshots, owners * rows, width), jnp.bfloat16),
+            pltpu.VMEM((snapshots, owners, rows, width), jnp.bfloat16),
+            pltpu.SemaphoreType.DMA((2, snapshots + 1)),
+        ],
+        compiler_params=pltpu.CompilerParams(vmem_limit_bytes=VMEM_LIMIT),
+        cost_estimate=pl.CostEstimate(
+            flops=flops, transcendentals=0, bytes_accessed=snapshots * owners * rows * width * 6
+        ),
+        name=f"structure_{layer}_{start}",
+    )(*hidden, in_hbm(links.reshape(snapshots, owners, share, nodes)), scale, in_hbm(w_struct))
 
 
 def temporal_kernel(
@@ -402,7 +551,10 @@
         arrived = []
         start = 0
         for rows in OUTWARD:
-            piece = structure(hidden, adjacency, w_struct, layer, start, rows, owners)
+            if layer == 0:
+                piece = structure(hidden, adjacency, w_struct, layer, start, rows, owners)
+            else:
+                piece = restructure(hidden, *staged, w_struct, layer, start, rows)
             piece = exchange(piece)
             arrived.append((start, piece.reshape(owners * snapshots, rows, width)))
             start += rows
@@ -415,6 +567,8 @@
             )
             hidden.append(exchange(finished.reshape(owners, snapshots, rows, width)))
             start += rows
+        if layer + 1 < BLOCKS:
+            staged = stage(adjacency, finished)
     result = None
     start = 0
     for piece in hidden:

time: 175 us -> 175 us (level)
  blocking collectives: 19.9 us -> 0 us
  waiting for transfers between devices: 52 us -> 64.7 us
  starting transfers between devices: 33.6 us -> 38.4 us
  Pallas kernels: 68.3 us -> 70.8 us
    all_to_all x1 -> x0, blocking collectives: 19.9 us -> none  [exchange(): lax.all_to_all(array, 'snap', split_axis=0, concat_axis=0, tiled=True)]
    all_to_all x7 -> x8, waiting for transfers between devices: 52 us -> 64.7 us  [exchange(): lax.all_to_all(array, 'snap', split_axis=0, concat_axis=0, tiled=True)]
    pallas_call x0 -> x3, Pallas kernels: none -> 11.1 us  [the longest x2 7.98 us: restructure(): pl.pallas_call(functools.partial(restructure_kernel, pieces=len(hidden),...]
    pallas_call x4 -> x2, Pallas kernels: 18.3 us -> 9.03 us  [structure(): pl.pallas_call(functools.partial(structure_kernel, pieces=len(hidden), la...]
    all_to_all x7 -> x8, starting transfers between devices: 33.6 us -> 38.4 us  [exchange(): lax.all_to_all(array, 'snap', split_axis=0, concat_axis=0, tiled=True)]
  transfers between devices with their start and end apart: 7 -> 8, of which waited for: 7 -> 8; matrix products, arithmetic and copies ran while one was open for 0% -> 0% of each run, Pallas kernels for 33% -> 35%
where the time goes in v4:
time: 175 us; the launch traced here: 174 us
  Pallas kernels  70.8 us (40%)
  waiting for transfers between devices  64.7 us (37%)
  starting transfers between devices  38.4 us (22%)
    all_to_all x8, waiting for transfers between devices, exchange(): lax.all_to_all(array, 'snap', split_axis=0, concat_axis=0, tiled=True)  64.7 us
    pallas_call x4, Pallas kernels, temporal(): pl.pallas_call(functools.partial(temporal_kernel, layer=layer, offset=off...  48.7 us
    all_to_all x8, starting transfers between devices, exchange(): lax.all_to_all(array, 'snap', split_axis=0, concat_axis=0, tiled=True)  38.4 us
    pallas_call x2, Pallas kernels, structure(): pl.pallas_call(functools.partial(structure_kernel, pieces=len(hidden), la...  9.03 us
    pallas_call x2, Pallas kernels, restructure(): pl.pallas_call(functools.partial(restructure_kernel, pieces=len(hidden),...  7.98 us
  transfers between devices with their start and end apart: 8, of which 8 were waited for; matrix products, arithmetic and copies ran while one was open for 0% of the time, Pallas kernels for 35%

profile of v4, /device:TPU:1, one launch (start us, length us, event | category | flops | bytes accessed | tf_op | source)
XLA Modules:
  0.0 174.2 jit_solution(5004030962181492059)
XLA Ops:
  0.0 4.5 %structure_0_16.1 = bf16[16,4,16,512]{3,2,1,0:T(8,128)(2,1)} custom-call(bf16[4,512,512]{2,1,0:T(8,128)(2,1)} %refs_0_.3, s32[4,16,32,512]{3,2,1,0:T(8,128)} %bitcast.14, bf16[2,512,512]{2,1,0:T(8,128)(2,1)} %refs_4_.3), custom_call_target="tpu_custom_call" | custom-call | flops 1073741824 | bytes 8388608 | tf_op jit(solution)/shard_map/structure_0_16/pallas_call | solution.py:122
  4.5 6.9 %all-to-all-start.2 = ((bf16[16,4,16,512]{3,2,1,0:T(8,128)(2,1)}), bf16[16,4,16,512]{3,2,1,0:T(8,128)(2,1)S(1)}, u32[]{:S(2)}, u32[]{:S(2)}) async-start(bf16[16,4,16,512]{3,2,1,0:T(8,128)(2,1)} %structure_0_16.1), calls=%async_computation.2 | async-start | bytes 2097152 | tf_op jit(solution)/shard_map/all_to_all | solution.py:546
  11.4 4.5 %structure_0_0.1 = bf16[16,4,16,512]{3,2,1,0:T(8,128)(2,1)} custom-call(bf16[4,512,512]{2,1,0:T(8,128)(2,1)} %refs_0_.3, s32[4,16,32,512]{3,2,1,0:T(8,128)} %bitcast.15, bf16[2,512,512]{2,1,0:T(8,128)(2,1)} %refs_4_.3), custom_call_target="tpu_custom_call" | custom-call | flops 1073741824 | bytes 8388608 | tf_op jit(solution)/shard_map/structure_0_0/pallas_call | solution.py:122
  16.0 11.1 %all-to-all-done.2 = bf16[16,4,16,512]{3,2,1,0:T(8,128)(2,1)S(1)} async-done(((bf16[16,4,16,512]{3,2,1,0:T(8,128)(2,1)}), bf16[16,4,16,512]{3,2,1,0:T(8,128)(2,1)S(1)}, u32[]{:S(2)}, u32[]{:S(2)}) %all-to-all-start.2) | async-done | bytes 1048608 | tf_op jit(solution)/shard_map/all_to_all | solution.py:546
  27.1 4.4 %all-to-all-start = ((bf16[16,4,16,512]{3,2,1,0:T(8,128)(2,1)}), bf16[16,4,16,512]{3,2,1,0:T(8,128)(2,1)S(1)}, u32[]{:S(2)}, u32[]{:S(2)}) async-start(bf16[16,4,16,512]{3,2,1,0:T(8,128)(2,1)} %structure_0_0.1), calls=%async_computation | async-start | bytes 2097152 | tf_op jit(solution)/shard_map/all_to_all | solution.py:546
  31.5 12.0 %temporal_0_16.1.after_hbm = bf16[64,16,512]{2,1,0:T(8,128)(2,1)} custom-call(s32[32]{0:T(128)S(1)} %copy-done.2, bf16[64,16,512]{2,1,0:T(8,128)(2,1)S(1)} %bitcast.13, bf16[64,512]{1,0:T(8,128)(2,1)S(1)} %copy-done, f32[2,2,512]{2,1,0:T(2,128)S(1)} %copy-done.1, bf16[2,512,512]{2,1,0:T(8,128)(2,1)} %wq_hbm.7, bf16[2,512,512]{2,1,0:T(8,128)(2,1)} %wk_hbm.7, ...), custom_call_target="tpu_custom_call" | custom-call | flops 4294967296 | bytes 1048576 | tf_op jit(solution)/shard_map/temporal_0_16/pallas_call | solution.py:462
  43.6 3.7 %all-to-all-done = bf16[16,4,16,512]{3,2,1,0:T(8,128)(2,1)S(1)} async-done(((bf16[16,4,16,512]{3,2,1,0:T(8,128)(2,1)}), bf16[16,4,16,512]{3,2,1,0:T(8,128)(2,1)S(1)}, u32[]{:S(2)}, u32[]{:S(2)}) %all-to-all-start) | async-done | bytes 1048608 | tf_op jit(solution)/shard_map/all_to_all | solution.py:546
  47.3 4.4 %all-to-all-start.3 = ((bf16[16,4,16,512]{3,2,1,0:T(8,128)(2,1)}), bf16[16,4,16,512]{3,2,1,0:T(8,128)(2,1)S(1)}, u32[]{:S(2)}, u32[]{:S(2)}) async-start(bf16[16,4,16,512]{3,2,1,0:T(8,128)(2,1)} %bitcast.18), calls=%async_computation.3 | async-start | bytes 2097152 | tf_op jit(solution)/shard_map/all_to_all | solution.py:546
  51.7 12.0 %temporal_0_0.1 = bf16[64,16,512]{2,1,0:T(8,128)(2,1)} custom-call(s32[32]{0:T(128)S(1)} %copy-done.2, bf16[64,16,512]{2,1,0:T(8,128)(2,1)S(1)} %bitcast.11, bf16[64,512]{1,0:T(8,128)(2,1)S(1)} %copy-done, f32[2,2,512]{2,1,0:T(2,128)S(1)} %copy-done.1, bf16[2,512,512]{2,1,0:T(8,128)(2,1)} %wq_hbm.7, bf16[2,512,512]{2,1,0:T(8,128)(2,1)} %wk_hbm.7, ...), custom_call_target="tpu_custom_call" | custom-call | flops 4294967296 | bytes 1048576 | tf_op jit(solution)/shard_map/temporal_0_0/pallas_call | solution.py:462
  63.7 3.8 %all-to-all-done.3.refs_1_ = bf16[16,4,16,512]{3,2,1,0:T(8,128)(2,1)S(1)} async-done(((bf16[16,4,16,512]{3,2,1,0:T(8,128)(2,1)}), bf16[16,4,16,512]{3,2,1,0:T(8,128)(2,1)S(1)}, u32[]{:S(2)}, u32[]{:S(2)}) %all-to-all-start.3) | async-done | bytes 1048608 | tf_op jit(solution)/shard_map/all_to_all | solution.py:546
  67.4 4.4 %all-to-all-start.1 = ((bf16[16,4,16,512]{3,2,1,0:T(8,128)(2,1)}), bf16[16,4,16,512]{3,2,1,0:T(8,128)(2,1)S(1)}, u32[]{:S(2)}, u32[]{:S(2)}) async-start(bf16[16,4,16,512]{3,2,1,0:T(8,128)(2,1)} %bitcast.19), calls=%async_computation.1 | async-start | bytes 2097152 | tf_op jit(solution)/shard_map/all_to_all | solution.py:546
  71.8 3.1 %stage.1 = (bf16[4,512,512]{2,1,0:T(8,128)(2,1)}, f32[4,512,128]{2,1,0:T(8,128)S(1)}) custom-call(s32[4,512,512]{2,1,0:T(8,128)} %links_hbm.1, bf16[64,16,512]{2,1,0:T(8,128)(2,1)} %temporal_0_16.1.after_hbm), custom_call_target="tpu_custom_call" | custom-call | bytes 7340032 | tf_op jit(solution)/shard_map/stage/pallas_call | solution.py:171
  75.0 12.6 %all-to-all-done.1.refs_0_ = bf16[16,4,16,512]{3,2,1,0:T(8,128)(2,1)S(1)} async-done(((bf16[16,4,16,512]{3,2,1,0:T(8,128)(2,1)}), bf16[16,4,16,512]{3,2,1,0:T(8,128)(2,1)S(1)}, u32[]{:S(2)}, u32[]{:S(2)}) %all-to-all-start.1) | async-done | bytes 1048608 | tf_op jit(solution)/shard_map/all_to_all | solution.py:546
  87.6 4.0 %structure_1_0.1 = bf16[16,4,16,512]{3,2,1,0:T(8,128)(2,1)} custom-call(bf16[16,4,16,512]{3,2,1,0:T(8,128)(2,1)S(1)} %all-to-all-done.1.refs_0_, bf16[16,4,16,512]{3,2,1,0:T(8,128)(2,1)S(1)} %all-to-all-done.3.refs_1_, bf16[4,16,32,512]{3,2,1,0:T(8,128)(2,1)} %bitcast.16, f32[4,512,128]{2,1,0:T(8,128)S(1)} %get-tuple-element.8.refs_3_, ...), custom_call_target="tpu_custom_call" | custom-call | flops 1073741824 | bytes 3145728 | tf_op jit(solution)/shard_map/structure_1_0/pallas_call | solution.py:258
  91.6 5.0 %all-to-all-start.6 = ((bf16[16,4,16,512]{3,2,1,0:T(8,128)(2,1)}), bf16[16,4,16,512]{3,2,1,0:T(8,128)(2,1)}, u32[]{:S(2)}, u32[]{:S(2)}) async-start(bf16[16,4,16,512]{3,2,1,0:T(8,128)(2,1)} %structure_1_0.1), calls=%async_computation.6 | async-start | bytes 2097152 | tf_op jit(solution)/shard_map/all_to_all | solution.py:546
  96.7 4.0 %structure_1_16.1 = bf16[16,4,16,512]{3,2,1,0:T(8,128)(2,1)} custom-call(bf16[16,4,16,512]{3,2,1,0:T(8,128)(2,1)S(1)} %all-to-all-done.1.refs_0_, bf16[16,4,16,512]{3,2,1,0:T(8,128)(2,1)S(1)} %all-to-all-done.3.refs_1_, bf16[4,16,32,512]{3,2,1,0:T(8,128)(2,1)} %bitcast.17, f32[4,512,128]{2,1,0:T(8,128)S(1)} %get-tuple-element.8.refs_3_, ...), custom_call_target="tpu_custom_call" | custom-call | flops 1073741824 | bytes 3145728 | tf_op jit(solution)/shard_map/structure_1_16/pallas_call | solution.py:258
  100.7 11.9 %all-to-all-done.6 = bf16[16,4,16,512]{3,2,1,0:T(8,128)(2,1)} async-done(((bf16[16,4,16,512]{3,2,1,0:T(8,128)(2,1)}), bf16[16,4,16,512]{3,2,1,0:T(8,128)(2,1)}, u32[]{:S(2)}, u32[]{:S(2)}) %all-to-all-start.6) | async-done | bytes 1048608 | tf_op jit(solution)/shard_map/all_to_all | solution.py:546
  112.5 4.4 %all-to-all-start.4 = ((bf16[16,4,16,512]{3,2,1,0:T(8,128)(2,1)}), bf16[16,4,16,512]{3,2,1,0:T(8,128)(2,1)S(1)}, u32[]{:S(2)}, u32[]{:S(2)}) async-start(bf16[16,4,16,512]{3,2,1,0:T(8,128)(2,1)} %structure_1_16.1), calls=%async_computation.4 | async-start | bytes 2097152 | tf_op jit(solution)/shard_map/all_to_all | solution.py:546
  116.9 12.7 %temporal_1_0.1 = bf16[64,16,512]{2,1,0:T(8,128)(2,1)} custom-call(s32[32]{0:T(128)S(1)} %copy-done.2, bf16[64,16,512]{2,1,0:T(8,128)(2,1)} %bitcast.8.x_ref, bf16[64,512]{1,0:T(8,128)(2,1)S(1)} %copy-done, f32[2,2,512]{2,1,0:T(2,128)S(1)} %copy-done.1, bf16[2,512,512]{2,1,0:T(8,128)(2,1)} %wq_hbm.7, bf16[2,512,512]{2,1,0:T(8,128)(2,1)} %wk_hbm.7, ...), custom_call_target="tpu_custom_call" | custom-call | flops 4294967296 | bytes 1048576 | tf_op jit(solution)/shard_map/temporal_1_0/pallas_call | solution.py:462
  132.7 4.4 %all-to-all-start.7 = ((bf16[16,4,16,512]{3,2,1,0:T(8,128)(2,1)}), bf16[16,4,16,512]{3,2,1,0:T(8,128)(2,1)S(1)}, u32[]{:S(2)}, u32[]{:S(2)}) async-start(bf16[16,4,16,512]{3,2,1,0:T(8,128)(2,1)} %bitcast.20), calls=%async_computation.7 | async-start | bytes 2097152 | tf_op jit(solution)/shard_map/all_to_all | solution.py:546
  137.1 12.0 %temporal_1_16.1 = bf16[64,16,512]{2,1,0:T(8,128)(2,1)} custom-call(s32[32]{0:T(128)S(1)} %copy-done.2, bf16[64,16,512]{2,1,0:T(8,128)(2,1)S(1)} %bitcast.12, bf16[64,512]{1,0:T(8,128)(2,1)S(1)} %copy-done, f32[2,2,512]{2,1,0:T(2,128)S(1)} %copy-done.1, bf16[2,512,512]{2,1,0:T(8,128)(2,1)} %wq_hbm.7, bf16[2,512,512]{2,1,0:T(8,128)(2,1)} %wk_hbm.7, ...), custom_call_target="tpu_custom_call" | custom-call | flops 4294967296 | bytes 1048576 | tf_op jit(solution)/shard_map/temporal_1_16/pallas_call | solution.py:462
  149.1 3.7 %all-to-all-done.7.piece_ref = bf16[16,4,16,512]{3,2,1,0:T(8,128)(2,1)S(1)} async-done(((bf16[16,4,16,512]{3,2,1,0:T(8,128)(2,1)}), bf16[16,4,16,512]{3,2,1,0:T(8,128)(2,1)S(1)}, u32[]{:S(2)}, u32[]{:S(2)}) %all-to-all-start.7) | async-done | bytes 1048608 | tf_op jit(solution)/shard_map/all_to_all | solution.py:546
  152.9 4.4 %all-to-all-start.5 = ((bf16[16,4,16,512]{3,2,1,0:T(8,128)(2,1)}), bf16[16,4,16,512]{3,2,1,0:T(8,128)(2,1)S(1)}, u32[]{:S(2)}, u32[]{:S(2)}) async-start(bf16[16,4,16,512]{3,2,1,0:T(8,128)(2,1)} %bitcast.21), calls=%async_computation.5 | async-start | bytes 2097152 | tf_op jit(solution)/shard_map/all_to_all | solution.py:546
  158.3 14.8 %all-to-all-done.5.piece_ref = bf16[16,4,16,512]{3,2,1,0:T(8,128)(2,1)S(1)} async-done(((bf16[16,4,16,512]{3,2,1,0:T(8,128)(2,1)}), bf16[16,4,16,512]{3,2,1,0:T(8,128)(2,1)S(1)}, u32[]{:S(2)}, u32[]{:S(2)}) %all-to-all-start.5) | async-done | bytes 1048608 | tf_op jit(solution)/shard_map/all_to_all | solution.py:546
  (9 shorter events, 5.1 us)
Async XLA Ops:
  4.5 22.6 %all-to-all-start.2 = ((bf16[16,4,16,512]{3,2,1,0:T(8,128)(2,1)}), bf16[16,4,16,512]{3,2,1,0:T(8,128)(2,1)S(1)}, u32[]{:S(2)}, u32[]{:S(2)}) async-start(bf16[16,4,16,512]{3,2,1,0:T(8,128)(2,1)} %structure_0_16.1), calls=%async_computation.2 | async-start | bytes 2097152 | tf_op jit(solution)/shard_map/all_to_all | solution.py:546
  15.9 15.6 %copy-start = (bf16[64,512]{1,0:T(8,128)(2,1)S(1)}, bf16[64,512]{1,0:T(8,128)(2,1)}, u32[]{:S(2)}) copy-start(bf16[64,512]{1,0:T(8,128)(2,1)} %pos_ref.7) | copy-start | bytes 196612
  16.0 15.6 %copy-start.1 = (f32[2,2,512]{2,1,0:T(2,128)S(1)}, f32[2,2,512]{2,1,0:T(2,128)}, u32[]{:S(2)}) copy-start(f32[2,2,512]{2,1,0:T(2,128)} %gain_ref.7) | copy-start | bytes 24580
  16.0 15.6 %copy-start.2 = (s32[32]{0:T(128)S(1)}, s32[32]{0:T(128)}, u32[]{:S(2)}) copy-start(s32[32]{0:T(128)} %first_ref.7) | copy-start | bytes 388
  27.1 20.2 %all-to-all-start = ((bf16[16,4,16,512]{3,2,1,0:T(8,128)(2,1)}), bf16[16,4,16,512]{3,2,1,0:T(8,128)(2,1)S(1)}, u32[]{:S(2)}, u32[]{:S(2)}) async-start(bf16[16,4,16,512]{3,2,1,0:T(8,128)(2,1)} %structure_0_0.1), calls=%async_computation | async-start | bytes 2097152 | tf_op jit(solution)/shard_map/all_to_all | solution.py:546
  47.3 20.2 %all-to-all-start.3 = ((bf16[16,4,16,512]{3,2,1,0:T(8,128)(2,1)}), bf16[16,4,16,512]{3,2,1,0:T(8,128)(2,1)S(1)}, u32[]{:S(2)}, u32[]{:S(2)}) async-start(bf16[16,4,16,512]{3,2,1,0:T(8,128)(2,1)} %bitcast.18), calls=%async_computation.3 | async-start | bytes 2097152 | tf_op jit(solution)/shard_map/all_to_all | solution.py:546
  67.4 20.2 %all-to-all-start.1 = ((bf16[16,4,16,512]{3,2,1,0:T(8,128)(2,1)}), bf16[16,4,16,512]{3,2,1,0:T(8,128)(2,1)S(1)}, u32[]{:S(2)}, u32[]{:S(2)}) async-start(bf16[16,4,16,512]{3,2,1,0:T(8,128)(2,1)} %bitcast.19), calls=%async_computation.1 | async-start | bytes 2097152 | tf_op jit(solution)/shard_map/all_to_all | solution.py:546
  91.6 20.9 %all-to-all-start.6 = ((bf16[16,4,16,512]{3,2,1,0:T(8,128)(2,1)}), bf16[16,4,16,512]{3,2,1,0:T(8,128)(2,1)}, u32[]{:S(2)}, u32[]{:S(2)}) async-start(bf16[16,4,16,512]{3,2,1,0:T(8,128)(2,1)} %structure_1_0.1), calls=%async_computation.6 | async-start | bytes 2097152 | tf_op jit(solution)/shard_map/all_to_all | solution.py:546
  112.5 20.2 %all-to-all-start.4 = ((bf16[16,4,16,512]{3,2,1,0:T(8,128)(2,1)}), bf16[16,4,16,512]{3,2,1,0:T(8,128)(2,1)S(1)}, u32[]{:S(2)}, u32[]{:S(2)}) async-start(bf16[16,4,16,512]{3,2,1,0:T(8,128)(2,1)} %structure_1_16.1), calls=%async_computation.4 | async-start | bytes 2097152 | tf_op jit(solution)/shard_map/all_to_all | solution.py:546
  132.7 20.2 %all-to-all-start.7 = ((bf16[16,4,16,512]{3,2,1,0:T(8,128)(2,1)}), bf16[16,4,16,512]{3,2,1,0:T(8,128)(2,1)S(1)}, u32[]{:S(2)}, u32[]{:S(2)}) async-start(bf16[16,4,16,512]{3,2,1,0:T(8,128)(2,1)} %bitcast.20), calls=%async_computation.7 | async-start | bytes 2097152 | tf_op jit(solution)/shard_map/all_to_all | solution.py:546
  152.9 20.2 %all-to-all-start.5 = ((bf16[16,4,16,512]{3,2,1,0:T(8,128)(2,1)}), bf16[16,4,16,512]{3,2,1,0:T(8,128)(2,1)S(1)}, u32[]{:S(2)}, u32[]{:S(2)}) async-start(bf16[16,4,16,512]{3,2,1,0:T(8,128)(2,1)} %bitcast.21), calls=%async_computation.5 | async-start | bytes 2097152 | tf_op jit(solution)/shard_map/all_to_all | solution.py:546

commit v5 on v4

--- a/solution.py
+++ b/solution.py
@@ -142,70 +142,53 @@
     )(*near, in_hbm(links), in_hbm(w_struct))
 
 
-def stage_kernel(links_hbm, after_hbm, narrow_hbm, scale_ref, whole, narrow, sems):
+def stage_kernel(links_hbm, after_hbm, staged_ref, whole, sems):
     del after_hbm
-    snapshots, nodes, _ = whole.shape
+    snapshots, owners, rows, nodes = whole.shape
     loads = [
-        pltpu.make_async_copy(links_hbm.at[s], whole.at[s], sems.at[0, s]) for s in range(snapshots)
-    ]
-    stores = [
-        pltpu.make_async_copy(narrow.at[s], narrow_hbm.at[s], sems.at[1, s])
+        pltpu.make_async_copy(links_hbm.at[s, :, 0:rows], whole.at[s], sems.at[s])
         for s in range(snapshots)
     ]
     for load in loads:
         load.start()
     for s in range(snapshots):
         loads[s].wait()
-        links = whole[s].astype(jnp.float32)
-        scale = 1.0 / (1.0 + jnp.sum(links, axis=1, keepdims=True))
-        scale_ref[s] = jnp.broadcast_to(scale, (nodes, LANES))
-        narrow[s] = links.astype(jnp.bfloat16)
-        stores[s].start()
-    for store in stores:
-        store.wait()
-
-
-def stage(adjacency, after):
+        links = whole[s].reshape(owners * rows, nodes)
+        staged_ref[s] = links.astype(jnp.float32).astype(jnp.bfloat16)
+
+
+def stage(adjacency, owners, rows, after):
     snapshots, nodes, _ = adjacency.shape
     far = pl.BlockSpec(memory_space=pltpu.HBM)
+    links = adjacency.reshape(snapshots, owners, nodes // owners, nodes)
     return pl.pallas_call(
         stage_kernel,
-        out_shape=[
-            pltpu.HBM(adjacency.shape, jnp.bfloat16),
-            pltpu.VMEM((snapshots, nodes, LANES), jnp.float32),
-        ],
+        out_shape=pltpu.VMEM((snapshots, owners * rows, nodes), jnp.bfloat16),
         in_specs=[far] * 2,
-        out_specs=[far, pl.BlockSpec(memory_space=pltpu.VMEM)],
+        out_specs=pl.BlockSpec(memory_space=pltpu.VMEM),
         scratch_shapes=[
-            pltpu.VMEM(adjacency.shape, adjacency.dtype),
-            pltpu.VMEM(adjacency.shape, jnp.bfloat16),
-            pltpu.SemaphoreType.DMA((2, snapshots)),
+            pltpu.VMEM((snapshots, owners, rows, nodes), adjacency.dtype),
+            pltpu.SemaphoreType.DMA((snapshots,)),
         ],
         compiler_params=pltpu.CompilerParams(vmem_limit_bytes=VMEM_LIMIT),
         cost_estimate=pl.CostEstimate(
-            flops=0, transcendentals=0, bytes_accessed=adjacency.size * 6 + 2**20
+            flops=0, transcendentals=0, bytes_accessed=adjacency.size * 3
         ),
         name="stage",
-    )(in_hbm(adjacency), in_hbm(after))
+    )(in_hbm(links), in_hbm(after))
 
 
 def restructure_kernel(*refs, pieces, layer, start):
     hidden_refs = refs[:pieces]
-    links_hbm, scale_ref, weight_hbm, out_hbm = refs[pieces : pieces + 4]
-    links_buf, weight, gathered, mixture, out_buf, sems = refs[pieces + 4 :]
+    staged_ref, weight_hbm, out_hbm, weight, gathered, scales, mixture, out_buf, sems = refs[pieces:]
     snapshots, owners, rows, width = out_buf.shape
-    nodes = links_hbm.shape[-1]
-    share = nodes // owners
+    nodes = staged_ref.shape[-1]
     chosen = slice(start, start + rows)
-    loads = [
-        pltpu.make_async_copy(links_hbm.at[s, :, chosen], links_buf.at[s], sems.at[0, s])
-        for s in range(snapshots)
-    ]
-    fetch = pltpu.make_async_copy(weight_hbm.at[layer], weight, sems.at[0, snapshots])
-    loads[0].start()
+    fetch = pltpu.make_async_copy(weight_hbm.at[layer], weight, sems.at[snapshots])
     fetch.start()
-    for load in loads[1:]:
-        load.start()
+
+    def links_of(s):
+        return staged_ref[s]
 
     def ready(s):
         below = 0
@@ -213,17 +196,16 @@
             count = ref.shape[2]
             gathered[s, :, below : below + count, :] = ref[:, s]
             below += count
+        degree = 1.0 + jnp.sum(links_of(s).astype(jnp.float32), axis=1, keepdims=True)
+        scales[s] = jnp.broadcast_to(1.0 / degree, (owners * rows, LANES))
 
     def own_rows(s):
         return gathered[s, :, chosen, :].reshape(owners * rows, width).astype(jnp.float32)
 
     def mix(s):
-        loads[s].wait()
-        links = links_buf[s].reshape(owners * rows, nodes)
-        scale = scale_ref[s].reshape(owners, share, LANES)[:, chosen].reshape(owners * rows, LANES)
-        scale = jnp.concatenate([scale] * (width // LANES), axis=1)
+        scale = jnp.concatenate([scales[s]] * (width // LANES), axis=1)
         summed = jnp.dot(
-            links, gathered[s].reshape(nodes, width), preferred_element_type=jnp.float32
+            links_of(s), gathered[s].reshape(nodes, width), preferred_element_type=jnp.float32
         )
         mixture[s] = ((summed + own_rows(s)) * scale).astype(jnp.bfloat16)
 
@@ -235,7 +217,7 @@
         mapped = jnp.dot(mixture[s], weight[...], preferred_element_type=jnp.float32)
         rounded = (bend(mapped) + own_rows(s)).astype(jnp.bfloat16)
         out_buf[s] = rounded.reshape(owners, rows, width)
-        stores.append(pltpu.make_async_copy(out_buf.at[s], out_hbm.at[:, s], sems.at[1, s]))
+        stores.append(pltpu.make_async_copy(out_buf.at[s], out_hbm.at[:, s], sems.at[s]))
         stores[-1].start()
 
     stages = (ready, mix, settle)
@@ -247,33 +229,31 @@
         store.wait()
 
 
-def restructure(hidden, links, scale, w_struct, layer, start, rows):
-    snapshots, nodes, _ = links.shape
-    width = w_struct.shape[-1]
-    owners = hidden[0].shape[0]
+def restructure(hidden, staged, w_struct, layer, start, rows):
+    snapshots, _, nodes = staged.shape
+    owners, _, _, width = hidden[0].shape
     share = nodes // owners
     flops = 2 * snapshots * owners * rows * width * (nodes + width)
     near = pl.BlockSpec(memory_space=pltpu.VMEM)
-    far = pl.BlockSpec(memory_space=pltpu.HBM)
     return pl.pallas_call(
         functools.partial(restructure_kernel, pieces=len(hidden), layer=layer, start=start),
         out_shape=pltpu.HBM((owners, snapshots, rows, width), jnp.bfloat16),
-        in_specs=[near] * len(hidden) + [far, near, far],
-        out_specs=far,
+        in_specs=[near] * (len(hidden) + 1) + [pl.BlockSpec(memory_space=pltpu.HBM)],
+        out_specs=pl.BlockSpec(memory_space=pltpu.HBM),
         scratch_shapes=[
-            pltpu.VMEM((snapshots, owners, rows, nodes), jnp.bfloat16),
             pltpu.VMEM((width, width), jnp.bfloat16),
             pltpu.VMEM((snapshots, owners, share, width), jnp.bfloat16),
+            pltpu.VMEM((snapshots, owners * rows, LANES), jnp.float32),
             pltpu.VMEM((snapshots, owners * rows, width), jnp.bfloat16),
             pltpu.VMEM((snapshots, owners, rows, width), jnp.bfloat16),
-            pltpu.SemaphoreType.DMA((2, snapshots + 1)),
+            pltpu.SemaphoreType.DMA((snapshots + 1,)),
         ],
         compiler_params=pltpu.CompilerParams(vmem_limit_bytes=VMEM_LIMIT),
         cost_estimate=pl.CostEstimate(
-            flops=flops, transcendentals=0, bytes_accessed=snapshots * owners * rows * width * 6
+            flops=flops, transcendentals=0, bytes_accessed=snapshots * owners * rows * width * 4
         ),
         name=f"structure_{layer}_{start}",
-    )(*hidden, in_hbm(links.reshape(snapshots, owners, share, nodes)), scale, in_hbm(w_struct))
+    )(*hidden, staged, in_hbm(w_struct))
 
 
 def temporal_kernel(
@@ -551,10 +531,10 @@
         arrived = []
         start = 0
         for rows in OUTWARD:
-            if layer == 0:
+            if layer == 0 or start > 0:
                 piece = structure(hidden, adjacency, w_struct, layer, start, rows, owners)
             else:
-                piece = restructure(hidden, *staged, w_struct, layer, start, rows)
+                piece = restructure(hidden, staged, w_struct, layer, start, rows)
             piece = exchange(piece)
             arrived.append((start, piece.reshape(owners * snapshots, rows, width)))
             start += rows
@@ -568,7 +548,7 @@
             hidden.append(exchange(finished.reshape(owners, snapshots, rows, width)))
             start += rows
         if layer + 1 < BLOCKS:
-            staged = stage(adjacency, finished)
+            staged = stage(adjacency, owners, OUTWARD[0], finished)
     result = None
     start = 0
     for piece in hidden:

time: 175 us -> 173 us (0.989)
  Pallas kernels: 70.8 us -> 67.9 us
  waiting for transfers between devices: 64.7 us -> 66.5 us
    pallas_call x2 -> x1, Pallas kernels: 7.98 us -> 3.07 us  [restructure(): pl.pallas_call(functools.partial(restructure_kernel, pieces=len(hidden),...]
    pallas_call x2 -> x3, Pallas kernels: 9.03 us -> 13.2 us  [structure(): pl.pallas_call(functools.partial(structure_kernel, pieces=len(hidden), la...]
    all_to_all x8, waiting for transfers between devices: 64.7 us -> 66.5 us  [exchange(): lax.all_to_all(array, 'snap', split_axis=0, concat_axis=0, tiled=True)]
  transfers between devices with their start and end apart: 8 -> 8, of which waited for: 8 -> 8; matrix products, arithmetic and copies ran while one was open for 0% -> 0% of each run, Pallas kernels for 35% -> 34%
where the time goes in v5:
time: 173 us
  Pallas kernels  67.9 us (39%)
  waiting for transfers between devices  66.5 us (38%)
  starting transfers between devices  37.8 us (22%)
    all_to_all x8, waiting for transfers between devices, exchange(): lax.all_to_all(array, 'snap', split_axis=0, concat_axis=0, tiled=True)  66.5 us
    pallas_call x4, Pallas kernels, temporal(): pl.pallas_call(functools.partial(temporal_kernel, layer=layer, offset=off...  48 us
    all_to_all x8, starting transfers between devices, exchange(): lax.all_to_all(array, 'snap', split_axis=0, concat_axis=0, tiled=True)  37.8 us
    pallas_call x3, Pallas kernels, structure(): pl.pallas_call(functools.partial(structure_kernel, pieces=len(hidden), la...  13.2 us
  transfers between devices with their start and end apart: 8, of which 8 were waited for; matrix products, arithmetic and copies ran while one was open for 0% of the time, Pallas kernels for 34%

profile of v5, /device:TPU:1, one launch (start us, length us, event | category | flops | bytes accessed | tf_op | source)
XLA Modules:
  0.0 172.5 jit_solution(579558624919429774)
XLA Ops:
  0.0 4.5 %structure_0_16.1 = bf16[16,4,16,512]{3,2,1,0:T(8,128)(2,1)} custom-call(bf16[4,512,512]{2,1,0:T(8,128)(2,1)} %refs_0_.3, s32[4,16,32,512]{3,2,1,0:T(8,128)} %bitcast.14, bf16[2,512,512]{2,1,0:T(8,128)(2,1)} %refs_3_.3), custom_call_target="tpu_custom_call" | custom-call | flops 1073741824 | bytes 8388608 | tf_op jit(solution)/shard_map/structure_0_16/pallas_call | solution.py:122
  4.5 6.9 %all-to-all-start.2 = ((bf16[16,4,16,512]{3,2,1,0:T(8,128)(2,1)}), bf16[16,4,16,512]{3,2,1,0:T(8,128)(2,1)S(1)}, u32[]{:S(2)}, u32[]{:S(2)}) async-start(bf16[16,4,16,512]{3,2,1,0:T(8,128)(2,1)} %structure_0_16.1), calls=%async_computation.2 | async-start | bytes 2097152 | tf_op jit(solution)/shard_map/all_to_all | solution.py:526
  11.4 4.5 %structure_0_0.1 = bf16[16,4,16,512]{3,2,1,0:T(8,128)(2,1)} custom-call(bf16[4,512,512]{2,1,0:T(8,128)(2,1)} %refs_0_.3, s32[4,16,32,512]{3,2,1,0:T(8,128)} %bitcast.15, bf16[2,512,512]{2,1,0:T(8,128)(2,1)} %refs_3_.3), custom_call_target="tpu_custom_call" | custom-call | flops 1073741824 | bytes 8388608 | tf_op jit(solution)/shard_map/structure_0_0/pallas_call | solution.py:122
  16.0 11.1 %all-to-all-done.2 = bf16[16,4,16,512]{3,2,1,0:T(8,128)(2,1)S(1)} async-done(((bf16[16,4,16,512]{3,2,1,0:T(8,128)(2,1)}), bf16[16,4,16,512]{3,2,1,0:T(8,128)(2,1)S(1)}, u32[]{:S(2)}, u32[]{:S(2)}) %all-to-all-start.2) | async-done | bytes 1048608 | tf_op jit(solution)/shard_map/all_to_all | solution.py:526
  27.1 4.4 %all-to-all-start = ((bf16[16,4,16,512]{3,2,1,0:T(8,128)(2,1)}), bf16[16,4,16,512]{3,2,1,0:T(8,128)(2,1)S(1)}, u32[]{:S(2)}, u32[]{:S(2)}) async-start(bf16[16,4,16,512]{3,2,1,0:T(8,128)(2,1)} %structure_0_0.1), calls=%async_computation | async-start | bytes 2097152 | tf_op jit(solution)/shard_map/all_to_all | solution.py:526
  31.5 12.0 %temporal_0_16.1.after_hbm = bf16[64,16,512]{2,1,0:T(8,128)(2,1)} custom-call(s32[32]{0:T(128)S(1)} %copy-done.2, bf16[64,16,512]{2,1,0:T(8,128)(2,1)S(1)} %bitcast.13, bf16[64,512]{1,0:T(8,128)(2,1)S(1)} %copy-done, f32[2,2,512]{2,1,0:T(2,128)S(1)} %copy-done.1, bf16[2,512,512]{2,1,0:T(8,128)(2,1)} %wq_hbm.7, bf16[2,512,512]{2,1,0:T(8,128)(2,1)} %wk_hbm.7, ...), custom_call_target="tpu_custom_call" | custom-call | flops 4294967296 | bytes 1048576 | tf_op jit(solution)/shard_map/temporal_0_16/pallas_call | solution.py:442
  43.5 3.7 %all-to-all-done = bf16[16,4,16,512]{3,2,1,0:T(8,128)(2,1)S(1)} async-done(((bf16[16,4,16,512]{3,2,1,0:T(8,128)(2,1)}), bf16[16,4,16,512]{3,2,1,0:T(8,128)(2,1)S(1)}, u32[]{:S(2)}, u32[]{:S(2)}) %all-to-all-start) | async-done | bytes 1048608 | tf_op jit(solution)/shard_map/all_to_all | solution.py:526
  47.3 4.4 %all-to-all-start.3 = ((bf16[16,4,16,512]{3,2,1,0:T(8,128)(2,1)}), bf16[16,4,16,512]{3,2,1,0:T(8,128)(2,1)S(1)}, u32[]{:S(2)}, u32[]{:S(2)}) async-start(bf16[16,4,16,512]{3,2,1,0:T(8,128)(2,1)} %bitcast.18), calls=%async_computation.3 | async-start | bytes 2097152 | tf_op jit(solution)/shard_map/all_to_all | solution.py:526
  51.7 11.9 %temporal_0_0.1 = bf16[64,16,512]{2,1,0:T(8,128)(2,1)} custom-call(s32[32]{0:T(128)S(1)} %copy-done.2, bf16[64,16,512]{2,1,0:T(8,128)(2,1)S(1)} %bitcast.11, bf16[64,512]{1,0:T(8,128)(2,1)S(1)} %copy-done, f32[2,2,512]{2,1,0:T(2,128)S(1)} %copy-done.1, bf16[2,512,512]{2,1,0:T(8,128)(2,1)} %wq_hbm.7, bf16[2,512,512]{2,1,0:T(8,128)(2,1)} %wk_hbm.7, ...), custom_call_target="tpu_custom_call" | custom-call | flops 4294967296 | bytes 1048576 | tf_op jit(solution)/shard_map/temporal_0_0/pallas_call | solution.py:442
  63.6 3.8 %all-to-all-done.3.refs_1_ = bf16[16,4,16,512]{3,2,1,0:T(8,128)(2,1)S(1)} async-done(((bf16[16,4,16,512]{3,2,1,0:T(8,128)(2,1)}), bf16[16,4,16,512]{3,2,1,0:T(8,128)(2,1)S(1)}, u32[]{:S(2)}, u32[]{:S(2)}) %all-to-all-start.3) | async-done | bytes 1048608 | tf_op jit(solution)/shard_map/all_to_all | solution.py:526
  67.4 4.4 %all-to-all-start.1 = ((bf16[16,4,16,512]{3,2,1,0:T(8,128)(2,1)}), bf16[16,4,16,512]{3,2,1,0:T(8,128)(2,1)S(1)}, u32[]{:S(2)}, u32[]{:S(2)}) async-start(bf16[16,4,16,512]{3,2,1,0:T(8,128)(2,1)} %bitcast.21), calls=%async_computation.1 | async-start | bytes 2097152 | tf_op jit(solution)/shard_map/all_to_all | solution.py:526
  73.4 14.2 %all-to-all-done.1.refs_0_ = bf16[16,4,16,512]{3,2,1,0:T(8,128)(2,1)S(1)} async-done(((bf16[16,4,16,512]{3,2,1,0:T(8,128)(2,1)}), bf16[16,4,16,512]{3,2,1,0:T(8,128)(2,1)S(1)}, u32[]{:S(2)}, u32[]{:S(2)}) %all-to-all-start.1) | async-done | bytes 1048608 | tf_op jit(solution)/shard_map/all_to_all | solution.py:526
  87.6 3.1 %structure_1_0.1 = bf16[16,4,16,512]{3,2,1,0:T(8,128)(2,1)} custom-call(bf16[16,4,16,512]{3,2,1,0:T(8,128)(2,1)S(1)} %all-to-all-done.1.refs_0_, bf16[16,4,16,512]{3,2,1,0:T(8,128)(2,1)S(1)} %all-to-all-done.3.refs_1_, bf16[4,256,512]{2,1,0:T(8,128)(2,1)S(1)} %stage.1.refs_2_, bf16[2,512,512]{2,1,0:T(8,128)(2,1)} %refs_3_.3), custom_call_target="tpu_custom_call" | custom-call | flops 1073741824 | bytes 2097152 | tf_op jit(solution)/shard_map/structure_1_0/pallas_call | solution.py:238
  90.7 4.4 %all-to-all-start.6 = ((bf16[16,4,16,512]{3,2,1,0:T(8,128)(2,1)}), bf16[16,4,16,512]{3,2,1,0:T(8,128)(2,1)S(1)}, u32[]{:S(2)}, u32[]{:S(2)}) async-start(bf16[16,4,16,512]{3,2,1,0:T(8,128)(2,1)} %structure_1_0.1), calls=%async_computation.6 | async-start | bytes 2097152 | tf_op jit(solution)/shard_map/all_to_all | solution.py:526
  95.1 4.2 %structure_1_16.1 = bf16[16,4,16,512]{3,2,1,0:T(8,128)(2,1)} custom-call(bf16[16,4,16,512]{3,2,1,0:T(8,128)(2,1)S(1)} %all-to-all-done.1.refs_0_, bf16[16,4,16,512]{3,2,1,0:T(8,128)(2,1)S(1)} %all-to-all-done.3.refs_1_, s32[4,16,32,512]{3,2,1,0:T(8,128)} %bitcast.17, bf16[2,512,512]{2,1,0:T(8,128)(2,1)} %refs_3_.3), custom_call_target="tpu_custom_call" | custom-call | flops 1073741824 | bytes 8388608 | tf_op jit(solution)/shard_map/structure_1_16/pallas_call | solution.py:122
  99.3 11.5 %all-to-all-done.6 = bf16[16,4,16,512]{3,2,1,0:T(8,128)(2,1)S(1)} async-done(((bf16[16,4,16,512]{3,2,1,0:T(8,128)(2,1)}), bf16[16,4,16,512]{3,2,1,0:T(8,128)(2,1)S(1)}, u32[]{:S(2)}, u32[]{:S(2)}) %all-to-all-start.6) | async-done | bytes 1048608 | tf_op jit(solution)/shard_map/all_to_all | solution.py:526
  110.8 4.4 %all-to-all-start.4 = ((bf16[16,4,16,512]{3,2,1,0:T(8,128)(2,1)}), bf16[16,4,16,512]{3,2,1,0:T(8,128)(2,1)S(1)}, u32[]{:S(2)}, u32[]{:S(2)}) async-start(bf16[16,4,16,512]{3,2,1,0:T(8,128)(2,1)} %structure_1_16.1), calls=%async_computation.4 | async-start | bytes 2097152 | tf_op jit(solution)/shard_map/all_to_all | solution.py:526
  115.3 12.0 %temporal_1_0.1 = bf16[64,16,512]{2,1,0:T(8,128)(2,1)} custom-call(s32[32]{0:T(128)S(1)} %copy-done.2, bf16[64,16,512]{2,1,0:T(8,128)(2,1)S(1)} %bitcast.10, bf16[64,512]{1,0:T(8,128)(2,1)S(1)} %copy-done, f32[2,2,512]{2,1,0:T(2,128)S(1)} %copy-done.1, bf16[2,512,512]{2,1,0:T(8,128)(2,1)} %wq_hbm.7, bf16[2,512,512]{2,1,0:T(8,128)(2,1)} %wk_hbm.7, ...), custom_call_target="tpu_custom_call" | custom-call | flops 4294967296 | bytes 1048576 | tf_op jit(solution)/shard_map/temporal_1_0/pallas_call | solution.py:442
  127.3 3.7 %all-to-all-done.4 = bf16[16,4,16,512]{3,2,1,0:T(8,128)(2,1)S(1)} async-done(((bf16[16,4,16,512]{3,2,1,0:T(8,128)(2,1)}), bf16[16,4,16,512]{3,2,1,0:T(8,128)(2,1)S(1)}, u32[]{:S(2)}, u32[]{:S(2)}) %all-to-all-start.4) | async-done | bytes 1048608 | tf_op jit(solution)/shard_map/all_to_all | solution.py:526
  131.0 4.4 %all-to-all-start.7 = ((bf16[16,4,16,512]{3,2,1,0:T(8,128)(2,1)}), bf16[16,4,16,512]{3,2,1,0:T(8,128)(2,1)S(1)}, u32[]{:S(2)}, u32[]{:S(2)}) async-start(bf16[16,4,16,512]{3,2,1,0:T(8,128)(2,1)} %bitcast.19), calls=%async_computation.7 | async-start | bytes 2097152 | tf_op jit(solution)/shard_map/all_to_all | solution.py:526
  135.4 12.0 %temporal_1_16.1 = bf16[64,16,512]{2,1,0:T(8,128)(2,1)} custom-call(s32[32]{0:T(128)S(1)} %copy-done.2, bf16[64,16,512]{2,1,0:T(8,128)(2,1)S(1)} %bitcast.12, bf16[64,512]{1,0:T(8,128)(2,1)S(1)} %copy-done, f32[2,2,512]{2,1,0:T(2,128)S(1)} %copy-done.1, bf16[2,512,512]{2,1,0:T(8,128)(2,1)} %wq_hbm.7, bf16[2,512,512]{2,1,0:T(8,128)(2,1)} %wk_hbm.7, ...), custom_call_target="tpu_custom_call" | custom-call | flops 4294967296 | bytes 1048576 | tf_op jit(solution)/shard_map/temporal_1_16/pallas_call | solution.py:442
  147.5 3.7 %all-to-all-done.7.piece_ref = bf16[16,4,16,512]{3,2,1,0:T(8,128)(2,1)S(1)} async-done(((bf16[16,4,16,512]{3,2,1,0:T(8,128)(2,1)}), bf16[16,4,16,512]{3,2,1,0:T(8,128)(2,1)S(1)}, u32[]{:S(2)}, u32[]{:S(2)}) %all-to-all-start.7) | async-done | bytes 1048608 | tf_op jit(solution)/shard_map/all_to_all | solution.py:526
  151.2 4.4 %all-to-all-start.5 = ((bf16[16,4,16,512]{3,2,1,0:T(8,128)(2,1)}), bf16[16,4,16,512]{3,2,1,0:T(8,128)(2,1)S(1)}, u32[]{:S(2)}, u32[]{:S(2)}) async-start(bf16[16,4,16,512]{3,2,1,0:T(8,128)(2,1)} %bitcast.20), calls=%async_computation.5 | async-start | bytes 2097152 | tf_op jit(solution)/shard_map/all_to_all | solution.py:526
  156.6 14.8 %all-to-all-done.5.piece_ref = bf16[16,4,16,512]{3,2,1,0:T(8,128)(2,1)S(1)} async-done(((bf16[16,4,16,512]{3,2,1,0:T(8,128)(2,1)}), bf16[16,4,16,512]{3,2,1,0:T(8,128)(2,1)S(1)}, u32[]{:S(2)}, u32[]{:S(2)}) %all-to-all-start.5) | async-done | bytes 1048608 | tf_op jit(solution)/shard_map/all_to_all | solution.py:526
  (9 shorter events, 3.6 us)
Async XLA Ops:
  4.5 22.6 %all-to-all-start.2 = ((bf16[16,4,16,512]{3,2,1,0:T(8,128)(2,1)}), bf16[16,4,16,512]{3,2,1,0:T(8,128)(2,1)S(1)}, u32[]{:S(2)}, u32[]{:S(2)}) async-start(bf16[16,4,16,512]{3,2,1,0:T(8,128)(2,1)} %structure_0_16.1), calls=%async_computation.2 | async-start | bytes 2097152 | tf_op jit(solution)/shard_map/all_to_all | solution.py:526
  15.9 15.6 %copy-start = (bf16[64,512]{1,0:T(8,128)(2,1)S(1)}, bf16[64,512]{1,0:T(8,128)(2,1)}, u32[]{:S(2)}) copy-start(bf16[64,512]{1,0:T(8,128)(2,1)} %pos_ref.7) | copy-start | bytes 196612
  15.9 15.6 %copy-start.1 = (f32[2,2,512]{2,1,0:T(2,128)S(1)}, f32[2,2,512]{2,1,0:T(2,128)}, u32[]{:S(2)}) copy-start(f32[2,2,512]{2,1,0:T(2,128)} %gain_ref.7) | copy-start | bytes 24580
  16.0 15.6 %copy-start.2 = (s32[32]{0:T(128)S(1)}, s32[32]{0:T(128)}, u32[]{:S(2)}) copy-start(s32[32]{0:T(128)} %first_ref.7) | copy-start | bytes 388
  27.1 20.2 %all-to-all-start = ((bf16[16,4,16,512]{3,2,1,0:T(8,128)(2,1)}), bf16[16,4,16,512]{3,2,1,0:T(8,128)(2,1)S(1)}, u32[]{:S(2)}, u32[]{:S(2)}) async-start(bf16[16,4,16,512]{3,2,1,0:T(8,128)(2,1)} %structure_0_0.1), calls=%async_computation | async-start | bytes 2097152 | tf_op jit(solution)/shard_map/all_to_all | solution.py:526
  47.3 20.2 %all-to-all-start.3 = ((bf16[16,4,16,512]{3,2,1,0:T(8,128)(2,1)}), bf16[16,4,16,512]{3,2,1,0:T(8,128)(2,1)S(1)}, u32[]{:S(2)}, u32[]{:S(2)}) async-start(bf16[16,4,16,512]{3,2,1,0:T(8,128)(2,1)} %bitcast.18), calls=%async_computation.3 | async-start | bytes 2097152 | tf_op jit(solution)/shard_map/all_to_all | solution.py:526
  67.4 20.2 %all-to-all-start.1 = ((bf16[16,4,16,512]{3,2,1,0:T(8,128)(2,1)}), bf16[16,4,16,512]{3,2,1,0:T(8,128)(2,1)S(1)}, u32[]{:S(2)}, u32[]{:S(2)}) async-start(bf16[16,4,16,512]{3,2,1,0:T(8,128)(2,1)} %bitcast.21), calls=%async_computation.1 | async-start | bytes 2097152 | tf_op jit(solution)/shard_map/all_to_all | solution.py:526
  90.7 20.2 %all-to-all-start.6 = ((bf16[16,4,16,512]{3,2,1,0:T(8,128)(2,1)}), bf16[16,4,16,512]{3,2,1,0:T(8,128)(2,1)S(1)}, u32[]{:S(2)}, u32[]{:S(2)}) async-start(bf16[16,4,16,512]{3,2,1,0:T(8,128)(2,1)} %structure_1_0.1), calls=%async_computation.6 | async-start | bytes 2097152 | tf_op jit(solution)/shard_map/all_to_all | solution.py:526
  110.8 20.2 %all-to-all-start.4 = ((bf16[16,4,16,512]{3,2,1,0:T(8,128)(2,1)}), bf16[16,4,16,512]{3,2,1,0:T(8,128)(2,1)S(1)}, u32[]{:S(2)}, u32[]{:S(2)}) async-start(bf16[16,4,16,512]{3,2,1,0:T(8,128)(2,1)} %structure_1_16.1), calls=%async_computation.4 | async-start | bytes 2097152 | tf_op jit(solution)/shard_map/all_to_all | solution.py:526
  131.0 20.2 %all-to-all-start.7 = ((bf16[16,4,16,512]{3,2,1,0:T(8,128)(2,1)}), bf16[16,4,16,512]{3,2,1,0:T(8,128)(2,1)S(1)}, u32[]{:S(2)}, u32[]{:S(2)}) async-start(bf16[16,4,16,512]{3,2,1,0:T(8,128)(2,1)} %bitcast.19), calls=%async_computation.7 | async-start | bytes 2097152 | tf_op jit(solution)/shard_map/all_to_all | solution.py:526
  151.2 20.2 %all-to-all-start.5 = ((bf16[16,4,16,512]{3,2,1,0:T(8,128)(2,1)}), bf16[16,4,16,512]{3,2,1,0:T(8,128)(2,1)S(1)}, u32[]{:S(2)}, u32[]{:S(2)}) async-start(bf16[16,4,16,512]{3,2,1,0:T(8,128)(2,1)} %bitcast.20), calls=%async_computation.5 | async-start | bytes 2097152 | tf_op jit(solution)/shard_map/all_to_all | solution.py:526

commit v6 on v5

--- a/solution.py
+++ b/solution.py
@@ -473,11 +473,15 @@
 def deliver_kernel(piece_ref, *refs, start):
     out_hbm, sems = refs[-2:]
     owners, snapshots, rows, _ = piece_ref.shape
+    half = owners // 2
     stores = [
         pltpu.make_async_copy(
-            piece_ref.at[:, s], out_hbm.at[s, :, start : start + rows], sems.at[s]
+            piece_ref.at[part * half : (part + 1) * half, s],
+            out_hbm.at[s, part * half : (part + 1) * half, start : start + rows],
+            sems.at[s, part],
         )
         for s in range(snapshots)
+        for part in range(2)
     ]
     for store in stores:
         store.start()
@@ -494,7 +498,7 @@
         out_shape=pltpu.HBM((snapshots, owners, share, width), piece.dtype),
         in_specs=[pl.BlockSpec(memory_space=pltpu.VMEM)] + [far] * (len(operands) - 1),
         out_specs=far,
-        scratch_shapes=[pltpu.SemaphoreType.DMA((snapshots,))],
+        scratch_shapes=[pltpu.SemaphoreType.DMA((snapshots, 2))],
         input_output_aliases={} if target is None else {1: 0},
         compiler_params=pltpu.CompilerParams(vmem_limit_bytes=VMEM_LIMIT),
         cost_estimate=pl.CostEstimate(

time: 173 us -> 173 us (level)
  no operation moved by 1% of the time
where the time goes in v6:
time: 173 us
  Pallas kernels  67.9 us (39%)
  waiting for transfers between devices  66.5 us (38%)
  starting transfers between devices  37.8 us (22%)
    all_to_all x8, waiting for transfers between devices, exchange(): lax.all_to_all(array, 'snap', split_axis=0, concat_axis=0, tiled=True)  66.5 us
    pallas_call x4, Pallas kernels, temporal(): pl.pallas_call(functools.partial(temporal_kernel, layer=layer, offset=off...  48 us
    all_to_all x8, starting transfers between devices, exchange(): lax.all_to_all(array, 'snap', split_axis=0, concat_axis=0, tiled=True)  37.8 us
    pallas_call x3, Pallas kernels, structure(): pl.pallas_call(functools.partial(structure_kernel, pieces=len(hidden), la...  13.2 us
  transfers between devices with their start and end apart: 8, of which 8 were waited for; matrix products, arithmetic and copies ran while one was open for 0% of the time, Pallas kernels for 34%

profile of v6, /device:TPU:1, one launch (start us, length us, event | category | flops | bytes accessed | tf_op | source)
XLA Modules:
  0.0 172.5 jit_solution(10290007986992544596)
XLA Ops:
  0.0 4.5 %structure_0_16.1 = bf16[16,4,16,512]{3,2,1,0:T(8,128)(2,1)} custom-call(bf16[4,512,512]{2,1,0:T(8,128)(2,1)} %refs_0_.3, s32[4,16,32,512]{3,2,1,0:T(8,128)} %bitcast.14, bf16[2,512,512]{2,1,0:T(8,128)(2,1)} %refs_3_.3), custom_call_target="tpu_custom_call" | custom-call | flops 1073741824 | bytes 8388608 | tf_op jit(solution)/shard_map/structure_0_16/pallas_call | solution.py:122
  4.5 6.9 %all-to-all-start.2 = ((bf16[16,4,16,512]{3,2,1,0:T(8,128)(2,1)}), bf16[16,4,16,512]{3,2,1,0:T(8,128)(2,1)S(1)}, u32[]{:S(2)}, u32[]{:S(2)}) async-start(bf16[16,4,16,512]{3,2,1,0:T(8,128)(2,1)} %structure_0_16.1), calls=%async_computation.2 | async-start | bytes 2097152 | tf_op jit(solution)/shard_map/all_to_all | solution.py:530
  11.4 4.5 %structure_0_0.1 = bf16[16,4,16,512]{3,2,1,0:T(8,128)(2,1)} custom-call(bf16[4,512,512]{2,1,0:T(8,128)(2,1)} %refs_0_.3, s32[4,16,32,512]{3,2,1,0:T(8,128)} %bitcast.15, bf16[2,512,512]{2,1,0:T(8,128)(2,1)} %refs_3_.3), custom_call_target="tpu_custom_call" | custom-call | flops 1073741824 | bytes 8388608 | tf_op jit(solution)/shard_map/structure_0_0/pallas_call | solution.py:122
  16.0 11.1 %all-to-all-done.2 = bf16[16,4,16,512]{3,2,1,0:T(8,128)(2,1)S(1)} async-done(((bf16[16,4,16,512]{3,2,1,0:T(8,128)(2,1)}), bf16[16,4,16,512]{3,2,1,0:T(8,128)(2,1)S(1)}, u32[]{:S(2)}, u32[]{:S(2)}) %all-to-all-start.2) | async-done | bytes 1048608 | tf_op jit(solution)/shard_map/all_to_all | solution.py:530
  27.1 4.4 %all-to-all-start = ((bf16[16,4,16,512]{3,2,1,0:T(8,128)(2,1)}), bf16[16,4,16,512]{3,2,1,0:T(8,128)(2,1)S(1)}, u32[]{:S(2)}, u32[]{:S(2)}) async-start(bf16[16,4,16,512]{3,2,1,0:T(8,128)(2,1)} %structure_0_0.1), calls=%async_computation | async-start | bytes 2097152 | tf_op jit(solution)/shard_map/all_to_all | solution.py:530
  31.5 12.0 %temporal_0_16.1.after_hbm = bf16[64,16,512]{2,1,0:T(8,128)(2,1)} custom-call(s32[32]{0:T(128)S(1)} %copy-done.2, bf16[64,16,512]{2,1,0:T(8,128)(2,1)S(1)} %bitcast.13, bf16[64,512]{1,0:T(8,128)(2,1)S(1)} %copy-done, f32[2,2,512]{2,1,0:T(2,128)S(1)} %copy-done.1, bf16[2,512,512]{2,1,0:T(8,128)(2,1)} %wq_hbm.7, bf16[2,512,512]{2,1,0:T(8,128)(2,1)} %wk_hbm.7, ...), custom_call_target="tpu_custom_call" | custom-call | flops 4294967296 | bytes 1048576 | tf_op jit(solution)/shard_map/temporal_0_16/pallas_call | solution.py:442
  43.5 3.7 %all-to-all-done = bf16[16,4,16,512]{3,2,1,0:T(8,128)(2,1)S(1)} async-done(((bf16[16,4,16,512]{3,2,1,0:T(8,128)(2,1)}), bf16[16,4,16,512]{3,2,1,0:T(8,128)(2,1)S(1)}, u32[]{:S(2)}, u32[]{:S(2)}) %all-to-all-start) | async-done | bytes 1048608 | tf_op jit(solution)/shard_map/all_to_all | solution.py:530
  47.3 4.4 %all-to-all-start.3 = ((bf16[16,4,16,512]{3,2,1,0:T(8,128)(2,1)}), bf16[16,4,16,512]{3,2,1,0:T(8,128)(2,1)S(1)}, u32[]{:S(2)}, u32[]{:S(2)}) async-start(bf16[16,4,16,512]{3,2,1,0:T(8,128)(2,1)} %bitcast.18), calls=%async_computation.3 | async-start | bytes 2097152 | tf_op jit(solution)/shard_map/all_to_all | solution.py:530
  51.7 11.9 %temporal_0_0.1 = bf16[64,16,512]{2,1,0:T(8,128)(2,1)} custom-call(s32[32]{0:T(128)S(1)} %copy-done.2, bf16[64,16,512]{2,1,0:T(8,128)(2,1)S(1)} %bitcast.11, bf16[64,512]{1,0:T(8,128)(2,1)S(1)} %copy-done, f32[2,2,512]{2,1,0:T(2,128)S(1)} %copy-done.1, bf16[2,512,512]{2,1,0:T(8,128)(2,1)} %wq_hbm.7, bf16[2,512,512]{2,1,0:T(8,128)(2,1)} %wk_hbm.7, ...), custom_call_target="tpu_custom_call" | custom-call | flops 4294967296 | bytes 1048576 | tf_op jit(solution)/shard_map/temporal_0_0/pallas_call | solution.py:442
  63.6 3.8 %all-to-all-done.3.refs_1_ = bf16[16,4,16,512]{3,2,1,0:T(8,128)(2,1)S(1)} async-done(((bf16[16,4,16,512]{3,2,1,0:T(8,128)(2,1)}), bf16[16,4,16,512]{3,2,1,0:T(8,128)(2,1)S(1)}, u32[]{:S(2)}, u32[]{:S(2)}) %all-to-all-start.3) | async-done | bytes 1048608 | tf_op jit(solution)/shard_map/all_to_all | solution.py:530
  67.4 4.4 %all-to-all-start.1 = ((bf16[16,4,16,512]{3,2,1,0:T(8,128)(2,1)}), bf16[16,4,16,512]{3,2,1,0:T(8,128)(2,1)S(1)}, u32[]{:S(2)}, u32[]{:S(2)}) async-start(bf16[16,4,16,512]{3,2,1,0:T(8,128)(2,1)} %bitcast.21), calls=%async_computation.1 | async-start | bytes 2097152 | tf_op jit(solution)/shard_map/all_to_all | solution.py:530
  73.4 14.2 %all-to-all-done.1.refs_0_ = bf16[16,4,16,512]{3,2,1,0:T(8,128)(2,1)S(1)} async-done(((bf16[16,4,16,512]{3,2,1,0:T(8,128)(2,1)}), bf16[16,4,16,512]{3,2,1,0:T(8,128)(2,1)S(1)}, u32[]{:S(2)}, u32[]{:S(2)}) %all-to-all-start.1) | async-done | bytes 1048608 | tf_op jit(solution)/shard_map/all_to_all | solution.py:530
  87.6 3.1 %structure_1_0.1 = bf16[16,4,16,512]{3,2,1,0:T(8,128)(2,1)} custom-call(bf16[16,4,16,512]{3,2,1,0:T(8,128)(2,1)S(1)} %all-to-all-done.1.refs_0_, bf16[16,4,16,512]{3,2,1,0:T(8,128)(2,1)S(1)} %all-to-all-done.3.refs_1_, bf16[4,256,512]{2,1,0:T(8,128)(2,1)S(1)} %stage.1.refs_2_, bf16[2,512,512]{2,1,0:T(8,128)(2,1)} %refs_3_.3), custom_call_target="tpu_custom_call" | custom-call | flops 1073741824 | bytes 2097152 | tf_op jit(solution)/shard_map/structure_1_0/pallas_call | solution.py:238
  90.7 4.4 %all-to-all-start.6 = ((bf16[16,4,16,512]{3,2,1,0:T(8,128)(2,1)}), bf16[16,4,16,512]{3,2,1,0:T(8,128)(2,1)S(1)}, u32[]{:S(2)}, u32[]{:S(2)}) async-start(bf16[16,4,16,512]{3,2,1,0:T(8,128)(2,1)} %structure_1_0.1), calls=%async_computation.6 | async-start | bytes 2097152 | tf_op jit(solution)/shard_map/all_to_all | solution.py:530
  95.1 4.2 %structure_1_16.1 = bf16[16,4,16,512]{3,2,1,0:T(8,128)(2,1)} custom-call(bf16[16,4,16,512]{3,2,1,0:T(8,128)(2,1)S(1)} %all-to-all-done.1.refs_0_, bf16[16,4,16,512]{3,2,1,0:T(8,128)(2,1)S(1)} %all-to-all-done.3.refs_1_, s32[4,16,32,512]{3,2,1,0:T(8,128)} %bitcast.17, bf16[2,512,512]{2,1,0:T(8,128)(2,1)} %refs_3_.3), custom_call_target="tpu_custom_call" | custom-call | flops 1073741824 | bytes 8388608 | tf_op jit(solution)/shard_map/structure_1_16/pallas_call | solution.py:122
  99.3 11.5 %all-to-all-done.6 = bf16[16,4,16,512]{3,2,1,0:T(8,128)(2,1)S(1)} async-done(((bf16[16,4,16,512]{3,2,1,0:T(8,128)(2,1)}), bf16[16,4,16,512]{3,2,1,0:T(8,128)(2,1)S(1)}, u32[]{:S(2)}, u32[]{:S(2)}) %all-to-all-start.6) | async-done | bytes 1048608 | tf_op jit(solution)/shard_map/all_to_all | solution.py:530
  110.8 4.4 %all-to-all-start.4 = ((bf16[16,4,16,512]{3,2,1,0:T(8,128)(2,1)}), bf16[16,4,16,512]{3,2,1,0:T(8,128)(2,1)S(1)}, u32[]{:S(2)}, u32[]{:S(2)}) async-start(bf16[16,4,16,512]{3,2,1,0:T(8,128)(2,1)} %structure_1_16.1), calls=%async_computation.4 | async-start | bytes 2097152 | tf_op jit(solution)/shard_map/all_to_all | solution.py:530
  115.3 12.0 %temporal_1_0.1 = bf16[64,16,512]{2,1,0:T(8,128)(2,1)} custom-call(s32[32]{0:T(128)S(1)} %copy-done.2, bf16[64,16,512]{2,1,0:T(8,128)(2,1)S(1)} %bitcast.10, bf16[64,512]{1,0:T(8,128)(2,1)S(1)} %copy-done, f32[2,2,512]{2,1,0:T(2,128)S(1)} %copy-done.1, bf16[2,512,512]{2,1,0:T(8,128)(2,1)} %wq_hbm.7, bf16[2,512,512]{2,1,0:T(8,128)(2,1)} %wk_hbm.7, ...), custom_call_target="tpu_custom_call" | custom-call | flops 4294967296 | bytes 1048576 | tf_op jit(solution)/shard_map/temporal_1_0/pallas_call | solution.py:442
  127.3 3.7 %all-to-all-done.4 = bf16[16,4,16,512]{3,2,1,0:T(8,128)(2,1)S(1)} async-done(((bf16[16,4,16,512]{3,2,1,0:T(8,128)(2,1)}), bf16[16,4,16,512]{3,2,1,0:T(8,128)(2,1)S(1)}, u32[]{:S(2)}, u32[]{:S(2)}) %all-to-all-start.4) | async-done | bytes 1048608 | tf_op jit(solution)/shard_map/all_to_all | solution.py:530
  131.0 4.4 %all-to-all-start.7 = ((bf16[16,4,16,512]{3,2,1,0:T(8,128)(2,1)}), bf16[16,4,16,512]{3,2,1,0:T(8,128)(2,1)S(1)}, u32[]{:S(2)}, u32[]{:S(2)}) async-start(bf16[16,4,16,512]{3,2,1,0:T(8,128)(2,1)} %bitcast.19), calls=%async_computation.7 | async-start | bytes 2097152 | tf_op jit(solution)/shard_map/all_to_all | solution.py:530
  135.4 12.0 %temporal_1_16.1 = bf16[64,16,512]{2,1,0:T(8,128)(2,1)} custom-call(s32[32]{0:T(128)S(1)} %copy-done.2, bf16[64,16,512]{2,1,0:T(8,128)(2,1)S(1)} %bitcast.12, bf16[64,512]{1,0:T(8,128)(2,1)S(1)} %copy-done, f32[2,2,512]{2,1,0:T(2,128)S(1)} %copy-done.1, bf16[2,512,512]{2,1,0:T(8,128)(2,1)} %wq_hbm.7, bf16[2,512,512]{2,1,0:T(8,128)(2,1)} %wk_hbm.7, ...), custom_call_target="tpu_custom_call" | custom-call | flops 4294967296 | bytes 1048576 | tf_op jit(solution)/shard_map/temporal_1_16/pallas_call | solution.py:442
  147.5 3.7 %all-to-all-done.7.piece_ref = bf16[16,4,16,512]{3,2,1,0:T(8,128)(2,1)S(1)} async-done(((bf16[16,4,16,512]{3,2,1,0:T(8,128)(2,1)}), bf16[16,4,16,512]{3,2,1,0:T(8,128)(2,1)S(1)}, u32[]{:S(2)}, u32[]{:S(2)}) %all-to-all-start.7) | async-done | bytes 1048608 | tf_op jit(solution)/shard_map/all_to_all | solution.py:530
  151.2 4.4 %all-to-all-start.5 = ((bf16[16,4,16,512]{3,2,1,0:T(8,128)(2,1)}), bf16[16,4,16,512]{3,2,1,0:T(8,128)(2,1)S(1)}, u32[]{:S(2)}, u32[]{:S(2)}) async-start(bf16[16,4,16,512]{3,2,1,0:T(8,128)(2,1)} %bitcast.20), calls=%async_computation.5 | async-start | bytes 2097152 | tf_op jit(solution)/shard_map/all_to_all | solution.py:530
  156.6 14.7 %all-to-all-done.5.piece_ref = bf16[16,4,16,512]{3,2,1,0:T(8,128)(2,1)S(1)} async-done(((bf16[16,4,16,512]{3,2,1,0:T(8,128)(2,1)}), bf16[16,4,16,512]{3,2,1,0:T(8,128)(2,1)S(1)}, u32[]{:S(2)}, u32[]{:S(2)}) %all-to-all-start.5) | async-done | bytes 1048608 | tf_op jit(solution)/shard_map/all_to_all | solution.py:530
  (9 shorter events, 3.6 us)
Async XLA Ops:
  4.5 22.6 %all-to-all-start.2 = ((bf16[16,4,16,512]{3,2,1,0:T(8,128)(2,1)}), bf16[16,4,16,512]{3,2,1,0:T(8,128)(2,1)S(1)}, u32[]{:S(2)}, u32[]{:S(2)}) async-start(bf16[16,4,16,512]{3,2,1,0:T(8,128)(2,1)} %structure_0_16.1), calls=%async_computation.2 | async-start | bytes 2097152 | tf_op jit(solution)/shard_map/all_to_all | solution.py:530
  15.9 15.6 %copy-start = (bf16[64,512]{1,0:T(8,128)(2,1)S(1)}, bf16[64,512]{1,0:T(8,128)(2,1)}, u32[]{:S(2)}) copy-start(bf16[64,512]{1,0:T(8,128)(2,1)} %pos_ref.7) | copy-start | bytes 196612
  15.9 15.6 %copy-start.1 = (f32[2,2,512]{2,1,0:T(2,128)S(1)}, f32[2,2,512]{2,1,0:T(2,128)}, u32[]{:S(2)}) copy-start(f32[2,2,512]{2,1,0:T(2,128)} %gain_ref.7) | copy-start | bytes 24580
  16.0 15.6 %copy-start.2 = (s32[32]{0:T(128)S(1)}, s32[32]{0:T(128)}, u32[]{:S(2)}) copy-start(s32[32]{0:T(128)} %first_ref.7) | copy-start | bytes 388
  27.1 20.2 %all-to-all-start = ((bf16[16,4,16,512]{3,2,1,0:T(8,128)(2,1)}), bf16[16,4,16,512]{3,2,1,0:T(8,128)(2,1)S(1)}, u32[]{:S(2)}, u32[]{:S(2)}) async-start(bf16[16,4,16,512]{3,2,1,0:T(8,128)(2,1)} %structure_0_0.1), calls=%async_computation | async-start | bytes 2097152 | tf_op jit(solution)/shard_map/all_to_all | solution.py:530
  47.3 20.2 %all-to-all-start.3 = ((bf16[16,4,16,512]{3,2,1,0:T(8,128)(2,1)}), bf16[16,4,16,512]{3,2,1,0:T(8,128)(2,1)S(1)}, u32[]{:S(2)}, u32[]{:S(2)}) async-start(bf16[16,4,16,512]{3,2,1,0:T(8,128)(2,1)} %bitcast.18), calls=%async_computation.3 | async-start | bytes 2097152 | tf_op jit(solution)/shard_map/all_to_all | solution.py:530
  67.4 20.2 %all-to-all-start.1 = ((bf16[16,4,16,512]{3,2,1,0:T(8,128)(2,1)}), bf16[16,4,16,512]{3,2,1,0:T(8,128)(2,1)S(1)}, u32[]{:S(2)}, u32[]{:S(2)}) async-start(bf16[16,4,16,512]{3,2,1,0:T(8,128)(2,1)} %bitcast.21), calls=%async_computation.1 | async-start | bytes 2097152 | tf_op jit(solution)/shard_map/all_to_all | solution.py:530
  90.7 20.2 %all-to-all-start.6 = ((bf16[16,4,16,512]{3,2,1,0:T(8,128)(2,1)}), bf16[16,4,16,512]{3,2,1,0:T(8,128)(2,1)S(1)}, u32[]{:S(2)}, u32[]{:S(2)}) async-start(bf16[16,4,16,512]{3,2,1,0:T(8,128)(2,1)} %structure_1_0.1), calls=%async_computation.6 | async-start | bytes 2097152 | tf_op jit(solution)/shard_map/all_to_all | solution.py:530
  110.8 20.2 %all-to-all-start.4 = ((bf16[16,4,16,512]{3,2,1,0:T(8,128)(2,1)}), bf16[16,4,16,512]{3,2,1,0:T(8,128)(2,1)S(1)}, u32[]{:S(2)}, u32[]{:S(2)}) async-start(bf16[16,4,16,512]{3,2,1,0:T(8,128)(2,1)} %structure_1_16.1), calls=%async_computation.4 | async-start | bytes 2097152 | tf_op jit(solution)/shard_map/all_to_all | solution.py:530
  131.0 20.2 %all-to-all-start.7 = ((bf16[16,4,16,512]{3,2,1,0:T(8,128)(2,1)}), bf16[16,4,16,512]{3,2,1,0:T(8,128)(2,1)S(1)}, u32[]{:S(2)}, u32[]{:S(2)}) async-start(bf16[16,4,16,512]{3,2,1,0:T(8,128)(2,1)} %bitcast.19), calls=%async_computation.7 | async-start | bytes 2097152 | tf_op jit(solution)/shard_map/all_to_all | solution.py:530
  151.2 20.2 %all-to-all-start.5 = ((bf16[16,4,16,512]{3,2,1,0:T(8,128)(2,1)}), bf16[16,4,16,512]{3,2,1,0:T(8,128)(2,1)S(1)}, u32[]{:S(2)}, u32[]{:S(2)}) async-start(bf16[16,4,16,512]{3,2,1,0:T(8,128)(2,1)} %bitcast.20), calls=%async_computation.5 | async-start | bytes 2097152 | tf_op jit(solution)/shard_map/all_to_all | solution.py:530
